TPU v7x, 256 devices: a whole 4x4x8 slice. The times are simulated.
256 devices in a mesh: sec: 2 (over core), grp: 128 (over y, z, x).
Axes of the slice: x: 4, y: 4, z: 8, core: 2. Of those that a mesh axis runs over, the one named last changes fastest.
Arguments:
- stratum_warmth_anomaly: float32 [90, 65536], P('sec', 'grp'), may hold values from 0.7 to 1.3
- pressure_depth: float32 [90, 65536], P('sec', 'grp'), may hold values from 0.5 to 2
- absorber_amounts: float32 [4, 90, 65536], P(None, 'sec', 'grp'), may hold values from 0.1 to 1
- ground_warmth_anomaly: float32 [65536], P('grp'), may hold values from 0.9 to 1.3
- sun_elevation_factor: float32 [65536], P('grp'), may hold values from 0.2 to 1
- daytime_mask: int32 [65536], P('grp'), may hold values 0 or 1
- dispatch_position: int32 [128, 512], P('grp'), may hold values from 0 to 511, each once within a row
- arrival_membership: int32 [128, 512], P('grp'), may hold values from 0 to 511, each once within a row
- adjacency_table: int32 [6, 65536], P(None, 'grp'), may hold values from 0 to 639, as said below
- blending_coefficient: float32 [6, 65536], P(None, 'grp'), may hold values from 0.02 to 0.15
- opacity_table: float32 [4, 112, 90], P(None, 'sec'), may hold values from 0.001 to 0.3
- emission_share: float32 [112], P('sec'), may hold values from 0.05 to 0.5
- sunshine_share: float32 [112], P('sec'), may hold values from 0.05 to 0.5
Outputs:
- heating: float32 [90, 65536], P('sec', 'grp')
- mixed: float32 [4, 90, 65536], P(None, 'sec', 'grp')
Inputs may be any that keep to these rules, and one draw needn't show every extreme that they name: `dispatch_position`: each row is a permutation of 0 to 511. `arrival_membership`: each row is a permutation of 0 to 511, so every radiation column has exactly four members. adjacency_table[k, c] - (c mod 512) lies in 0 to 128.
All inputs are finite; a program needn't handle non-finite values. No bound on the sum of `daytime_mask` on one device may be relied on, other than what follows from the above.
Results may differ from a plain program's by a relative error of at most 0.0003.
Values sent between devices are 32-bit elements; how exact they have to be, the bound alone decides.
No kernel may reach another device: no remote copies, remote signals or barrier semaphores. Data moves between devices by JAX's collectives and lax.ppermute only.
A program may use at most 64 MiB of HBM per device.

v0:
```python
import jax
import jax.numpy as jnp
from jax import lax
from jax.sharding import PartitionSpec as P

STEPS = 4
LEVEL_BLOCK = 9
HALO = 64


DIFFUSE = 1.66
TOP = lax.Precision.HIGHEST


def padded(shard, sides, width):
    for axis, dim in sides:
        size, length = (lax.axis_size(axis), shard.shape[dim])
        up = [(i, (i + 1) % size) for i in range(size)]
        down = [(j, i) for i, j in up]
        last = lax.slice_in_dim(shard, length - width, length, axis=dim)
        first = lax.slice_in_dim(shard, 0, width, axis=dim)
        before = lax.ppermute(last, axis, up)
        after = lax.ppermute(first, axis, down)
        shard = jnp.concatenate([before, shard, after], axis=dim)
    return shard


def select_matrix(ids, count):
    return (ids[:, None] == jnp.arange(count, dtype=jnp.int32)[None, :]).astype(jnp.float32)


def pick_columns(values, selector):
    return lax.dot_general(values, selector, (((1,), (1,)), ((), ())), precision=TOP)


def optical(level_table, radiant_species, stratum_index):
    coeffs = lax.dynamic_index_in_dim(level_table, stratum_index, 0, keepdims=False)
    amounts = lax.dynamic_index_in_dim(radiant_species, stratum_index, 1, keepdims=False)
    optical_depth = coeffs[0][:, None] * amounts[0][None, :]
    for species in range(1, coeffs.shape[0]):
        optical_depth = optical_depth + coeffs[species][:, None] * amounts[species][None, :]
    return optical_depth


def compute_flux_heating(
    radiant_warmth,
    radiant_depth,
    radiant_species,
    radiant_ground,
    sunlight_incline,
    incoming_sunshine,
    opacity_table,
    emission_share,
    sunshine_share,
):
    strata_range, radiant_span = radiant_warmth.shape
    blocks = strata_range // LEVEL_BLOCK
    gpoints = emission_share.shape[0]
    block_ids = jnp.arange(blocks, dtype=jnp.int32)
    level_table = jnp.transpose(opacity_table, (2, 0, 1))

    def layer_terms(stratum_index):
        optical_depth = optical(level_table, radiant_species, stratum_index)
        stratum_warmth = lax.dynamic_index_in_dim(radiant_warmth, stratum_index, 0, keepdims=False)
        source = emission_share[:, None] * (stratum_warmth**4)[None, :]
        return (optical_depth, jnp.exp(-DIFFUSE * optical_depth), source)

    def down_block(fluxes, block_id):
        thermal, direct = fluxes
        thermal_rows = []
        direct_rows = []
        for inner_id in range(LEVEL_BLOCK):
            optical_depth, transmit, source = layer_terms(block_id * LEVEL_BLOCK + inner_id)
            thermal = transmit * thermal + (1.0 - transmit) * source
            direct = direct * jnp.exp(-optical_depth / sunlight_incline[None, :])
            thermal_rows.append(jnp.sum(thermal, axis=0))
            direct_rows.append(jnp.sum(direct, axis=0))
        return ((thermal, direct), (jnp.stack(thermal_rows), jnp.stack(direct_rows)))

    down_init = (
        jnp.zeros((gpoints, radiant_span), jnp.float32),
        sunshine_share[:, None] * incoming_sunshine[None, :],
    )
    final_down, (down_rows, direct_rows) = lax.scan(down_block, down_init, block_ids)
    thermal_down = jnp.concatenate(
        [jnp.zeros((1, radiant_span), jnp.float32), down_rows.reshape(strata_range, radiant_span)],
        axis=0,
    )
    direct_down = jnp.concatenate(
        [jnp.sum(down_init[1], axis=0)[None], direct_rows.reshape(strata_range, radiant_span)],
        axis=0,
    )

    def up_block(upward, block_id):
        upward_rows = []
        for inner_id in range(LEVEL_BLOCK - 1, -1, -1):
            optical_depth, transmit, source = layer_terms(block_id * LEVEL_BLOCK + inner_id)
            upward = transmit * upward + (1.0 - transmit) * source
            upward_rows.append(jnp.sum(upward, axis=0))
        return (upward, jnp.stack(upward_rows[::-1]))

    up_init = emission_share[:, None] * (radiant_ground**4)[None, :]
    final_up, up_rows = lax.scan(up_block, up_init, block_ids, reverse=True)
    upward_flux = jnp.concatenate(
        [up_rows.reshape(strata_range, radiant_span), jnp.sum(up_init, axis=0)[None]], axis=0
    )
    net_flux = thermal_down - upward_flux + direct_down
    return (net_flux[:-1] - net_flux[1:]) / radiant_depth


def per_device(
    stratum_warmth_anomaly,
    pressure_depth,
    absorber_amounts,
    ground_warmth_anomaly,
    sun_elevation_factor,
    daytime_mask,
    dispatch_position,
    arrival_membership,
    adjacency_table,
    blending_coefficient,
    opacity_table,
    emission_share,
    sunshine_share,
):
    cell_sequence = stratum_warmth_anomaly.shape[1]
    position = dispatch_position[0]
    placing = select_matrix(position, cell_sequence)
    state_bundle = jnp.concatenate(
        [stratum_warmth_anomaly[None], pressure_depth[None], absorber_amounts], axis=0
    )
    surface = jnp.stack(
        [
            ground_warmth_anomaly,
            sun_elevation_factor,
            daytime_mask.astype(jnp.float32) * sun_elevation_factor,
        ],
        axis=0,
    )[:, None, :]
    packed = jnp.dot(state_bundle.reshape(-1, cell_sequence), placing, precision=TOP).reshape(
        state_bundle.shape
    )
    packed_surface = jnp.dot(surface.reshape(3, cell_sequence), placing, precision=TOP).reshape(
        surface.shape
    )
    groups_dev = cell_sequence // 4
    group_ids = arrival_membership[0] // 4
    whole_levels = lax.all_gather(packed, "sec", axis=1, tiled=True)
    arrived, arrived_surface = (
        lax.all_to_all(whole_levels, "grp", split_axis=2, concat_axis=2, tiled=True),
        lax.all_to_all(packed_surface, "grp", split_axis=2, concat_axis=2, tiled=True),
    )
    selector = select_matrix(group_ids, groups_dev)
    member = selector * 0.25
    flattened = arrived.reshape(-1, cell_sequence)
    pooled = jnp.dot(flattened, member, precision=TOP).reshape(
        arrived.shape[0], arrived.shape[1], groups_dev
    )
    pooled_surface = jnp.dot(arrived_surface.reshape(3, cell_sequence), member, precision=TOP)
    heat_part = compute_flux_heating(
        pooled[0],
        pooled[1],
        pooled[2:],
        pooled_surface[0],
        pooled_surface[1],
        pooled_surface[2],
        opacity_table,
        emission_share,
        sunshine_share,
    )
    slot_heat = pick_columns(heat_part, selector)
    returned = lax.all_to_all(slot_heat, "grp", split_axis=1, concat_axis=1, tiled=True)
    own_heat = pick_columns(returned, placing)
    heating = lax.psum_scatter(own_heat, "sec", scatter_dimension=0, tiled=True)
    extended_span = cell_sequence + 2 * HALO
    source_rows = jnp.arange(extended_span, dtype=jnp.int32)[:, None]
    blend_matrix = jnp.zeros((extended_span, cell_sequence), jnp.float32)
    for near_id in range(adjacency_table.shape[0]):
        blend_matrix = blend_matrix + jnp.where(
            adjacency_table[near_id][None, :] == source_rows,
            blending_coefficient[near_id][None, :],
            0.0,
        )
    centre_rows = jnp.arange(cell_sequence, dtype=jnp.int32)[None, :] + HALO
    weight_total = jnp.sum(blending_coefficient, axis=0)
    blend_matrix = blend_matrix - jnp.where(source_rows == centre_rows, weight_total[None, :], 0.0)
    mixed = absorber_amounts
    for step_id in range(STEPS):
        extended = padded(mixed, (("grp", 2),), HALO)
        update = jnp.dot(extended.reshape(-1, extended_span), blend_matrix, precision=TOP).reshape(
            mixed.shape
        )
        mixed = mixed + update
    return (heating, mixed)


def solution(mesh):
    in_specs = (
        P("sec", "grp"),
        P("sec", "grp"),
        P(None, "sec", "grp"),
        P("grp"),
        P("grp"),
        P("grp"),
        P("grp", None),
        P("grp", None),
        P(None, "grp"),
        P(None, "grp"),
        P(None, "sec", None),
        P("sec"),
        P("sec"),
    )
    out_specs = (P("sec", "grp"), P(None, "sec", "grp"))
    return jax.shard_map(
        per_device, mesh=mesh, in_specs=in_specs, out_specs=out_specs, check_vma=False
    )
```

profile of v0, /device:TPU:1, one launch (start us, length us, event | category | flops | bytes accessed | tf_op | source)
XLA Modules:
  0.0 232.5 jit_solution(9307211473138988006)
XLA Ops:
  7.2 1.1 copy.43
  8.3 1.8 fusion.151
  10.1 1.2 copy.44
  11.4 1.8 fusion.150
  13.2 16.3 %all-to-all-start = ((f32[3,1,512]{0,1,2:T(1,128)}), f32[3,1,512]{0,1,2:T(1,128)S(1)}, u32[]{:S(2)}, u32[]{:S(2)}) async-start(f32[3,1,512]{0,1,2:T(1,128)} %bitcast.226), calls=%async_computation | async-start | bytes 524288 | tf_op jit(solution)/shard_map/all_to_all | solution.py:151
  29.6 6.8 %collective-permute-start.1 = (f32[4,45,64]{2,1,0:T(8,128)S(1)}, f32[4,45,64]{2,1,0:T(8,128)S(1)}, u32[]{:S(2)}, u32[]{:S(2)}) collective-permute-start(f32[4,45,64]{2,1,0:T(8,128)S(1)} %get-tuple-element.643), channel_id=1, source_target_pairs={{1,0},{2,1},{3,2},{4,3},{5,4},{6,5},{7,6},{8,7},{9,8},{10,9},{11,1... | collective-permute-start | bytes 138248 | tf_op jit(solution)/shard_map/ppermute | solution.py:23
  36.5 3.0 %copy.45 = f32[6,90,512]{1,0,2:T(8,128)} copy(f32[6,90,512]{2,0,1:T(8,128)} %all-gather.2.cloned.1.call-done) | data formatting | bytes 2211840 | tf_op jit(solution)/shard_map/all_gather | solution.py:148
  39.5 2.5 %all-to-all-done = f32[3,1,512]{0,1,2:T(1,128)S(1)} async-done(((f32[3,1,512]{0,1,2:T(1,128)}), f32[3,1,512]{0,1,2:T(1,128)S(1)}, u32[]{:S(2)}, u32[]{:S(2)}) %all-to-all-start) | async-done | bytes 6176 | tf_op jit(solution)/shard_map/all_to_all | solution.py:151
  42.1 8.0 %all-to-all-start.1 = ((f32[6,90,512]{1,0,2:T(8,128)}), f32[6,90,512]{1,0,2:T(8,128)S(1)}, u32[]{:S(2)}, u32[]{:S(2)}) async-start(f32[6,90,512]{1,0,2:T(8,128)} %copy.45), calls=%async_computation.1 | async-start | bytes 4194304 | tf_op jit(solution)/shard_map/all_to_all | solution.py:150
  50.1 0.8 copy.42
  53.0 2.3 %fusion.136 = f32[4,45,512]{2,1,0:T(8,128)S(1)} fusion(f32[4,45,512]{2,1,0:T(8,128)S(1)} %copy.43, f32[4,45,64]{2,1,0:T(8,128)S(1)} %collective-permute-done.1, f32[4,45,64]{2,1,0:T(8,128)S(1)} %collective-permute-done, f32[512]{0:T(512)S(1)} %reduce_sum.380, s32[512]{0:T(512)S(1)} %iota_add_fusion, f32[512]{0:T(512)S(1)} %bitcast.576, ...), kind=kOutput, calls=%fused_computation.362 | convolution fusion | flops 714664960 | bytes 858112 | tf_op jit(solution)/shard_map/dot_general | solution.py:190
  55.4 7.0 %collective-permute-start.3 = (f32[4,45,64]{2,1,0:T(8,128)S(1)}, f32[4,45,64]{2,1,0:T(8,128)S(1)}, u32[]{:S(2)}, u32[]{:S(2)}) collective-permute-start(f32[4,45,64]{2,1,0:T(8,128)S(1)} %get-tuple-element.641), channel_id=1, source_target_pairs={{1,0},{2,1},{3,2},{4,3},{5,4},{6,5},{7,6},{8,7},{9,8},{10,9},{11,1... | collective-permute-start | bytes 138248 | tf_op jit(solution)/shard_map/ppermute | solution.py:23
  62.5 32.1 %collective-permute-done.3 = f32[4,45,64]{2,1,0:T(8,128)S(1)} collective-permute-done((f32[4,45,64]{2,1,0:T(8,128)S(1)}, f32[4,45,64]{2,1,0:T(8,128)S(1)}, u32[]{:S(2)}, u32[]{:S(2)}) %collective-permute-start.3) | collective-permute-done | bytes 46112 | tf_op jit(solution)/shard_map/ppermute | solution.py:23
  94.7 7.4 %collective-permute-done.2 = f32[4,45,64]{2,1,0:T(8,128)S(1)} collective-permute-done((f32[4,45,64]{2,1,0:T(8,128)S(1)}, f32[4,45,64]{2,1,0:T(8,128)S(1)}, u32[]{:S(2)}, u32[]{:S(2)}) %collective-permute-start.2) | collective-permute-done | bytes 46112 | tf_op jit(solution)/shard_map/ppermute | solution.py:22
  102.1 2.3 %fusion.139 = f32[4,45,512]{2,1,0:T(8,128)S(1)} fusion(f32[4,45,512]{2,1,0:T(8,128)S(1)} %fusion.136, f32[4,45,64]{2,1,0:T(8,128)S(1)} %collective-permute-done.3, f32[4,45,64]{2,1,0:T(8,128)S(1)} %collective-permute-done.2, f32[512]{0:T(512)S(1)} %reduce_sum.380, s32[512]{0:T(512)S(1)} %iota_add_fusion, f32[512]{0:T(512)S(1)} %bitcast.577, ...), kind=kOutput, calls=%fused_computation.363 | convolution fusion | flops 714664960 | bytes 858112 | tf_op jit(solution)/shard_map/dot_general | solution.py:190
  104.4 0.8 fusion.227
  105.8 0.9 collective-permute-start.4
  107.2 2.3 fusion.181
  109.5 37.1 %while.35 = (s32[]{:T(128)}, f32[56,128]{1,0:T(8,128)S(1)}, f32[10,9,128]{2,1,0:T(8,128)S(1)}, s32[10]{0:T(128)S(1)}, f32[90,4,56]{2,1,0:T(4,128)}, /*index=5*/f...) while((s32[]{:T(128)}, f32[56,128]{1,0:T(8,128)S(1)}, ...), condition=%wide.region_30.31_spmd, body=%wide.region_20.30_spmd.sunk | while | flops 904362 | bytes 658635 | solution.py:103
  109.6 0.7 dynamic_slice.604
  111.2 0.8 constant_dynamic-slice_fusion.111
  113.3 0.7 dynamic_slice.604
  114.9 0.8 constant_dynamic-slice_fusion.111
  117.0 0.7 dynamic_slice.604
  118.6 0.8 constant_dynamic-slice_fusion.111
  120.7 0.7 dynamic_slice.604
  122.3 0.8 constant_dynamic-slice_fusion.111
  124.4 0.7 dynamic_slice.604
  126.0 0.8 constant_dynamic-slice_fusion.111
  128.1 0.7 dynamic_slice.604
  129.7 0.8 constant_dynamic-slice_fusion.111
  131.8 0.7 dynamic_slice.604
  133.4 0.8 constant_dynamic-slice_fusion.111
  135.5 0.7 dynamic_slice.604
  137.1 0.8 constant_dynamic-slice_fusion.111
  139.2 0.7 dynamic_slice.604
  140.8 0.8 constant_dynamic-slice_fusion.111
  142.9 0.7 dynamic_slice.604
  144.5 0.8 constant_dynamic-slice_fusion.111
  146.7 42.0 %while.36 = (s32[]{:T(128)}, f32[56,128]{1,0:T(8,128)S(1)}, f32[56,128]{1,0:T(8,128)S(1)}, f32[10,9,128]{2,1,0:T(8,128)S(1)}, f32[10,9,128]{2,1,0:T(8,128)S(1)},...) while((s32[]{:T(128)}, f32[56,128]{1,0:T(8,128)S(1)}, ...), condition=%wide.region_19.20_spmd.clone, body=%wide.region_0.19_spmd.clone.sunk | while | flops 1620010 | bytes 1230241 | solution.py:84
  146.7 0.7 dynamic_slice.607
  148.3 0.8 constant_dynamic-slice_fusion.112
  152.5 0.8 constant_dynamic-slice_fusion.112
  155.1 0.7 dynamic_slice.607
  156.7 0.8 constant_dynamic-slice_fusion.112
  159.3 0.7 dynamic_slice.607
  160.9 0.8 constant_dynamic-slice_fusion.112
  163.4 0.7 dynamic_slice.607
  165.1 0.8 constant_dynamic-slice_fusion.112
  169.3 0.8 constant_dynamic-slice_fusion.112
  173.5 0.8 constant_dynamic-slice_fusion.112
  177.7 0.8 constant_dynamic-slice_fusion.112
  181.8 0.8 constant_dynamic-slice_fusion.112
  186.0 0.8 constant_dynamic-slice_fusion.112
  188.7 1.0 fusion.185
  189.8 10.5 %all-to-all-start.2 = ((f32[90,128,4]{0,2,1:T(4,128)}), f32[90,128,4]{0,2,1:T(4,128)S(1)}, u32[]{:S(2)}, u32[]{:S(2)}) async-start(f32[90,128,4]{0,2,1:T(4,128)} %bitcast.107), calls=%async_computation.2 | async-start | bytes 524288 | tf_op jit(solution)/shard_map/all_to_all | solution.py:172
  200.4 3.3 %fusion.142 = f32[4,45,512]{2,1,0:T(8,128)S(1)} fusion(f32[4,45,512]{2,1,0:T(8,128)S(1)} %copy-done.3, f32[4,45,64]{2,1,0:T(8,128)} %collective-permute-done.5, f32[4,45,64]{2,1,0:T(8,128)} %collective-permute-done.4, f32[512]{0:T(512)S(1)} %reduce_sum.380, s32[512]{0:T(512)S(1)} %copy-done.19, f32[512]{0:T(512)S(1)} %bitcast.578, s32[512]{0:T(512)S(1)} %bitcast.598, ...), kind=kOutput, calls=%fused_computation.364 | convolution fusion | flops 714664960 | bytes 858112 | tf_op jit(solution)/shard_map/dot_general | solution.py:190
  203.7 6.8 %collective-permute-start.7 = (f32[4,45,64]{2,1,0:T(8,128)S(1)}, f32[4,45,64]{2,1,0:T(8,128)S(1)}, u32[]{:S(2)}, u32[]{:S(2)}) collective-permute-start(f32[4,45,64]{2,1,0:T(8,128)S(1)} %get-tuple-element.637), channel_id=1, source_target_pairs={{1,0},{2,1},{3,2},{4,3},{5,4},{6,5},{7,6},{8,7},{9,8},{10,9},{11,1... | collective-permute-start | bytes 138248 | tf_op jit(solution)/shard_map/ppermute | solution.py:23
  210.6 1.7 all-to-all-done.2
  212.2 0.8 fusion.148
  213.0 7.2 %fusion = f32[48,512]{1,0:T(8,128)S(1)} fusion(f32[90,512]{1,0:T(8,128)S(1)} %fusion.148), kind=kCustom, calls=%all-reduce-scatter | all-reduce-scatter fusion | flops 49153 | bytes 283648
  220.2 1.3 collective-permute-start.8
  221.5 2.3 %fusion.145 = f32[4,45,512]{2,1,0:T(8,128)S(1)} fusion(f32[4,45,512]{2,1,0:T(8,128)S(1)} %fusion.142, f32[4,45,64]{2,1,0:T(8,128)S(1)} %collective-permute-done.7, f32[4,45,64]{2,1,0:T(8,128)S(1)} %collective-permute-done.6, f32[512]{0:T(512)S(1)} %reduce_sum.380, s32[512]{0:T(512)S(1)} %copy-done.19, f32[512]{0:T(512)S(1)} %bitcast.579, ...), kind=kOutput, calls=%fused_computation.365 | convolution fusion | flops 714664960 | bytes 858112 | tf_op jit(solution)/shard_map/dot_general | solution.py:190
  223.8 1.0 copy.52
  (597 shorter events, 40.2 us)
Async XLA Ops:
  7.2 29.3 %all-gather.2.cloned.1.call-start = ((), (), s32[]{:S(2)}) async-start(), calls=%async_computation.3 | async-start | bytes 2211840 | tf_op jit(solution)/shard_map/all_gather | solution.py:148
  10.1 1.3 copy-start.7
  10.1 1.3 copy-start.8
  10.1 1.3 copy-start.6
  10.1 1.3 copy-start.22
  11.3 25.1 %copy-start.4 = (f32[6,512]{1,0:T(8,128)S(1)}, f32[6,512]{1,0:T(8,128)}, u32[]{:S(2)}) copy-start(f32[6,512]{1,0:T(8,128)} %param.26) | copy-start | bytes 36868
  13.2 28.8 %all-to-all-start = ((f32[3,1,512]{0,1,2:T(1,128)}), f32[3,1,512]{0,1,2:T(1,128)S(1)}, u32[]{:S(2)}, u32[]{:S(2)}) async-start(f32[3,1,512]{0,1,2:T(1,128)} %bitcast.226), calls=%async_computation | async-start | bytes 524288 | tf_op jit(solution)/shard_map/all_to_all | solution.py:151
  29.6 23.3 %collective-permute-start.1 = (f32[4,45,64]{2,1,0:T(8,128)S(1)}, f32[4,45,64]{2,1,0:T(8,128)S(1)}, u32[]{:S(2)}, u32[]{:S(2)}) collective-permute-start(f32[4,45,64]{2,1,0:T(8,128)S(1)} %get-tuple-element.643), channel_id=1, source_target_pairs={{1,0},{2,1},{3,2},{4,3},{5,4},{6,5},{7,6},{8,7},{9,8},{10,9},{11,1... | collective-permute-start | bytes 138248 | tf_op jit(solution)/shard_map/ppermute | solution.py:23
  36.5 16.5 %collective-permute-start = (f32[4,45,64]{2,1,0:T(8,128)S(1)}, f32[4,45,64]{2,1,0:T(8,128)S(1)}, u32[]{:S(2)}, u32[]{:S(2)}) collective-permute-start(f32[4,45,64]{2,1,0:T(8,128)S(1)} %get-tuple-element.642), channel_id=1, source_target_pairs={{0,1},{1,2},{2,3},{3,4},{4,5},{5,6},{6,7},{7,8},{8,9},{9,10},{10,1... | collective-permute-start | bytes 138248 | tf_op jit(solution)/shard_map/ppermute | solution.py:22
  39.5 10.6 %copy-start.17 = (s32[1,512]{1,0:T(1,128)S(1)}, s32[1,512]{1,0:T(1,128)}, u32[]{:S(2)}) copy-start(s32[1,512]{1,0:T(1,128)} %param.24) | copy-start | bytes 6148
  39.5 10.6 %copy-start.1 = (f32[4,56,90]{2,1,0:T(8,128)S(1)}, f32[4,56,90]{2,1,0:T(8,128)}, u32[]{:S(2)}) copy-start(f32[4,56,90]{2,1,0:T(8,128)} %param.27) | copy-start | bytes 241924
  39.5 11.4 %copy-start.21 = (u32[256]{0:T(256)S(1)}, u32[256]{0:T(256)}, u32[]{:S(2)}) copy-start(u32[256]{0:T(256)} %constant.406) | copy-start | bytes 3076
  39.5 12.7 %copy-start.5 = (s32[6,512]{1,0:T(8,128)S(1)}, s32[6,512]{1,0:T(8,128)}, u32[]{:S(2)}) copy-start(s32[6,512]{1,0:T(8,128)} %param.25) | copy-start | bytes 36868
  42.1 64.6 %all-to-all-start.1 = ((f32[6,90,512]{1,0,2:T(8,128)}), f32[6,90,512]{1,0,2:T(8,128)S(1)}, u32[]{:S(2)}, u32[]{:S(2)}) async-start(f32[6,90,512]{1,0,2:T(8,128)} %copy.45), calls=%async_computation.1 | async-start | bytes 4194304 | tf_op jit(solution)/shard_map/all_to_all | solution.py:150
  52.2 49.8 %copy-start.18 = (s32[512]{0:T(512)}, s32[512]{0:T(512)S(1)}, u32[]{:S(2)}) copy-start(s32[512]{0:T(512)S(1)} %iota_add_fusion) | copy-start | bytes 6148
  52.2 49.8 %copy-start.9 = (s32[1,512]{1,0:T(1,128)}, s32[1,512]{1,0:T(1,128)S(1)}, u32[]{:S(2)}) copy-start(s32[1,512]{1,0:T(1,128)S(1)} %get-tuple-element.646) | copy-start | bytes 6148
  52.3 49.8 %copy-start.11 = (s32[1,512]{1,0:T(1,128)}, s32[1,512]{1,0:T(1,128)S(1)}, u32[]{:S(2)}) copy-start(s32[1,512]{1,0:T(1,128)S(1)} %get-tuple-element.647) | copy-start | bytes 6148
  52.3 49.8 %copy-start.13 = (s32[1,512]{1,0:T(1,128)}, s32[1,512]{1,0:T(1,128)S(1)}, u32[]{:S(2)}) copy-start(s32[1,512]{1,0:T(1,128)S(1)} %get-tuple-element.648) | copy-start | bytes 6148
  52.3 49.8 %copy-start.15 = (s32[1,512]{1,0:T(1,128)}, s32[1,512]{1,0:T(1,128)S(1)}, u32[]{:S(2)}) copy-start(s32[1,512]{1,0:T(1,128)S(1)} %get-tuple-element.649) | copy-start | bytes 6148
  53.0 9.5 %copy-start = (f32[56]{0:T(128)S(1)}, f32[56]{0:T(128)}, u32[]{:S(2)}) copy-start(f32[56]{0:T(128)} %param.28) | copy-start | bytes 676
  53.0 9.5 %copy-start.20 = (f32[56]{0:T(128)S(1)}, f32[56]{0:T(128)}, u32[]{:S(2)}) copy-start(f32[56]{0:T(128)} %param.29) | copy-start | bytes 676
  55.4 39.2 %collective-permute-start.3 = (f32[4,45,64]{2,1,0:T(8,128)S(1)}, f32[4,45,64]{2,1,0:T(8,128)S(1)}, u32[]{:S(2)}, u32[]{:S(2)}) collective-permute-start(f32[4,45,64]{2,1,0:T(8,128)S(1)} %get-tuple-element.641), channel_id=1, source_target_pairs={{1,0},{2,1},{3,2},{4,3},{5,4},{6,5},{7,6},{8,7},{9,8},{10,9},{11,1... | collective-permute-start | bytes 138248 | tf_op jit(solution)/shard_map/ppermute | solution.py:23
  62.4 39.6 %collective-permute-start.2 = (f32[4,45,64]{2,1,0:T(8,128)S(1)}, f32[4,45,64]{2,1,0:T(8,128)S(1)}, u32[]{:S(2)}, u32[]{:S(2)}) collective-permute-start(f32[4,45,64]{2,1,0:T(8,128)S(1)} %get-tuple-element.640), channel_id=1, source_target_pairs={{0,1},{1,2},{2,3},{3,4},{4,5},{5,6},{6,7},{7,8},{8,9},{9,10},{10,1... | collective-permute-start | bytes 138248 | tf_op jit(solution)/shard_map/ppermute | solution.py:22
  104.4 2.3 copy-start.2
  105.2 95.1 %collective-permute-start.5 = (f32[4,45,64]{2,1,0:T(8,128)}, f32[4,45,64]{2,1,0:T(8,128)}, u32[]{:S(2)}, u32[]{:S(2)}) collective-permute-start(f32[4,45,64]{2,1,0:T(8,128)} %get-tuple-element.639), channel_id=1, source_target_pairs={{1,0},{2,1},{3,2},{4,3},{5,4},{6,5},{7,6},{8,7},{9,8},{10,9},{11,1... | collective-permute-start | bytes 138248 | tf_op jit(solution)/shard_map/ppermute | solution.py:23
  105.8 94.5 %collective-permute-start.4 = (f32[4,45,64]{2,1,0:T(8,128)}, f32[4,45,64]{2,1,0:T(8,128)}, u32[]{:S(2)}, u32[]{:S(2)}) collective-permute-start(f32[4,45,64]{2,1,0:T(8,128)} %get-tuple-element.638), channel_id=1, source_target_pairs={{0,1},{1,2},{2,3},{3,4},{4,5},{5,6},{6,7},{7,8},{8,9},{9,10},{10,1... | collective-permute-start | bytes 138248 | tf_op jit(solution)/shard_map/ppermute | solution.py:22
  188.6 11.7 %copy-start.3 = (f32[4,45,512]{2,1,0:T(8,128)S(1)}, f32[4,45,512]{2,1,0:T(8,128)}, u32[]{:S(2)}) copy-start(f32[4,45,512]{2,1,0:T(8,128)} %copy-done.2) | copy-start | bytes 1105924
  188.6 11.7 %copy-start.10 = (s32[1,512]{1,0:T(1,128)S(1)}, s32[1,512]{1,0:T(1,128)}, u32[]{:S(2)}) copy-start(s32[1,512]{1,0:T(1,128)} %copy-done.9) | copy-start | bytes 6148
  188.6 11.7 %copy-start.12 = (s32[1,512]{1,0:T(1,128)S(1)}, s32[1,512]{1,0:T(1,128)}, u32[]{:S(2)}) copy-start(s32[1,512]{1,0:T(1,128)} %copy-done.11) | copy-start | bytes 6148
  188.6 11.7 %copy-start.14 = (s32[1,512]{1,0:T(1,128)S(1)}, s32[1,512]{1,0:T(1,128)}, u32[]{:S(2)}) copy-start(s32[1,512]{1,0:T(1,128)} %copy-done.13) | copy-start | bytes 6148
  188.7 11.7 %copy-start.16 = (s32[1,512]{1,0:T(1,128)S(1)}, s32[1,512]{1,0:T(1,128)}, u32[]{:S(2)}) copy-start(s32[1,512]{1,0:T(1,128)} %copy-done.15) | copy-start | bytes 6148
  188.7 11.7 %copy-start.19 = (s32[512]{0:T(512)S(1)}, s32[512]{0:T(512)}, u32[]{:S(2)}) copy-start(s32[512]{0:T(512)} %copy-done.18) | copy-start | bytes 6148
  189.8 22.5 %all-to-all-start.2 = ((f32[90,128,4]{0,2,1:T(4,128)}), f32[90,128,4]{0,2,1:T(4,128)S(1)}, u32[]{:S(2)}, u32[]{:S(2)}) async-start(f32[90,128,4]{0,2,1:T(4,128)} %bitcast.107), calls=%async_computation.2 | async-start | bytes 524288 | tf_op jit(solution)/shard_map/all_to_all | solution.py:172
  203.7 17.8 %collective-permute-start.7 = (f32[4,45,64]{2,1,0:T(8,128)S(1)}, f32[4,45,64]{2,1,0:T(8,128)S(1)}, u32[]{:S(2)}, u32[]{:S(2)}) collective-permute-start(f32[4,45,64]{2,1,0:T(8,128)S(1)} %get-tuple-element.637), channel_id=1, source_target_pairs={{1,0},{2,1},{3,2},{4,3},{5,4},{6,5},{7,6},{8,7},{9,8},{10,9},{11,1... | collective-permute-start | bytes 138248 | tf_op jit(solution)/shard_map/ppermute | solution.py:23
  210.5 10.9 %collective-permute-start.6 = (f32[4,45,64]{2,1,0:T(8,128)S(1)}, f32[4,45,64]{2,1,0:T(8,128)S(1)}, u32[]{:S(2)}, u32[]{:S(2)}) collective-permute-start(f32[4,45,64]{2,1,0:T(8,128)S(1)} %get-tuple-element.636), channel_id=1, source_target_pairs={{0,1},{1,2},{2,3},{3,4},{4,5},{5,6},{6,7},{7,8},{8,9},{9,10},{10,1... | collective-permute-start | bytes 138248 | tf_op jit(solution)/shard_map/ppermute | solution.py:22
  220.2 4.6 %collective-permute-start.8 = (f32[3,512]{1,0:T(4,128)S(1)}, f32[3,512]{1,0:T(4,128)S(1)}, u32[]{:S(2)}, u32[]{:S(2)}) collective-permute-start(f32[3,512]{1,0:T(4,128)S(1)} %slice.1427), channel_id=1, source_target_pairs={{0,128},{1,129},{2,130},{3,131},{4,132},{5,133},{6,134},{7,135},{8... | collective-permute-start | bytes 18440
Sparse Core Ops, SparseCore 0:
  11.5 19.4 all-gather.1
where the time goes:
time: 234 us; the launch traced here: 233 us
  starting transfers between devices  58.3 us (25%)
  local copies, waits for them, and re-layouts  45.5 us (19%)
  waiting for transfers between devices  43.8 us (19%)
  other arithmetic  27.4 us (12%)
  matrix products  18.5 us (8%)
  loops' own time  16.6 us (7%)
  between operations  15.3 us (7%)
  blocking collectives  7.17 us (3%)
    ppermute x4, waiting for transfers between devices, padded(): after = lax.ppermute(first, axis, down)  32.1 us
    ppermute x4, starting transfers between devices, padded(): after = lax.ppermute(first, axis, down)  21.3 us
    dynamic_slice x20, local copies, waits for them, and re-layouts, optical(): lax.dynamic_index_in_dim(level_table, stratum_index, 0, keepdims=False)  16.7 us
    all_to_all x1, starting transfers between devices, per_device(): lax.all_to_all(packed_surface, 'grp', split_axis=2, concat_axis=2, tiled=...  16.3 us
    dynamic_slice x20, local copies, waits for them, and re-layouts, compute_flux_heating(): lax.scan(down_block, down_init, block_ids)  13.3 us
    reduce_sum x90, other arithmetic, up_block(): upward_rows.append(jnp.sum(upward, axis=0))  11.3 us
    all_to_all x1, starting transfers between devices, per_device(): lax.all_to_all(slot_heat, 'grp', split_axis=1, concat_axis=1, tiled=True)  10.5 us
    dot_general x4, matrix products, per_device(): jnp.dot(extended.reshape(-1, extended_span), blend_matrix, precision=TOP)  10.2 us
  transfers between devices with their start and end apart: 13, of which 4 were waited for; matrix products, arithmetic and copies ran while one was open for 40% of the time, Pallas kernels for 0%

commit v1 on v0

v1 whole, which is shorter than its diff:
```python
import functools
import math

import jax
import jax.numpy as jnp
from jax import lax
from jax.experimental import pallas as pl
from jax.experimental.pallas import tpu as pltpu
from jax.sharding import PartitionSpec as P

STEPS = 4
HALO = 64
DIFFUSE = 1.66
LOG2E = math.log2(math.e)
BF = jnp.bfloat16
F32 = jnp.float32

PEERS = 128
SLOTS = 4
COLS = 512
LEV = 45
ROW = 48
FIELDS = 6
FEAT = ROW * FIELDS
CHUNK = SLOTS * FEAT // 128
RAD = 128
GH = 56
REACH = STEPS * HALO
WIDE = COLS + 2 * REACH
SPECIES = 4
NEAR = 6
UNROLL = 9
NT = (((1,), (1,)), ((), ()))
NN = (((1,), (0,)), ((), ()))


def split(x):
    hi = x.astype(BF)
    return hi, (x - hi.astype(F32)).astype(BF)


def dot(a, b, dims):
    return lax.dot_general(a, b, dims, preferred_element_type=F32)


def slot_matrix(position):
    rows = lax.broadcasted_iota(jnp.int32, (COLS, COLS), 0)
    slot = (rows & (PEERS - 1)) * SLOTS + (rows >> 7)
    return jnp.where(slot == position, 1.0, 0.0).astype(BF)


def pack_kernel(temp, thick, tracers, ground, sun, day, pos, adj, coef, send, right, left, table, bundle):
    fields = [temp[...], thick[...]] + [tracers[s] for s in range(SPECIES)]
    for k, field in enumerate(fields):
        bundle[k * ROW : k * ROW + LEV, :] = field
        if k:
            bundle[k * ROW + LEV : (k + 1) * ROW, :] = jnp.zeros((ROW - LEV, COLS), F32)
    sunny = sun[...]
    bundle[LEV : LEV + 1, :] = ground[...]
    bundle[LEV + 1 : LEV + 2, :] = sunny
    bundle[LEV + 2 : LEV + 3, :] = day[...].astype(F32) * sunny
    tail = bundle[256:288, :]
    for k in range(1, 4):
        bundle[256 + 32 * k : 288 + 32 * k, :] = tail
    placing = slot_matrix(pos[...])
    hi, lo = split(bundle[...])
    packed = dot(placing, hi, NT) + dot(placing, lo, NT)
    lane = lax.broadcasted_iota(jnp.int32, (PEERS, 128), 1) >> 5
    last = jnp.zeros((PEERS, 128), F32)
    for m in range(SLOTS):
        block = packed[m * PEERS : (m + 1) * PEERS, :]
        send[pl.ds(2 * m, PEERS, CHUNK), :] = block[:, 0:128]
        send[pl.ds(2 * m + 1, PEERS, CHUNK), :] = block[:, 128:256]
        last = jnp.where(lane == m, block[:, 256:384], last)
    send[pl.ds(CHUNK - 1, PEERS, CHUNK), :] = last
    body = SPECIES * ROW
    right[0:body, :] = bundle[2 * ROW : FEAT, COLS - REACH :]
    left[0:body, :] = bundle[2 * ROW : FEAT, :REACH]
    column = lax.broadcasted_iota(jnp.int32, (NEAR, COLS), 1)
    reach = (adj[...] - column).astype(F32)
    pad = jnp.zeros((2, COLS), F32)
    both = jnp.concatenate([reach, pad, coef[...], pad], axis=0)
    table[...] = both
    right[body : body + 16, :] = both[:, COLS - REACH :]
    left[body : body + 16, :] = both[:, :REACH]


def pool_kernel(arrived, member, pooled, stage):
    ids = member[...] >> 2
    rows = lax.broadcasted_iota(jnp.int32, (RAD, 128), 0)
    lane = lax.broadcasted_iota(jnp.int32, (PEERS, 128), 1) >> 5
    last = arrived[pl.ds(CHUNK - 1, PEERS, CHUNK), :]
    chosen = []
    for m in range(SLOTS):
        chosen.append(jnp.where(rows == ids[m : m + 1, :], 0.25, 0.0).astype(BF))
        span = slice(m * PEERS, (m + 1) * PEERS)
        stage[span, 0:128] = arrived[pl.ds(2 * m, PEERS, CHUNK), :]
        stage[span, 128:256] = arrived[pl.ds(2 * m + 1, PEERS, CHUNK), :]
        stage[span, 256:384] = jnp.where(lane == m, last, 0.0)
    selector = jnp.concatenate(chosen, axis=1)
    hi, lo = split(stage[...])
    total = dot(selector, hi, NN) + dot(selector, lo, NN)
    pooled[0:128, :] = total[:, 0:128].T
    pooled[128:256, :] = total[:, 128:256].T
    tail = total[:, 256:384].T
    pooled[256:288, :] = tail[0:32] + tail[32:64] + tail[64:96] + tail[96:128]


def flux_kernel(side, own, other, opacity, emission, sunshine, mine, theirs, fields, warm, kept, sums, net):
    me = side[0]
    fields[pl.ds(me, 1)] = own[...][None]
    fields[pl.ds(1 - me, 1)] = other[...][None]
    for h in range(2):
        warm[h] = jnp.square(jnp.square(fields[h, 0:ROW, :]))
        fields[h, 2 * ROW : FEAT, :] = fields[h, 2 * ROW : FEAT, :] * (-DIFFUSE * LOG2E)
    surface = own[40:48, :]
    ground4 = jnp.square(jnp.square(surface[5:6, :]))
    slant = 1.0 / (DIFFUSE * surface[6:7, :])
    slant = jnp.broadcast_to(slant, (GH, RAD))
    insolation = surface[7:8, :]
    emit = jnp.broadcast_to(emission[...], (GH, RAD))

    def fold(x):
        return jnp.sum(x.reshape(GH // 8, 8, RAD), axis=0)

    def down(h, block, carry):
        thermal, direct = carry
        start = h * LEV + block * UNROLL
        shift = lax.rem(128 - start, 128)
        coeffs = [pltpu.roll(opacity[s], shift, 1) for s in range(SPECIES)]
        for i in range(UNROLL):
            inner = block * UNROLL + i
            tau = None
            for s in range(SPECIES):
                amount = fields[h, pl.ds((2 + s) * ROW + inner, 1), :]
                term = jnp.broadcast_to(coeffs[s][:, i : i + 1], (GH, RAD)) * amount
                tau = term if tau is None else tau + term
            opaque = 1.0 - jnp.exp2(tau)
            kept[start + i] = opaque
            source = emit * warm[h, pl.ds(inner, 1), :]
            gain = opaque * (thermal - source)
            thermal = thermal - gain
            passed = direct * jnp.exp2(tau * slant)
            sums[pl.ds(8 * (start + i), 8), :] = fold(gain + (direct - passed))
            direct = passed
        return thermal, direct

    def up(h, block, upward):
        start = h * LEV + block * UNROLL
        for i in range(UNROLL - 1, -1, -1):
            source = emit * warm[h, pl.ds(block * UNROLL + i, 1), :]
            gain = kept[start + i] * (upward - source)
            upward = upward - gain
            rows = pl.ds(8 * (start + i), 8)
            sums[rows, :] = sums[rows, :] + fold(gain)
        return upward

    blocks = LEV // UNROLL
    carry = (jnp.zeros((GH, RAD), F32), sunshine[...] * insolation)
    for h in range(2):
        carry = lax.fori_loop(0, blocks, functools.partial(down, h), carry)
    upward = emit * ground4
    for h in (1, 0):
        upward = lax.fori_loop(0, blocks, lambda b, u, h=h: up(h, blocks - 1 - b, u), upward)
    for h in range(2):
        total = None
        for k in range(8):
            part = sums[pl.ds(8 * LEV * h + k, LEV, 8), :]
            total = part if total is None else total + part
        net[h, 0:LEV, :] = total
        net[h, LEV:ROW, :] = jnp.zeros((ROW - LEV, RAD), F32)
    mine[...] = net[pl.ds(me, 1)][0]
    theirs[...] = net[pl.ds(1 - me, 1)][0]


def spread_kernel(mine, gotten, own, member, send):
    heat = (mine[...] + gotten[...]) / own[ROW : 2 * ROW, :]
    rows = lax.broadcasted_iota(jnp.int32, (ROW, RAD), 0)
    heat = jnp.where(rows < LEV, heat, 0.0)
    gap = jnp.zeros((16, RAD), F32)
    hi, lo = split(jnp.concatenate([heat, gap, heat, gap], axis=0))
    ids = member[...] >> 2
    lanes = lax.broadcasted_iota(jnp.int32, (PEERS, RAD), 1)
    for h in range(2):
        parts = []
        for m in (2 * h, 2 * h + 1):
            selector = jnp.where(lanes == ids[:, m : m + 1], 1.0, 0.0).astype(BF)
            parts.append(dot(selector, hi, NT) + dot(selector, lo, NT))
        send[pl.ds(h, PEERS, 2), :] = jnp.where(lanes < 64, parts[0], parts[1])


def unplace_kernel(returned, pos, heating):
    parts = []
    for h in range(2):
        turned = returned[pl.ds(h, PEERS, 2), :].T
        parts += [turned[0:ROW, :], turned[64 : 64 + ROW, :]]
    hi, lo = split(jnp.concatenate(parts, axis=1))
    placing = slot_matrix(pos[...])
    heating[...] = (dot(hi, placing, NN) + dot(lo, placing, NN))[0:LEV, :]


def mix_kernel(tracers, table, from_left, from_right, mixed, high, low, band):
    body = SPECIES * ROW
    hi, lo = split(from_left[0:body, :])
    high[0, :, 0:REACH] = hi
    low[0, :, 0:REACH] = lo
    hi, lo = split(from_right[0:body, :])
    high[0, :, REACH + COLS :] = hi
    low[0, :, REACH + COLS :] = lo
    for s in range(SPECIES):
        fill = jnp.concatenate([tracers[s], jnp.zeros((ROW - LEV, COLS), F32)], axis=0)
        hi, lo = split(fill)
        high[0, s * ROW : (s + 1) * ROW, REACH : REACH + COLS] = hi
        low[0, s * ROW : (s + 1) * ROW, REACH : REACH + COLS] = lo
    tables = jnp.concatenate([from_left[body:, :], table[...], from_right[body:, :]], axis=1)
    shifted = pltpu.roll(tables, WIDE - HALO, 1)
    rows = lax.broadcasted_iota(jnp.int32, (256, 128), 0).astype(F32)
    lanes = lax.broadcasted_iota(jnp.int32, (1, 128), 1).astype(F32)

    def build(source, k):
        part = source[:, k * 128 : (k + 1) * 128]
        blend = jnp.where(rows == lanes + HALO, 1.0 - jnp.sum(part[8:14, :], axis=0, keepdims=True), 0.0)
        for n in range(NEAR):
            blend = blend + jnp.where(rows == lanes + part[n : n + 1, :], part[8 + n : 9 + n, :], 0.0)
        return split(blend)

    for k in range(7):
        hi, lo = build(shifted, k)
        band[0, 0, k] = hi
        band[0, 1, k] = lo
    for k in range(6):
        hi, lo = build(tables, k + 1)
        band[1, 0, k] = hi
        band[1, 1, k] = lo
    for step in range(STEPS):
        now, later = step % 2, (step + 1) % 2
        tiles = 7 - step
        first = step // 2
        for k in range(tiles):
            window = slice(k * 128, k * 128 + 256)
            bh, bl = band[now, 0, k + first], band[now, 1, k + first]
            xh, xl = high[now, :, window], low[now, :, window]
            new = dot(xh, bh, NN) + (dot(xh, bl, NN) + dot(xl, bh, NN))
            if step < STEPS - 1:
                hi, lo = split(new)
                high[later, :, k * 128 : (k + 1) * 128] = hi
                low[later, :, k * 128 : (k + 1) * 128] = lo
            else:
                for s in range(SPECIES):
                    mixed[s, :, k * 128 : (k + 1) * 128] = new[s * ROW : s * ROW + LEV, :]


def shape(*dims):
    return jax.ShapeDtypeStruct(dims, F32)


def per_device(
    stratum_warmth_anomaly,
    pressure_depth,
    absorber_amounts,
    ground_warmth_anomaly,
    sun_elevation_factor,
    daytime_mask,
    dispatch_position,
    arrival_membership,
    adjacency_table,
    blending_coefficient,
    opacity_table,
    emission_share,
    sunshine_share,
):
    n = lax.axis_size("grp")
    up = [(i, (i + 1) % n) for i in range(n)]
    down = [(j, i) for i, j in up]
    swap = [(0, 1), (1, 0)]
    halo_rows = SPECIES * ROW + 16

    send, right, left, table = pl.pallas_call(
        pack_kernel,
        out_shape=(shape(PEERS * CHUNK, 128), shape(halo_rows, REACH), shape(halo_rows, REACH), shape(16, COLS)),
        scratch_shapes=[pltpu.VMEM((384, COLS), F32)],
        name="pack",
    )(
        stratum_warmth_anomaly,
        pressure_depth,
        absorber_amounts,
        ground_warmth_anomaly[None],
        sun_elevation_factor[None],
        daytime_mask[None],
        dispatch_position,
        adjacency_table,
        blending_coefficient,
    )
    from_left = lax.ppermute(right, "grp", up)
    from_right = lax.ppermute(left, "grp", down)
    arrived = lax.all_to_all(
        send.reshape(PEERS * CHUNK, 1, 128), "grp", split_axis=0, concat_axis=0, tiled=True
    ).reshape(PEERS * CHUNK, 128)

    mixed = pl.pallas_call(
        mix_kernel,
        out_shape=shape(SPECIES, LEV, COLS),
        scratch_shapes=[
            pltpu.VMEM((2, SPECIES * ROW, WIDE), BF),
            pltpu.VMEM((2, SPECIES * ROW, WIDE), BF),
            pltpu.VMEM((2, 2, 7, 256, 128), BF),
        ],
        name="mix",
    )(absorber_amounts, table, from_left, from_right)

    members = arrival_membership.reshape(PEERS, SLOTS)
    pooled = pl.pallas_call(
        pool_kernel,
        out_shape=shape(FEAT, RAD),
        scratch_shapes=[pltpu.VMEM((COLS, 384), F32)],
        name="pool",
    )(arrived, members.T)
    other = lax.ppermute(pooled, "sec", swap)
    side = lax.axis_index("sec").astype(jnp.int32)[None]
    opacity = jnp.pad(opacity_table, ((0, 0), (0, 0), (0, 128 - 2 * LEV)))
    mine, theirs = pl.pallas_call(
        flux_kernel,
        out_shape=(shape(ROW, RAD), shape(ROW, RAD)),
        in_specs=[pl.BlockSpec(memory_space=pltpu.SMEM)] + [pl.BlockSpec(memory_space=pltpu.VMEM)] * 5,
        scratch_shapes=[
            pltpu.VMEM((2, FEAT, RAD), F32),
            pltpu.VMEM((2, ROW, RAD), F32),
            pltpu.VMEM((2 * LEV, GH, RAD), F32),
            pltpu.VMEM((2 * LEV * 8, RAD), F32),
            pltpu.VMEM((2, ROW, RAD), F32),
        ],
        name="flux",
    )(side, pooled, other, opacity, emission_share[:, None], sunshine_share[:, None])
    gotten = lax.ppermute(theirs, "sec", swap)
    back = pl.pallas_call(spread_kernel, out_shape=shape(PEERS * 2, 128), name="spread")(
        mine, gotten, pooled, members
    )
    returned = lax.all_to_all(
        back.reshape(PEERS * 2, 1, 128), "grp", split_axis=0, concat_axis=0, tiled=True
    ).reshape(PEERS * 2, 128)
    heating = pl.pallas_call(unplace_kernel, out_shape=shape(LEV, COLS), name="unplace")(
        returned, dispatch_position
    )
    return (heating, mixed)


def solution(mesh):
    in_specs = (
        P("sec", "grp"),
        P("sec", "grp"),
        P(None, "sec", "grp"),
        P("grp"),
        P("grp"),
        P("grp"),
        P("grp", None),
        P("grp", None),
        P(None, "grp"),
        P(None, "grp"),
        P(None, "sec", None),
        P("sec"),
        P("sec"),
    )
    out_specs = (P("sec", "grp"), P(None, "sec", "grp"))
    return jax.shard_map(
        per_device, mesh=mesh, in_specs=in_specs, out_specs=out_specs, check_vma=False
    )
```

time: 234 us -> 93.6 us (0.40)
  local copies, waits for them, and re-layouts: 45.5 us -> 12 us
  other arithmetic: 27.4 us -> 0.66 us
  starting transfers between devices: 58.3 us -> 34 us
  Pallas kernels: 0 us -> 20.8 us
  waiting for transfers between devices: 43.8 us -> 24.9 us
  matrix products: 18.5 us -> 0 us
  loops' own time: 16.6 us -> 0 us
  between operations: 15.3 us -> 0.69 us
  blocking collectives: 7.17 us -> 0 us
    ppermute x8 -> x4, waiting for transfers between devices: 39.5 us -> 8.82 us  [the longest x1 7.41 us: per_device(): from_left = lax.ppermute(right, 'grp', up)]
    dynamic_slice x40 -> x0, local copies, waits for them, and re-layouts: 30 us -> none  [the longest x20 16.7 us: optical(): lax.dynamic_index_in_dim(level_table, stratum_index, 0, keepdims=False)]
    reduce_sum x271 -> x0, other arithmetic: 26.5 us -> none  [the longest x90 11.3 us: up_block(): upward_rows.append(jnp.sum(upward, axis=0))]
    pallas_call x0 -> x6, Pallas kernels: none -> 20.8 us  [the longest x1 6.68 us: per_device(): pl.pallas_call(flux_kernel, out_shape=(shape(ROW, RAD), shape(ROW, RAD)),...]
    dot_general x10 -> x0, matrix products: 18.5 us -> none  [the longest x4 10.2 us: per_device(): jnp.dot(extended.reshape(-1, extended_span), blend_matrix, precision=TOP)]
    another operation x2 -> x0, loops' own time: 16.6 us -> none  [the longest x1 8.55 us: compute_flux_heating(): lax.scan(down_block, down_init, block_ids)]
    all_to_all x3 -> x2, waiting for transfers between devices: 4.19 us -> 16.1 us  [the longest x1 16.1 us: per_device(): lax.all_to_all(send.reshape(PEERS * CHUNK, 1, 128), 'grp', split_axis=0,...]
    ppermute x8 -> x4, starting transfers between devices: 22.1 us -> 10.5 us  [the longest x1 6.46 us: per_device(): from_right = lax.ppermute(left, 'grp', down)]
  transfers between devices with their start and end apart: 13 -> 6, of which waited for: 4 -> 3; matrix products, arithmetic and copies ran while one was open for 40% -> 6% of each run, Pallas kernels for 0% -> 6%
where the time goes in v1:
time: 93.6 us; the launch traced here: 93.1 us
  starting transfers between devices  34 us (36%)
  waiting for transfers between devices  24.9 us (27%)
  Pallas kernels  20.8 us (22%)
  local copies, waits for them, and re-layouts  12 us (13%)
    all_to_all x1, starting transfers between devices, per_device(): lax.all_to_all(send.reshape(PEERS * CHUNK, 1, 128), 'grp', split_axis=0,...  16.5 us
    all_to_all x1, waiting for transfers between devices, per_device(): lax.all_to_all(send.reshape(PEERS * CHUNK, 1, 128), 'grp', split_axis=0,...  16.1 us
    unnamed x29, local copies, waits for them, and re-layouts  9.18 us
    ppermute x1, waiting for transfers between devices, per_device(): from_left = lax.ppermute(right, 'grp', up)  7.41 us
    all_to_all x1, starting transfers between devices, per_device(): lax.all_to_all(back.reshape(PEERS * 2, 1, 128), 'grp', split_axis=0, conc...  7.07 us
    pallas_call x1, Pallas kernels, per_device(): pl.pallas_call(flux_kernel, out_shape=(shape(ROW, RAD), shape(ROW, RAD)),...  6.68 us
    ppermute x1, starting transfers between devices, per_device(): from_right = lax.ppermute(left, 'grp', down)  6.46 us
    pallas_call x1, Pallas kernels, per_device(): pl.pallas_call(mix_kernel, out_shape=shape(SPECIES, LEV, COLS), scratch_s...  5.32 us
  transfers between devices with their start and end apart: 6, of which 3 were waited for; matrix products, arithmetic and copies ran while one was open for 6% of the time, Pallas kernels for 6%

profile of v1, /device:TPU:1, one launch (start us, length us, event | category | flops | bytes accessed | tf_op | source)
XLA Modules:
  0.0 93.1 jit_solution(13530779350166235085)
XLA Ops:
  0.6 1.9 %copy.27.tracers = f32[4,45,512]{2,1,0:T(8,128)} copy(f32[4,45,512]{2,0,1:T(4,128)} %param.15) | data formatting | bytes 737280 | tf_op args[2]
  2.5 2.8 %pack.1 = (f32[1152,128]{1,0:T(8,128)}, f32[208,256]{1,0:T(8,128)}, f32[208,256]{1,0:T(8,128)}, f32[16,512]{1,0:T(8,128)}) custom-call(f32[45,512]{1,0:T(8,128)} %temp.1, f32[45,512]{1,0:T(8,128)} %thick.1, f32[4,45,512]{2,1,0:T(8,128)} %copy.27.tracers, f32[1,512]{1,0:T(1,128)} %bitcast.20, f32[1,512]{1,0:T(1,128)} %bitcast.21, s32[1,512]{1,0:T(1,128)} %bitcast.22, ...), custom_call_target="tpu_custom_call" | custom-call | tf_op jit(solution)/shard_map/pack/pallas_call | solution.py:278
  5.3 0.0 copy-start.8
  5.3 16.5 %all-to-all-start = ((f32[1152,1,128]{2,1,0:T(1,128)}), f32[1152,1,128]{2,1,0:T(1,128)S(1)}, u32[]{:S(2)}, u32[]{:S(2)}) async-start(f32[1152,1,128]{2,1,0:T(1,128)} %bitcast.16), calls=%async_computation | async-start | bytes 1179648 | tf_op jit(solution)/shard_map/all_to_all | solution.py:296
  21.7 0.5 broadcast.5
  22.2 0.0 copy-done.8
  22.2 0.7 reduce.3
  22.9 0.1 reshape.21.member
  23.0 0.0 copy-start.1
  23.0 0.7 copy.29
  23.7 16.1 %all-to-all-done = f32[1152,1,128]{2,1,0:T(1,128)S(1)} async-done(((f32[1152,1,128]{2,1,0:T(1,128)}), f32[1152,1,128]{2,1,0:T(1,128)S(1)}, u32[]{:S(2)}, u32[]{:S(2)}) %all-to-all-start) | async-done | bytes 589856 | tf_op jit(solution)/shard_map/all_to_all | solution.py:296
  39.8 0.0 copy-start
  39.8 0.8 copy-done
  40.6 0.0 copy-start.6
  40.6 2.2 %pool.1.own = f32[288,128]{1,0:T(8,128)} custom-call(f32[1152,128]{1,0:T(8,128)} %bitcast.15, s32[4,128]{1,0:T(4,128)} %bitcast.19), custom_call_target="tpu_custom_call" | custom-call | tf_op jit(solution)/shard_map/pool/pallas_call | solution.py:312
  42.8 0.0 copy-done.1
  42.8 3.4 %collective-permute-start = (f32[288,128]{1,0:T(8,128)}, f32[288,128]{1,0:T(8,128)S(1)}, u32[]{:S(2)}, u32[]{:S(2)}) collective-permute-start(f32[288,128]{1,0:T(8,128)} %pool.1.own), channel_id=1, source_target_pairs={{0,128},{128,0},{1,129},{129,1},{2,130},{130,2},{3,131},{131,3},{4... | collective-permute-start | bytes 442376 | tf_op jit(solution)/shard_map/ppermute | solution.py:318
  46.2 0.0 copy-start.9
  46.2 0.7 copy-done.9
  46.8 0.7 copy.30.emission
  47.5 0.0 copy-start.10
  47.5 0.7 copy-done.10
  48.2 0.7 copy.31.sunshine
  48.9 0.0 copy-done.6
  48.9 0.7 pad.4.opacity
  49.6 0.0 collective-permute-done.other
  49.6 0.0 copy-start.5
  49.6 0.6 copy-done.5
  50.2 6.7 %flux.1 = (f32[48,128]{1,0:T(8,128)}, f32[48,128]{1,0:T(8,128)}) custom-call(s32[1]{0:T(128)} %bitcast.side, f32[288,128]{1,0:T(8,128)} %pool.1.own, f32[288,128]{1,0:T(8,128)} %copy-done.5, f32[4,56,128]{2,1,0:T(8,128)} %pad.4.opacity, f32[56,1]{1,0:T(8,128)} %copy.30.emission, f32[56,1]{1,0:T(8,128)} %copy.31.sunshine), custom_call_target="tpu_custom_call" | custom-call | tf_op jit(solution)/shard_map/flux/pallas_call | solution.py:321
  56.9 0.0 collective-permute-start.1
  56.9 1.4 %collective-permute-done.1.gotten = f32[48,128]{1,0:T(8,128)S(1)} collective-permute-done((f32[48,128]{1,0:T(8,128)}, f32[48,128]{1,0:T(8,128)S(1)}, u32[]{:S(2)}, u32[]{:S(2)}) %collective-permute-start.1) | collective-permute-done | bytes 24608 | tf_op jit(solution)/shard_map/ppermute | solution.py:334
  58.3 0.0 copy-start.7
  58.3 0.6 copy-done.7
  58.9 0.0 copy-start.12
  58.9 2.0 %spread.1 = f32[256,128]{1,0:T(8,128)} custom-call(f32[48,128]{1,0:T(8,128)} %get-tuple-element.9.mine, f32[48,128]{1,0:T(8,128)} %copy-done.7, f32[288,128]{1,0:T(8,128)} %pool.1.own, s32[128,4]{1,0:T(8,128)} %copy-done.1), custom_call_target="tpu_custom_call" | custom-call | tf_op jit(solution)/shard_map/spread/pallas_call | solution.py:335
  60.9 0.0 copy-start.11
  60.9 7.1 %all-to-all-start.1 = ((f32[256,1,128]{2,1,0:T(1,128)}), f32[256,1,128]{2,1,0:T(1,128)S(1)}, u32[]{:S(2)}, u32[]{:S(2)}) async-start(f32[256,1,128]{2,1,0:T(1,128)} %bitcast.17), calls=%async_computation.1 | async-start | bytes 262144 | tf_op jit(solution)/shard_map/all_to_all | solution.py:338
  68.0 0.0 copy-done.12
  68.0 0.7 collective-permute-start.2
  68.6 0.0 copy-done.11
  68.6 6.5 %collective-permute-start.3 = (f32[208,256]{1,0:T(8,128)S(1)}, f32[208,256]{1,0:T(8,128)S(1)}, u32[]{:S(2)}, u32[]{:S(2)}) collective-permute-start(f32[208,256]{1,0:T(8,128)S(1)} %copy-done.11), channel_id=1, source_target_pairs={{1,0},{2,1},{3,2},{4,3},{5,4},{6,5},{7,6},{8,7},{9,8},{10,9},{11,1... | collective-permute-start | bytes 638984 | tf_op jit(solution)/shard_map/ppermute | solution.py:295
  75.1 7.4 %collective-permute-done.2.from_left = f32[208,256]{1,0:T(8,128)S(1)} collective-permute-done((f32[208,256]{1,0:T(8,128)S(1)}, f32[208,256]{1,0:T(8,128)S(1)}, u32[]{:S(2)}, u32[]{:S(2)}) %collective-permute-start.2) | collective-permute-done | bytes 213024 | tf_op jit(solution)/shard_map/ppermute | solution.py:294
  82.5 0.0 copy-start.3
  82.5 0.0 collective-permute-done.3.from_right
  82.5 0.0 copy-start.4
  82.5 0.7 copy-done.3
  83.2 0.1 copy-done.4
  83.3 5.3 %mix.1 = f32[4,45,512]{2,1,0:T(8,128)} custom-call(f32[4,45,512]{2,1,0:T(8,128)} %copy.27.tracers, f32[16,512]{1,0:T(8,128)} %get-tuple-element.11.table, f32[208,256]{1,0:T(8,128)} %copy-done.3, f32[208,256]{1,0:T(8,128)} %copy-done.4), custom_call_target="tpu_custom_call" | custom-call | tf_op jit(solution)/shard_map/mix/pallas_call | solution.py:300
  88.6 2.0 %copy.34 = f32[4,45,512]{2,0,1:T(4,128)} copy(f32[4,45,512]{2,1,0:T(8,128)} %mix.1) | data formatting | bytes 737280
  90.6 0.0 all-to-all-done.1
  90.6 0.0 copy-start.2
  90.6 0.6 copy-done.2
  91.2 1.9 %unplace.1 = f32[45,512]{1,0:T(8,128)} custom-call(f32[256,128]{1,0:T(8,128)} %bitcast.18, s32[1,512]{1,0:T(1,128)} %pos.3), custom_call_target="tpu_custom_call" | custom-call | tf_op jit(solution)/shard_map/unplace/pallas_call | solution.py:341
Async XLA Ops:
  5.3 17.0 %copy-start.8 = (s32[1,512]{1,0:T(1,128)S(1)}, s32[1,512]{1,0:T(1,128)}, u32[]{:S(2)}) copy-start(s32[1,512]{1,0:T(1,128)} %param.20) | copy-start | bytes 6148
  5.3 34.5 %all-to-all-start = ((f32[1152,1,128]{2,1,0:T(1,128)}), f32[1152,1,128]{2,1,0:T(1,128)S(1)}, u32[]{:S(2)}, u32[]{:S(2)}) async-start(f32[1152,1,128]{2,1,0:T(1,128)} %bitcast.16), calls=%async_computation | async-start | bytes 1179648 | tf_op jit(solution)/shard_map/all_to_all | solution.py:296
  23.0 19.8 %copy-start.1 = (s32[128,4]{1,0:T(8,128)}, s32[128,4]{1,0:T(8,128)S(1)}, u32[]{:S(2)}) copy-start(s32[128,4]{1,0:T(8,128)S(1)} %reshape.21.member) | copy-start | bytes 6148
  39.8 0.8 copy-start
  40.6 8.3 %copy-start.6 = (f32[4,56,90]{2,1,0:T(8,128)S(1)}, f32[4,56,90]{2,1,0:T(8,128)}, u32[]{:S(2)}) copy-start(f32[4,56,90]{2,1,0:T(8,128)} %param.23) | copy-start | bytes 241924
  42.8 6.8 %collective-permute-start = (f32[288,128]{1,0:T(8,128)}, f32[288,128]{1,0:T(8,128)S(1)}, u32[]{:S(2)}, u32[]{:S(2)}) collective-permute-start(f32[288,128]{1,0:T(8,128)} %pool.1.own), channel_id=1, source_target_pairs={{0,128},{128,0},{1,129},{129,1},{2,130},{130,2},{3,131},{131,3},{4... | collective-permute-start | bytes 442376 | tf_op jit(solution)/shard_map/ppermute | solution.py:318
  46.2 0.7 copy-start.9
  47.5 0.7 copy-start.10
  49.6 0.6 copy-start.5
  56.9 1.4 %collective-permute-start.1 = (f32[48,128]{1,0:T(8,128)}, f32[48,128]{1,0:T(8,128)S(1)}, u32[]{:S(2)}, u32[]{:S(2)}) collective-permute-start(f32[48,128]{1,0:T(8,128)} %get-tuple-element.10), channel_id=1, source_target_pairs={{0,128},{128,0},{1,129},{129,1},{2,130},{130,2},{3,131},{131,3},{4... | collective-permute-start | bytes 73736 | tf_op jit(solution)/shard_map/ppermute | solution.py:334
  58.3 0.6 copy-start.7
  58.9 9.1 %copy-start.12 = (f32[208,256]{1,0:T(8,128)S(1)}, f32[208,256]{1,0:T(8,128)}, u32[]{:S(2)}) copy-start(f32[208,256]{1,0:T(8,128)} %get-tuple-element.12) | copy-start | bytes 638980
  60.9 7.7 %copy-start.11 = (f32[208,256]{1,0:T(8,128)S(1)}, f32[208,256]{1,0:T(8,128)}, u32[]{:S(2)}) copy-start(f32[208,256]{1,0:T(8,128)} %get-tuple-element.13) | copy-start | bytes 638980
  60.9 29.7 %all-to-all-start.1 = ((f32[256,1,128]{2,1,0:T(1,128)}), f32[256,1,128]{2,1,0:T(1,128)S(1)}, u32[]{:S(2)}, u32[]{:S(2)}) async-start(f32[256,1,128]{2,1,0:T(1,128)} %bitcast.17), calls=%async_computation.1 | async-start | bytes 262144 | tf_op jit(solution)/shard_map/all_to_all | solution.py:338
  68.0 14.5 %collective-permute-start.2 = (f32[208,256]{1,0:T(8,128)S(1)}, f32[208,256]{1,0:T(8,128)S(1)}, u32[]{:S(2)}, u32[]{:S(2)}) collective-permute-start(f32[208,256]{1,0:T(8,128)S(1)} %copy-done.12), channel_id=1, source_target_pairs={{0,1},{1,2},{2,3},{3,4},{4,5},{5,6},{6,7},{7,8},{8,9},{9,10},{10,1... | collective-permute-start | bytes 638984 | tf_op jit(solution)/shard_map/ppermute | solution.py:294
  68.6 13.9 %collective-permute-start.3 = (f32[208,256]{1,0:T(8,128)S(1)}, f32[208,256]{1,0:T(8,128)S(1)}, u32[]{:S(2)}, u32[]{:S(2)}) collective-permute-start(f32[208,256]{1,0:T(8,128)S(1)} %copy-done.11), channel_id=1, source_target_pairs={{1,0},{2,1},{3,2},{4,3},{5,4},{6,5},{7,6},{8,7},{9,8},{10,9},{11,1... | collective-permute-start | bytes 638984 | tf_op jit(solution)/shard_map/ppermute | solution.py:295
  82.5 0.7 copy-start.3
  82.5 0.8 copy-start.4
  90.6 0.6 copy-start.2

commit v2 on v1

--- a/solution.py
+++ b/solution.py
@@ -20,8 +20,9 @@
 COLS = 512
 LEV = 45
 ROW = 48
-FIELDS = 6
-FEAT = ROW * FIELDS
+BASE = 2 * ROW
+BODY = 192
+FEAT = BASE + BODY
 CHUNK = SLOTS * FEAT // 128
 RAD = 128
 GH = 56
@@ -50,11 +51,13 @@
 
 
 def pack_kernel(temp, thick, tracers, ground, sun, day, pos, adj, coef, send, right, left, table, bundle):
-    fields = [temp[...], thick[...]] + [tracers[s] for s in range(SPECIES)]
-    for k, field in enumerate(fields):
-        bundle[k * ROW : k * ROW + LEV, :] = field
-        if k:
-            bundle[k * ROW + LEV : (k + 1) * ROW, :] = jnp.zeros((ROW - LEV, COLS), F32)
+    bundle[0:LEV, :] = temp[...]
+    bundle[ROW : ROW + LEV, :] = thick[...]
+    bundle[ROW + LEV : BASE, :] = jnp.zeros((ROW - LEV, COLS), F32)
+    spare = BASE + LEV * SPECIES
+    bundle[spare:FEAT, :] = jnp.zeros((FEAT - spare, COLS), F32)
+    for l in range(LEV):
+        bundle[BASE + SPECIES * l : BASE + SPECIES * (l + 1), :] = tracers[l]
     sunny = sun[...]
     bundle[LEV : LEV + 1, :] = ground[...]
     bundle[LEV + 1 : LEV + 2, :] = sunny
@@ -73,16 +76,15 @@
         send[pl.ds(2 * m + 1, PEERS, CHUNK), :] = block[:, 128:256]
         last = jnp.where(lane == m, block[:, 256:384], last)
     send[pl.ds(CHUNK - 1, PEERS, CHUNK), :] = last
-    body = SPECIES * ROW
-    right[0:body, :] = bundle[2 * ROW : FEAT, COLS - REACH :]
-    left[0:body, :] = bundle[2 * ROW : FEAT, :REACH]
+    right[0:BODY, :] = bundle[BASE:FEAT, COLS - REACH :]
+    left[0:BODY, :] = bundle[BASE:FEAT, :REACH]
     column = lax.broadcasted_iota(jnp.int32, (NEAR, COLS), 1)
     reach = (adj[...] - column).astype(F32)
     pad = jnp.zeros((2, COLS), F32)
     both = jnp.concatenate([reach, pad, coef[...], pad], axis=0)
     table[...] = both
-    right[body : body + 16, :] = both[:, COLS - REACH :]
-    left[body : body + 16, :] = both[:, :REACH]
+    right[BODY : BODY + 16, :] = both[:, COLS - REACH :]
+    left[BODY : BODY + 16, :] = both[:, :REACH]
 
 
 def pool_kernel(arrived, member, pooled, stage):
@@ -112,7 +114,7 @@
     fields[pl.ds(1 - me, 1)] = other[...][None]
     for h in range(2):
         warm[h] = jnp.square(jnp.square(fields[h, 0:ROW, :]))
-        fields[h, 2 * ROW : FEAT, :] = fields[h, 2 * ROW : FEAT, :] * (-DIFFUSE * LOG2E)
+        fields[h, BASE:FEAT, :] = fields[h, BASE:FEAT, :] * (-DIFFUSE * LOG2E)
     surface = own[40:48, :]
     ground4 = jnp.square(jnp.square(surface[5:6, :]))
     slant = 1.0 / (DIFFUSE * surface[6:7, :])
@@ -132,7 +134,7 @@
             inner = block * UNROLL + i
             tau = None
             for s in range(SPECIES):
-                amount = fields[h, pl.ds((2 + s) * ROW + inner, 1), :]
+                amount = fields[h, pl.ds(BASE + SPECIES * inner + s, 1), :]
                 term = jnp.broadcast_to(coeffs[s][:, i : i + 1], (GH, RAD)) * amount
                 tau = term if tau is None else tau + term
             opaque = 1.0 - jnp.exp2(tau)
@@ -174,7 +176,7 @@
 
 
 def spread_kernel(mine, gotten, own, member, send):
-    heat = (mine[...] + gotten[...]) / own[ROW : 2 * ROW, :]
+    heat = (mine[...] + gotten[...]) / own[ROW:BASE, :]
     rows = lax.broadcasted_iota(jnp.int32, (ROW, RAD), 0)
     heat = jnp.where(rows < LEV, heat, 0.0)
     gap = jnp.zeros((16, RAD), F32)
@@ -199,20 +201,17 @@
     heating[...] = (dot(hi, placing, NN) + dot(lo, placing, NN))[0:LEV, :]
 
 
-def mix_kernel(tracers, table, from_left, from_right, mixed, high, low, band):
-    body = SPECIES * ROW
-    hi, lo = split(from_left[0:body, :])
-    high[0, :, 0:REACH] = hi
-    low[0, :, 0:REACH] = lo
-    hi, lo = split(from_right[0:body, :])
-    high[0, :, REACH + COLS :] = hi
-    low[0, :, REACH + COLS :] = lo
-    for s in range(SPECIES):
-        fill = jnp.concatenate([tracers[s], jnp.zeros((ROW - LEV, COLS), F32)], axis=0)
-        hi, lo = split(fill)
-        high[0, s * ROW : (s + 1) * ROW, REACH : REACH + COLS] = hi
-        low[0, s * ROW : (s + 1) * ROW, REACH : REACH + COLS] = lo
-    tables = jnp.concatenate([from_left[body:, :], table[...], from_right[body:, :]], axis=1)
+def mix_kernel(tracers, table, from_left, from_right, mixed, high, low, band, stage):
+    spare = LEV * SPECIES
+    stage[spare:BODY, :] = jnp.zeros((BODY - spare, COLS), F32)
+    for l in range(LEV):
+        stage[SPECIES * l : SPECIES * (l + 1), :] = tracers[l]
+    parts = (from_left[0:BODY, :], stage[...], from_right[0:BODY, :])
+    for part, start in zip(parts, (0, REACH, REACH + COLS)):
+        hi, lo = split(part)
+        high[0, :, start : start + part.shape[1]] = hi
+        low[0, :, start : start + part.shape[1]] = lo
+    tables = jnp.concatenate([from_left[BODY:, :], table[...], from_right[BODY:, :]], axis=1)
     shifted = pltpu.roll(tables, WIDE - HALO, 1)
     rows = lax.broadcasted_iota(jnp.int32, (256, 128), 0).astype(F32)
     lanes = lax.broadcasted_iota(jnp.int32, (1, 128), 1).astype(F32)
@@ -246,12 +245,24 @@
                 high[later, :, k * 128 : (k + 1) * 128] = hi
                 low[later, :, k * 128 : (k + 1) * 128] = lo
             else:
-                for s in range(SPECIES):
-                    mixed[s, :, k * 128 : (k + 1) * 128] = new[s * ROW : s * ROW + LEV, :]
+                for l in range(LEV):
+                    mixed[l, :, k * 128 : (k + 1) * 128] = new[SPECIES * l : SPECIES * (l + 1), :]
 
 
 def shape(*dims):
     return jax.ShapeDtypeStruct(dims, F32)
+
+
+def call(kernel, name, out_shape, scratch, in_specs=None, grant=16):
+    specs = {} if in_specs is None else {"in_specs": in_specs}
+    return pl.pallas_call(
+        kernel,
+        out_shape=out_shape,
+        scratch_shapes=scratch,
+        name=name,
+        compiler_params=pltpu.CompilerParams(vmem_limit_bytes=grant << 20),
+        **specs,
+    )
 
 
 def per_device(
@@ -273,17 +284,19 @@
     up = [(i, (i + 1) % n) for i in range(n)]
     down = [(j, i) for i, j in up]
     swap = [(0, 1), (1, 0)]
-    halo_rows = SPECIES * ROW + 16
-
-    send, right, left, table = pl.pallas_call(
+    halo_rows = BODY + 16
+    tracers = jnp.transpose(absorber_amounts, (1, 0, 2))
+
+    send, right, left, table = call(
         pack_kernel,
-        out_shape=(shape(PEERS * CHUNK, 128), shape(halo_rows, REACH), shape(halo_rows, REACH), shape(16, COLS)),
-        scratch_shapes=[pltpu.VMEM((384, COLS), F32)],
-        name="pack",
+        "pack",
+        (shape(PEERS * CHUNK, 128), shape(halo_rows, REACH), shape(halo_rows, REACH), shape(16, COLS)),
+        [pltpu.VMEM((384, COLS), F32)],
+        grant=60,
     )(
         stratum_warmth_anomaly,
         pressure_depth,
-        absorber_amounts,
+        tracers,
         ground_warmth_anomaly[None],
         sun_elevation_factor[None],
         daytime_mask[None],
@@ -295,53 +308,49 @@
     from_right = lax.ppermute(left, "grp", down)
     arrived = lax.all_to_all(
         send.reshape(PEERS * CHUNK, 1, 128), "grp", split_axis=0, concat_axis=0, tiled=True
-    ).reshape(PEERS * CHUNK, 128)
-
-    mixed = pl.pallas_call(
+    )
+    mixed = call(
         mix_kernel,
-        out_shape=shape(SPECIES, LEV, COLS),
-        scratch_shapes=[
-            pltpu.VMEM((2, SPECIES * ROW, WIDE), BF),
-            pltpu.VMEM((2, SPECIES * ROW, WIDE), BF),
+        "mix",
+        shape(LEV, SPECIES, COLS),
+        [
+            pltpu.VMEM((2, BODY, WIDE), BF),
+            pltpu.VMEM((2, BODY, WIDE), BF),
             pltpu.VMEM((2, 2, 7, 256, 128), BF),
+            pltpu.VMEM((BODY, COLS), F32),
         ],
-        name="mix",
-    )(absorber_amounts, table, from_left, from_right)
-
+    )(tracers, table, from_left, from_right)
     members = arrival_membership.reshape(PEERS, SLOTS)
-    pooled = pl.pallas_call(
-        pool_kernel,
-        out_shape=shape(FEAT, RAD),
-        scratch_shapes=[pltpu.VMEM((COLS, 384), F32)],
-        name="pool",
-    )(arrived, members.T)
+    opacity = jnp.pad(opacity_table, ((0, 0), (0, 0), (0, 128 - 2 * LEV)))
+    side = lax.axis_index("sec").astype(jnp.int32)[None]
+    arrived, mixed, members, members_t, opacity, emission, sunshine, side = lax.optimization_barrier(
+        (arrived, mixed, members, members.T, opacity, emission_share[:, None], sunshine_share[:, None], side)
+    )
+
+    pooled = call(pool_kernel, "pool", shape(FEAT, RAD), [pltpu.VMEM((COLS, 384), F32)])(
+        arrived.reshape(PEERS * CHUNK, 128), members_t
+    )
     other = lax.ppermute(pooled, "sec", swap)
-    side = lax.axis_index("sec").astype(jnp.int32)[None]
-    opacity = jnp.pad(opacity_table, ((0, 0), (0, 0), (0, 128 - 2 * LEV)))
-    mine, theirs = pl.pallas_call(
+    mine, theirs = call(
         flux_kernel,
-        out_shape=(shape(ROW, RAD), shape(ROW, RAD)),
-        in_specs=[pl.BlockSpec(memory_space=pltpu.SMEM)] + [pl.BlockSpec(memory_space=pltpu.VMEM)] * 5,
-        scratch_shapes=[
+        "flux",
+        (shape(ROW, RAD), shape(ROW, RAD)),
+        [
             pltpu.VMEM((2, FEAT, RAD), F32),
             pltpu.VMEM((2, ROW, RAD), F32),
             pltpu.VMEM((2 * LEV, GH, RAD), F32),
             pltpu.VMEM((2 * LEV * 8, RAD), F32),
             pltpu.VMEM((2, ROW, RAD), F32),
         ],
-        name="flux",
-    )(side, pooled, other, opacity, emission_share[:, None], sunshine_share[:, None])
+        [pl.BlockSpec(memory_space=pltpu.SMEM)] + [pl.BlockSpec(memory_space=pltpu.VMEM)] * 5,
+    )(side, pooled, other, opacity, emission, sunshine)
     gotten = lax.ppermute(theirs, "sec", swap)
-    back = pl.pallas_call(spread_kernel, out_shape=shape(PEERS * 2, 128), name="spread")(
-        mine, gotten, pooled, members
-    )
+    back = call(spread_kernel, "spread", shape(PEERS * 2, 128), [])(mine, gotten, pooled, members)
     returned = lax.all_to_all(
         back.reshape(PEERS * 2, 1, 128), "grp", split_axis=0, concat_axis=0, tiled=True
     ).reshape(PEERS * 2, 128)
-    heating = pl.pallas_call(unplace_kernel, out_shape=shape(LEV, COLS), name="unplace")(
-        returned, dispatch_position
-    )
-    return (heating, mixed)
+    heating = call(unplace_kernel, "unplace", shape(LEV, COLS), [])(returned, dispatch_position)
+    return (heating, jnp.transpose(mixed, (1, 0, 2)))
 
 
 def solution(mesh):

time: 93.6 us -> 75.7 us (0.81)
  blocking collectives: 0 us -> 17.3 us
  local copies, waits for them, and re-layouts: 12 us -> 0.94 us
  starting transfers between devices: 34 us -> 25.3 us
  waiting for transfers between devices: 24.9 us -> 16.8 us
  Pallas kernels: 20.8 us -> 13.7 us
    all_to_all x0 -> x1, blocking collectives: none -> 17.3 us  [per_device(): lax.all_to_all(back.reshape(PEERS * 2, 1, 128), 'grp', split_axis=0, conc...]
    all_to_all x1, waiting for transfers between devices: 16.1 us -> 0.01 us  [per_device(): lax.all_to_all(send.reshape(PEERS * CHUNK, 1, 128), 'grp', split_axis=0,...]
    unnamed x29 -> x19, local copies, waits for them, and re-layouts: 9.18 us -> 0.56 us
    ppermute x1, waiting for transfers between devices: 7.41 us -> 15.2 us  [per_device(): from_left = lax.ppermute(right, 'grp', up)]
    pallas_call x6, Pallas kernels: 20.8 us -> 13.7 us  [the longest x1 4.99 us: per_device(): call(flux_kernel, 'flux', (shape(ROW, RAD), shape(ROW, RAD)), [pltpu.VMEM...]
    all_to_all x1 -> x0, starting transfers between devices: 7.07 us -> none  [per_device(): lax.all_to_all(back.reshape(PEERS * 2, 1, 128), 'grp', split_axis=0, conc...]
    ppermute x1, starting transfers between devices: 3.38 us -> 1.45 us  [per_device(): other = lax.ppermute(pooled, 'sec', swap)]
    broadcast_in_dim x2 -> x0, local copies, waits for them, and re-layouts: 1.41 us -> none  [the longest x1 0.71 us: per_device(): emission_share[:, None]]
  transfers between devices with their start and end apart: 6 -> 5, of which waited for: 3 -> 3; matrix products, arithmetic and copies ran while one was open for 6% -> 2% of each run, Pallas kernels for 6% -> 6%
where the time goes in v2:
time: 75.7 us; the launch traced here: 75.5 us
  starting transfers between devices  25.3 us (33%)
  blocking collectives  17.3 us (23%)
  waiting for transfers between devices  16.8 us (22%)
  Pallas kernels  13.7 us (18%)
  local copies, waits for them, and re-layouts  0.94 us (1%)
    all_to_all x1, blocking collectives, per_device(): lax.all_to_all(back.reshape(PEERS * 2, 1, 128), 'grp', split_axis=0, conc...  17.3 us
    all_to_all x1, starting transfers between devices, per_device(): lax.all_to_all(send.reshape(PEERS * CHUNK, 1, 128), 'grp', split_axis=0,...  16.5 us
    ppermute x1, waiting for transfers between devices, per_device(): from_left = lax.ppermute(right, 'grp', up)  15.2 us
    ppermute x1, starting transfers between devices, per_device(): from_right = lax.ppermute(left, 'grp', down)  6.32 us
    pallas_call x1, Pallas kernels, per_device(): call(flux_kernel, 'flux', (shape(ROW, RAD), shape(ROW, RAD)), [pltpu.VMEM...  4.99 us
    pallas_call x1, Pallas kernels, per_device(): call(mix_kernel, 'mix', shape(LEV, SPECIES, COLS), [pltpu.VMEM((2, BODY,...  4.17 us
    pallas_call x1, Pallas kernels, per_device(): call(pack_kernel, 'pack', (shape(PEERS * CHUNK, 128), shape(halo_rows, RE...  2.76 us
  transfers between devices with their start and end apart: 5, of which 3 were waited for; matrix products, arithmetic and copies ran while one was open for 2% of the time, Pallas kernels for 6%

profile of v2, /device:TPU:1, one launch (start us, length us, event | category | flops | bytes accessed | tf_op | source)
XLA Modules:
  0.0 75.5 jit_solution(81043171722213811)
XLA Ops:
  0.6 2.8 %pack.1 = (f32[1152,128]{1,0:T(8,128)}, f32[208,256]{1,0:T(8,128)}, f32[208,256]{1,0:T(8,128)}, f32[16,512]{1,0:T(8,128)}) custom-call(f32[45,512]{1,0:T(8,128)} %temp.1, f32[45,512]{1,0:T(8,128)} %thick.1, f32[45,4,512]{2,1,0:T(4,128)} %bitcast.18, f32[1,512]{1,0:T(1,128)} %bitcast.25, f32[1,512]{1,0:T(1,128)} %bitcast.26, s32[1,512]{1,0:T(1,128)} %bitcast.27, ...), custom_call_target="tpu_custom_call" | custom-call | tf_op jit(solution)/shard_map/pack/pallas_call | solution.py:290
  3.4 0.0 copy-start.8
  3.4 0.0 copy-start.7
  3.4 0.0 copy-start.4
  3.4 0.0 copy-start.3
  3.4 0.0 copy-start.1
  3.4 16.5 %all-to-all-start = ((f32[1152,1,128]{2,1,0:T(1,128)}), f32[1152,1,128]{2,1,0:T(1,128)S(1)}, u32[]{:S(2)}, u32[]{:S(2)}) async-start(f32[1152,1,128]{2,1,0:T(1,128)} %bitcast.23), calls=%async_computation | async-start | bytes 1179648 | tf_op jit(solution)/shard_map/all_to_all | solution.py:309
  19.9 0.0 copy-start
  19.9 0.0 copy-done.8
  19.9 0.7 collective-permute-start
  20.6 0.0 copy-done.7
  20.6 6.3 %collective-permute-start.1 = (f32[208,256]{1,0:T(8,128)S(1)}, f32[208,256]{1,0:T(8,128)S(1)}, u32[]{:S(2)}, u32[]{:S(2)}) collective-permute-start(f32[208,256]{1,0:T(8,128)S(1)} %copy-done.7), channel_id=1, source_target_pairs={{1,0},{2,1},{3,2},{4,3},{5,4},{6,5},{7,6},{8,7},{9,8},{10,9},{11,1... | collective-permute-start | bytes 638984 | tf_op jit(solution)/shard_map/ppermute | solution.py:308
  26.9 0.5 broadcast.5
  27.4 0.0 copy-done.4
  27.4 0.7 reduce.3
  28.1 0.1 reshape.20.member
  28.2 0.1 copy.22
  28.3 0.0 copy-done.3
  28.3 15.2 %collective-permute-done.from_left = f32[208,256]{1,0:T(8,128)S(1)} collective-permute-done((f32[208,256]{1,0:T(8,128)S(1)}, f32[208,256]{1,0:T(8,128)S(1)}, u32[]{:S(2)}, u32[]{:S(2)}) %collective-permute-start) | collective-permute-done | bytes 213024 | tf_op jit(solution)/shard_map/ppermute | solution.py:307
  43.5 0.0 collective-permute-done.1.from_right
  43.5 0.0 copy-done.1
  43.5 0.0 copy-done
  43.5 4.2 %mix.1 = f32[45,4,512]{2,1,0:T(4,128)} custom-call(f32[45,4,512]{2,1,0:T(4,128)S(1)} %bitcast.19, f32[16,512]{1,0:T(8,128)S(1)} %copy-done.1, f32[208,256]{1,0:T(8,128)S(1)} %collective-permute-done.from_left, f32[208,256]{1,0:T(8,128)S(1)} %collective-permute-done.1.from_right), custom_call_target="tpu_custom_call" | custom-call | tf_op jit(solution)/shard_map/mix/pallas_call | solution.py:312
  47.7 0.0 all-to-all-done
  47.7 0.0 copy-start.5
  47.7 0.4 pool.1.own
  48.1 0.0 copy-start.6
  48.1 1.5 %collective-permute-start.2 = (f32[288,128]{1,0:T(8,128)S(1)}, f32[288,128]{1,0:T(8,128)S(1)}, u32[]{:S(2)}, u32[]{:S(2)}) collective-permute-start(f32[288,128]{1,0:T(8,128)S(1)} %pool.1.own), channel_id=1, source_target_pairs={{0,128},{128,0},{1,129},{129,1},{2,130},{130,2},{3,131},{131,3},{4... | collective-permute-start | bytes 442376 | tf_op jit(solution)/shard_map/ppermute | solution.py:333
  49.6 0.0 copy-done.5
  49.6 0.1 copy.23.emission
  49.7 0.0 copy-done.6
  49.7 0.1 copy.24.sunshine
  49.8 0.8 %collective-permute-done.2.other = f32[288,128]{1,0:T(8,128)S(1)} collective-permute-done((f32[288,128]{1,0:T(8,128)S(1)}, f32[288,128]{1,0:T(8,128)S(1)}, u32[]{:S(2)}, u32[]{:S(2)}) %collective-permute-start.2) | collective-permute-done | bytes 147488 | tf_op jit(solution)/shard_map/ppermute | solution.py:333
  50.6 5.0 %flux.1 = (f32[48,128]{1,0:T(8,128)S(1)}, f32[48,128]{1,0:T(8,128)S(1)}) custom-call(s32[1]{0:T(128)} %bitcast.9.side, f32[288,128]{1,0:T(8,128)S(1)} %pool.1.own, f32[288,128]{1,0:T(8,128)S(1)} %collective-permute-done.2.other, f32[4,56,128]{2,1,0:T(8,128)S(1)} %pad.4.opacity, f32[56,1]{1,0:T(8,128)S(1)} %copy.23.emission, f32[56,1]{1,0:T(8,128)S(1)} %copy.24.sunshine), custom_call_target="tpu_custom_call" | custom-call | tf_op jit(solution)/shard_map/flux/pallas_call | solution.py:334
  55.6 0.4 collective-permute-start.3
  56.0 0.8 %collective-permute-done.3.gotten = f32[48,128]{1,0:T(8,128)S(1)} collective-permute-done((f32[48,128]{1,0:T(8,128)S(1)}, f32[48,128]{1,0:T(8,128)S(1)}, u32[]{:S(2)}, u32[]{:S(2)}) %collective-permute-start.3) | collective-permute-done | bytes 24608 | tf_op jit(solution)/shard_map/ppermute | solution.py:347
  56.9 0.3 spread.1
  57.2 0.0 copy-start.2
  57.2 17.3 %all_to_all.10 = f32[256,1,128]{2,1,0:T(1,128)S(1)} all-to-all(f32[256,1,128]{2,1,0:T(1,128)S(1)} %bitcast.20), channel_id=1, replica_groups=mesh['sec'=2,'grp'=128] {'grp'}, dimensions={0} | all-to-all | bytes 262144 | tf_op jit(solution)/shard_map/all_to_all | solution.py:349
  74.5 0.0 copy-done.2
  74.5 1.0 %unplace.1 = f32[45,512]{1,0:T(8,128)} custom-call(f32[256,128]{1,0:T(8,128)S(1)} %bitcast.21, s32[1,512]{1,0:T(1,128)S(1)} %copy-done.2), custom_call_target="tpu_custom_call" | custom-call | tf_op jit(solution)/shard_map/unplace/pallas_call | solution.py:352
  (1 shorter events, 0.0 us)
Async XLA Ops:
  3.4 16.5 %copy-start.8 = (f32[208,256]{1,0:T(8,128)S(1)}, f32[208,256]{1,0:T(8,128)}, u32[]{:S(2)}) copy-start(f32[208,256]{1,0:T(8,128)} %get-tuple-element.18) | copy-start | bytes 638980
  3.4 17.2 %copy-start.7 = (f32[208,256]{1,0:T(8,128)S(1)}, f32[208,256]{1,0:T(8,128)}, u32[]{:S(2)}) copy-start(f32[208,256]{1,0:T(8,128)} %get-tuple-element.19) | copy-start | bytes 638980
  3.4 24.0 %copy-start.4 = (s32[1,512]{1,0:T(1,128)S(1)}, s32[1,512]{1,0:T(1,128)}, u32[]{:S(2)}) copy-start(s32[1,512]{1,0:T(1,128)} %param.20) | copy-start | bytes 6148
  3.4 24.9 %copy-start.3 = (f32[4,56,90]{2,1,0:T(8,128)S(1)}, f32[4,56,90]{2,1,0:T(8,128)}, u32[]{:S(2)}) copy-start(f32[4,56,90]{2,1,0:T(8,128)} %param.23) | copy-start | bytes 241924
  3.4 40.1 %copy-start.1 = (f32[16,512]{1,0:T(8,128)S(1)}, f32[16,512]{1,0:T(8,128)}, u32[]{:S(2)}) copy-start(f32[16,512]{1,0:T(8,128)} %get-tuple-element.17.table) | copy-start | bytes 98308
  3.4 44.2 %all-to-all-start = ((f32[1152,1,128]{2,1,0:T(1,128)}), f32[1152,1,128]{2,1,0:T(1,128)S(1)}, u32[]{:S(2)}, u32[]{:S(2)}) async-start(f32[1152,1,128]{2,1,0:T(1,128)} %bitcast.23), calls=%async_computation | async-start | bytes 1179648 | tf_op jit(solution)/shard_map/all_to_all | solution.py:309
  19.9 23.6 %copy-start = (f32[4,45,512]{2,0,1:T(4,128)S(1)}, f32[4,45,512]{2,0,1:T(4,128)}, u32[]{:S(2)}) copy-start(f32[4,45,512]{2,0,1:T(4,128)} %param.15) | copy-start | bytes 1105924
  19.9 23.5 %collective-permute-start = (f32[208,256]{1,0:T(8,128)S(1)}, f32[208,256]{1,0:T(8,128)S(1)}, u32[]{:S(2)}, u32[]{:S(2)}) collective-permute-start(f32[208,256]{1,0:T(8,128)S(1)} %copy-done.8), channel_id=1, source_target_pairs={{0,1},{1,2},{2,3},{3,4},{4,5},{5,6},{6,7},{7,8},{8,9},{9,10},{10,1... | collective-permute-start | bytes 638984 | tf_op jit(solution)/shard_map/ppermute | solution.py:307
  20.6 22.9 %collective-permute-start.1 = (f32[208,256]{1,0:T(8,128)S(1)}, f32[208,256]{1,0:T(8,128)S(1)}, u32[]{:S(2)}, u32[]{:S(2)}) collective-permute-start(f32[208,256]{1,0:T(8,128)S(1)} %copy-done.7), channel_id=1, source_target_pairs={{1,0},{2,1},{3,2},{4,3},{5,4},{6,5},{7,6},{8,7},{9,8},{10,9},{11,1... | collective-permute-start | bytes 638984 | tf_op jit(solution)/shard_map/ppermute | solution.py:308
  47.7 1.9 %copy-start.5 = (f32[56]{0:T(128)S(1)}, f32[56]{0:T(128)}, u32[]{:S(2)}) copy-start(f32[56]{0:T(128)} %param.24) | copy-start | bytes 676
  48.1 1.6 %copy-start.6 = (f32[56]{0:T(128)S(1)}, f32[56]{0:T(128)}, u32[]{:S(2)}) copy-start(f32[56]{0:T(128)} %param.25) | copy-start | bytes 676
  48.1 2.5 %collective-permute-start.2 = (f32[288,128]{1,0:T(8,128)S(1)}, f32[288,128]{1,0:T(8,128)S(1)}, u32[]{:S(2)}, u32[]{:S(2)}) collective-permute-start(f32[288,128]{1,0:T(8,128)S(1)} %pool.1.own), channel_id=1, source_target_pairs={{0,128},{128,0},{1,129},{129,1},{2,130},{130,2},{3,131},{131,3},{4... | collective-permute-start | bytes 442376 | tf_op jit(solution)/shard_map/ppermute | solution.py:333
  55.6 1.3 %collective-permute-start.3 = (f32[48,128]{1,0:T(8,128)S(1)}, f32[48,128]{1,0:T(8,128)S(1)}, u32[]{:S(2)}, u32[]{:S(2)}) collective-permute-start(f32[48,128]{1,0:T(8,128)S(1)} %get-tuple-element.27), channel_id=1, source_target_pairs={{0,128},{128,0},{1,129},{129,1},{2,130},{130,2},{3,131},{131,3},{4... | collective-permute-start | bytes 73736 | tf_op jit(solution)/shard_map/ppermute | solution.py:347
  57.2 17.3 %copy-start.2 = (s32[1,512]{1,0:T(1,128)S(1)}, s32[1,512]{1,0:T(1,128)}, u32[]{:S(2)}) copy-start(s32[1,512]{1,0:T(1,128)} %pos.3) | copy-start | bytes 6148

commit v3 on v2

--- a/solution.py
+++ b/solution.py
@@ -7,6 +7,7 @@
 from jax.experimental import pallas as pl
 from jax.experimental.pallas import tpu as pltpu
 from jax.sharding import PartitionSpec as P
+
 
 STEPS = 4
 HALO = 64
@@ -253,13 +254,12 @@
     return jax.ShapeDtypeStruct(dims, F32)
 
 
-def call(kernel, name, out_shape, scratch, in_specs=None, grant=16):
+def call(kernel, out_shape, scratch, in_specs=None, grant=16):
     specs = {} if in_specs is None else {"in_specs": in_specs}
     return pl.pallas_call(
         kernel,
         out_shape=out_shape,
         scratch_shapes=scratch,
-        name=name,
         compiler_params=pltpu.CompilerParams(vmem_limit_bytes=grant << 20),
         **specs,
     )
@@ -289,7 +289,6 @@
 
     send, right, left, table = call(
         pack_kernel,
-        "pack",
         (shape(PEERS * CHUNK, 128), shape(halo_rows, REACH), shape(halo_rows, REACH), shape(16, COLS)),
         [pltpu.VMEM((384, COLS), F32)],
         grant=60,
@@ -306,12 +305,9 @@
     )
     from_left = lax.ppermute(right, "grp", up)
     from_right = lax.ppermute(left, "grp", down)
-    arrived = lax.all_to_all(
-        send.reshape(PEERS * CHUNK, 1, 128), "grp", split_axis=0, concat_axis=0, tiled=True
-    )
+    arrived = lax.all_to_all(send.reshape(PEERS * CHUNK, 1, 128), "grp", split_axis=0, concat_axis=0, tiled=True)
     mixed = call(
         mix_kernel,
-        "mix",
         shape(LEV, SPECIES, COLS),
         [
             pltpu.VMEM((2, BODY, WIDE), BF),
@@ -327,13 +323,12 @@
         (arrived, mixed, members, members.T, opacity, emission_share[:, None], sunshine_share[:, None], side)
     )
 
-    pooled = call(pool_kernel, "pool", shape(FEAT, RAD), [pltpu.VMEM((COLS, 384), F32)])(
+    pooled = call(pool_kernel, shape(FEAT, RAD), [pltpu.VMEM((COLS, 384), F32)])(
         arrived.reshape(PEERS * CHUNK, 128), members_t
     )
     other = lax.ppermute(pooled, "sec", swap)
     mine, theirs = call(
         flux_kernel,
-        "flux",
         (shape(ROW, RAD), shape(ROW, RAD)),
         [
             pltpu.VMEM((2, FEAT, RAD), F32),
@@ -345,11 +340,11 @@
         [pl.BlockSpec(memory_space=pltpu.SMEM)] + [pl.BlockSpec(memory_space=pltpu.VMEM)] * 5,
     )(side, pooled, other, opacity, emission, sunshine)
     gotten = lax.ppermute(theirs, "sec", swap)
-    back = call(spread_kernel, "spread", shape(PEERS * 2, 128), [])(mine, gotten, pooled, members)
+    back = call(spread_kernel, shape(PEERS * 2, 128), [])(mine, gotten, pooled, members)
     returned = lax.all_to_all(
         back.reshape(PEERS * 2, 1, 128), "grp", split_axis=0, concat_axis=0, tiled=True
     ).reshape(PEERS * 2, 128)
-    heating = call(unplace_kernel, "unplace", shape(LEV, COLS), [])(returned, dispatch_position)
+    heating = call(unplace_kernel, shape(LEV, COLS), [])(returned, dispatch_position)
     return (heating, jnp.transpose(mixed, (1, 0, 2)))
 
 

time: 75.7 us -> 75.7 us (level)
  no operation moved by 1% of the time
where the time goes in v3:
time: 75.7 us; the launch traced here: 75.5 us
  starting transfers between devices  25.3 us (33%)
  blocking collectives  17.3 us (23%)
  waiting for transfers between devices  16.8 us (22%)
  Pallas kernels  13.7 us (18%)
  local copies, waits for them, and re-layouts  0.94 us (1%)
    all_to_all x1, blocking collectives, per_device(): lax.all_to_all(back.reshape(PEERS * 2, 1, 128), 'grp', split_axis=0, conc...  17.3 us
    all_to_all x1, starting transfers between devices, per_device(): lax.all_to_all(send.reshape(PEERS * CHUNK, 1, 128), 'grp', split_axis=0,...  16.5 us
    ppermute x1, waiting for transfers between devices, per_device(): from_left = lax.ppermute(right, 'grp', up)  15.2 us
    ppermute x1, starting transfers between devices, per_device(): from_right = lax.ppermute(left, 'grp', down)  6.32 us
    pallas_call x1, Pallas kernels, per_device(): call(flux_kernel, (shape(ROW, RAD), shape(ROW, RAD)), [pltpu.VMEM((2, FEA...  4.99 us
    pallas_call x1, Pallas kernels, per_device(): call(mix_kernel, shape(LEV, SPECIES, COLS), [pltpu.VMEM((2, BODY, WIDE),...  4.17 us
    pallas_call x1, Pallas kernels, per_device(): call(pack_kernel, (shape(PEERS * CHUNK, 128), shape(halo_rows, REACH), sh...  2.76 us
  transfers between devices with their start and end apart: 5, of which 3 were waited for; matrix products, arithmetic and copies ran while one was open for 2% of the time, Pallas kernels for 6%

profile of v3, /device:TPU:1, one launch (start us, length us, event | category | flops | bytes accessed | tf_op | source)
XLA Modules:
  0.0 75.5 jit_solution(81043171722213811)
XLA Ops:
  0.6 2.8 %shard_map.140 = (f32[1152,128]{1,0:T(8,128)}, f32[208,256]{1,0:T(8,128)}, f32[208,256]{1,0:T(8,128)}, f32[16,512]{1,0:T(8,128)}) custom-call(f32[45,512]{1,0:T(8,128)} %temp.1, f32[45,512]{1,0:T(8,128)} %thick.1, f32[45,4,512]{2,1,0:T(4,128)} %bitcast.18, f32[1,512]{1,0:T(1,128)} %bitcast.25, f32[1,512]{1,0:T(1,128)} %bitcast.26, s32[1,512]{1,0:T(1,128)} %bitcast.27, ...), custom_call_target="tpu_custom_call" | custom-call | tf_op jit(solution)/shard_map/pallas_call | solution.py:290
  3.4 0.0 copy-start.8
  3.4 0.0 copy-start.7
  3.4 0.0 copy-start.4
  3.4 0.0 copy-start.3
  3.4 0.0 copy-start.1
  3.4 16.5 %all-to-all-start = ((f32[1152,1,128]{2,1,0:T(1,128)}), f32[1152,1,128]{2,1,0:T(1,128)S(1)}, u32[]{:S(2)}, u32[]{:S(2)}) async-start(f32[1152,1,128]{2,1,0:T(1,128)} %bitcast.23), calls=%async_computation | async-start | bytes 1179648 | tf_op jit(solution)/shard_map/all_to_all | solution.py:308
  19.9 0.0 copy-start
  19.9 0.0 copy-done.8
  19.9 0.7 collective-permute-start
  20.6 0.0 copy-done.7
  20.6 6.3 %collective-permute-start.1 = (f32[208,256]{1,0:T(8,128)S(1)}, f32[208,256]{1,0:T(8,128)S(1)}, u32[]{:S(2)}, u32[]{:S(2)}) collective-permute-start(f32[208,256]{1,0:T(8,128)S(1)} %copy-done.7), channel_id=1, source_target_pairs={{1,0},{2,1},{3,2},{4,3},{5,4},{6,5},{7,6},{8,7},{9,8},{10,9},{11,1... | collective-permute-start | bytes 638984 | tf_op jit(solution)/shard_map/ppermute | solution.py:307
  26.9 0.5 broadcast.5
  27.4 0.0 copy-done.4
  27.4 0.7 reduce.3
  28.1 0.1 reshape.20.member
  28.2 0.1 copy.22
  28.3 0.0 copy-done.3
  28.3 15.2 %collective-permute-done.from_left = f32[208,256]{1,0:T(8,128)S(1)} collective-permute-done((f32[208,256]{1,0:T(8,128)S(1)}, f32[208,256]{1,0:T(8,128)S(1)}, u32[]{:S(2)}, u32[]{:S(2)}) %collective-permute-start) | collective-permute-done | bytes 213024 | tf_op jit(solution)/shard_map/ppermute | solution.py:306
  43.5 0.0 collective-permute-done.1.from_right
  43.5 0.0 copy-done.1
  43.5 0.0 copy-done
  43.5 4.2 %shard_map.141 = f32[45,4,512]{2,1,0:T(4,128)} custom-call(f32[45,4,512]{2,1,0:T(4,128)S(1)} %bitcast.19, f32[16,512]{1,0:T(8,128)S(1)} %copy-done.1, f32[208,256]{1,0:T(8,128)S(1)} %collective-permute-done.from_left, f32[208,256]{1,0:T(8,128)S(1)} %collective-permute-done.1.from_right), custom_call_target="tpu_custom_call" | custom-call | tf_op jit(solution)/shard_map/pallas_call | solution.py:309
  47.7 0.0 all-to-all-done
  47.7 0.0 copy-start.5
  47.7 0.4 shard_map.142.own
  48.1 0.0 copy-start.6
  48.1 1.5 %collective-permute-start.2 = (f32[288,128]{1,0:T(8,128)S(1)}, f32[288,128]{1,0:T(8,128)S(1)}, u32[]{:S(2)}, u32[]{:S(2)}) collective-permute-start(f32[288,128]{1,0:T(8,128)S(1)} %shard_map.142.own), channel_id=1, source_target_pairs={{0,128},{128,0},{1,129},{129,1},{2,130},{130,2},{3,131},{131,3},{4... | collective-permute-start | bytes 442376 | tf_op jit(solution)/shard_map/ppermute | solution.py:329
  49.6 0.0 copy-done.5
  49.6 0.1 copy.23.emission
  49.7 0.0 copy-done.6
  49.7 0.1 copy.24.sunshine
  49.8 0.8 %collective-permute-done.2.other = f32[288,128]{1,0:T(8,128)S(1)} collective-permute-done((f32[288,128]{1,0:T(8,128)S(1)}, f32[288,128]{1,0:T(8,128)S(1)}, u32[]{:S(2)}, u32[]{:S(2)}) %collective-permute-start.2) | collective-permute-done | bytes 147488 | tf_op jit(solution)/shard_map/ppermute | solution.py:329
  50.6 5.0 %shard_map.143 = (f32[48,128]{1,0:T(8,128)S(1)}, f32[48,128]{1,0:T(8,128)S(1)}) custom-call(s32[1]{0:T(128)} %bitcast.9.side, f32[288,128]{1,0:T(8,128)S(1)} %shard_map.142.own, f32[288,128]{1,0:T(8,128)S(1)} %collective-permute-done.2.other, f32[4,56,128]{2,1,0:T(8,128)S(1)} %pad.4.opacity, f32[56,1]{1,0:T(8,128)S(1)} %copy.23.emission, ...), custom_call_target="tpu_custom_call" | custom-call | tf_op jit(solution)/shard_map/pallas_call | solution.py:330
  55.6 0.4 collective-permute-start.3
  56.0 0.8 %collective-permute-done.3.gotten = f32[48,128]{1,0:T(8,128)S(1)} collective-permute-done((f32[48,128]{1,0:T(8,128)S(1)}, f32[48,128]{1,0:T(8,128)S(1)}, u32[]{:S(2)}, u32[]{:S(2)}) %collective-permute-start.3) | collective-permute-done | bytes 24608 | tf_op jit(solution)/shard_map/ppermute | solution.py:342
  56.9 0.3 shard_map.144
  57.2 0.0 copy-start.2
  57.2 17.3 %all_to_all.10 = f32[256,1,128]{2,1,0:T(1,128)S(1)} all-to-all(f32[256,1,128]{2,1,0:T(1,128)S(1)} %bitcast.20), channel_id=1, replica_groups=mesh['sec'=2,'grp'=128] {'grp'}, dimensions={0} | all-to-all | bytes 262144 | tf_op jit(solution)/shard_map/all_to_all | solution.py:344
  74.5 0.0 copy-done.2
  74.5 1.0 %shard_map.145 = f32[45,512]{1,0:T(8,128)} custom-call(f32[256,128]{1,0:T(8,128)S(1)} %bitcast.21, s32[1,512]{1,0:T(1,128)S(1)} %copy-done.2), custom_call_target="tpu_custom_call" | custom-call | tf_op jit(solution)/shard_map/pallas_call | solution.py:347
  (1 shorter events, 0.0 us)
Async XLA Ops:
  3.4 16.5 %copy-start.8 = (f32[208,256]{1,0:T(8,128)S(1)}, f32[208,256]{1,0:T(8,128)}, u32[]{:S(2)}) copy-start(f32[208,256]{1,0:T(8,128)} %get-tuple-element.18) | copy-start | bytes 638980
  3.4 17.2 %copy-start.7 = (f32[208,256]{1,0:T(8,128)S(1)}, f32[208,256]{1,0:T(8,128)}, u32[]{:S(2)}) copy-start(f32[208,256]{1,0:T(8,128)} %get-tuple-element.19) | copy-start | bytes 638980
  3.4 24.0 %copy-start.4 = (s32[1,512]{1,0:T(1,128)S(1)}, s32[1,512]{1,0:T(1,128)}, u32[]{:S(2)}) copy-start(s32[1,512]{1,0:T(1,128)} %param.20) | copy-start | bytes 6148
  3.4 24.9 %copy-start.3 = (f32[4,56,90]{2,1,0:T(8,128)S(1)}, f32[4,56,90]{2,1,0:T(8,128)}, u32[]{:S(2)}) copy-start(f32[4,56,90]{2,1,0:T(8,128)} %param.23) | copy-start | bytes 241924
  3.4 40.1 %copy-start.1 = (f32[16,512]{1,0:T(8,128)S(1)}, f32[16,512]{1,0:T(8,128)}, u32[]{:S(2)}) copy-start(f32[16,512]{1,0:T(8,128)} %get-tuple-element.17.table) | copy-start | bytes 98308
  3.4 44.2 %all-to-all-start = ((f32[1152,1,128]{2,1,0:T(1,128)}), f32[1152,1,128]{2,1,0:T(1,128)S(1)}, u32[]{:S(2)}, u32[]{:S(2)}) async-start(f32[1152,1,128]{2,1,0:T(1,128)} %bitcast.23), calls=%async_computation | async-start | bytes 1179648 | tf_op jit(solution)/shard_map/all_to_all | solution.py:308
  19.9 23.6 %copy-start = (f32[4,45,512]{2,0,1:T(4,128)S(1)}, f32[4,45,512]{2,0,1:T(4,128)}, u32[]{:S(2)}) copy-start(f32[4,45,512]{2,0,1:T(4,128)} %param.15) | copy-start | bytes 1105924
  19.9 23.5 %collective-permute-start = (f32[208,256]{1,0:T(8,128)S(1)}, f32[208,256]{1,0:T(8,128)S(1)}, u32[]{:S(2)}, u32[]{:S(2)}) collective-permute-start(f32[208,256]{1,0:T(8,128)S(1)} %copy-done.8), channel_id=1, source_target_pairs={{0,1},{1,2},{2,3},{3,4},{4,5},{5,6},{6,7},{7,8},{8,9},{9,10},{10,1... | collective-permute-start | bytes 638984 | tf_op jit(solution)/shard_map/ppermute | solution.py:306
  20.6 22.9 %collective-permute-start.1 = (f32[208,256]{1,0:T(8,128)S(1)}, f32[208,256]{1,0:T(8,128)S(1)}, u32[]{:S(2)}, u32[]{:S(2)}) collective-permute-start(f32[208,256]{1,0:T(8,128)S(1)} %copy-done.7), channel_id=1, source_target_pairs={{1,0},{2,1},{3,2},{4,3},{5,4},{6,5},{7,6},{8,7},{9,8},{10,9},{11,1... | collective-permute-start | bytes 638984 | tf_op jit(solution)/shard_map/ppermute | solution.py:307
  47.7 1.9 %copy-start.5 = (f32[56]{0:T(128)S(1)}, f32[56]{0:T(128)}, u32[]{:S(2)}) copy-start(f32[56]{0:T(128)} %param.24) | copy-start | bytes 676
  48.1 1.6 %copy-start.6 = (f32[56]{0:T(128)S(1)}, f32[56]{0:T(128)}, u32[]{:S(2)}) copy-start(f32[56]{0:T(128)} %param.25) | copy-start | bytes 676
  48.1 2.5 %collective-permute-start.2 = (f32[288,128]{1,0:T(8,128)S(1)}, f32[288,128]{1,0:T(8,128)S(1)}, u32[]{:S(2)}, u32[]{:S(2)}) collective-permute-start(f32[288,128]{1,0:T(8,128)S(1)} %shard_map.142.own), channel_id=1, source_target_pairs={{0,128},{128,0},{1,129},{129,1},{2,130},{130,2},{3,131},{131,3},{4... | collective-permute-start | bytes 442376 | tf_op jit(solution)/shard_map/ppermute | solution.py:329
  55.6 1.3 %collective-permute-start.3 = (f32[48,128]{1,0:T(8,128)S(1)}, f32[48,128]{1,0:T(8,128)S(1)}, u32[]{:S(2)}, u32[]{:S(2)}) collective-permute-start(f32[48,128]{1,0:T(8,128)S(1)} %get-tuple-element.27), channel_id=1, source_target_pairs={{0,128},{128,0},{1,129},{129,1},{2,130},{130,2},{3,131},{131,3},{4... | collective-permute-start | bytes 73736 | tf_op jit(solution)/shard_map/ppermute | solution.py:342
  57.2 17.3 %copy-start.2 = (s32[1,512]{1,0:T(1,128)S(1)}, s32[1,512]{1,0:T(1,128)}, u32[]{:S(2)}) copy-start(s32[1,512]{1,0:T(1,128)} %pos.3) | copy-start | bytes 6148

commit v4 on v3

--- a/solution.py
+++ b/solution.py
@@ -1,4 +1,3 @@
-import functools
 import math
 
 import jax
@@ -31,7 +30,10 @@
 WIDE = COLS + 2 * REACH
 SPECIES = 4
 NEAR = 6
-UNROLL = 9
+BLOCK = 9
+BLOCKS = 2 * LEV // BLOCK
+TALL = 64
+PART = 40
 NT = (((1,), (1,)), ((), ()))
 NN = (((1,), (0,)), ((), ()))
 
@@ -51,14 +53,38 @@
     return jnp.where(slot == position, 1.0, 0.0).astype(BF)
 
 
-def pack_kernel(temp, thick, tracers, ground, sun, day, pos, adj, coef, send, right, left, table, bundle):
-    bundle[0:LEV, :] = temp[...]
-    bundle[ROW : ROW + LEV, :] = thick[...]
+def pack_kernel(*refs):
+    sources, outs, scratch = refs[:9], refs[9:13], refs[13:]
+    temp, thick, tracers, ground, sun, day, pos, adj, coef = scratch[:9]
+    send, right, left, table, bundle, sems, done = scratch[9:]
+    copies = [pltpu.make_async_copy(a, b, sems.at[i]) for i, (a, b) in enumerate(zip(sources, scratch))]
+    for i in (6, 7, 8, 2, 0, 1, 3, 4, 5):
+        copies[i].start()
+    stores = [pltpu.make_async_copy(a, b, done.at[i]) for i, (a, b) in enumerate(zip((send, right, left, table), outs))]
     bundle[ROW + LEV : BASE, :] = jnp.zeros((ROW - LEV, COLS), F32)
     spare = BASE + LEV * SPECIES
     bundle[spare:FEAT, :] = jnp.zeros((FEAT - spare, COLS), F32)
+    for i in (6, 7, 8):
+        copies[i].wait()
+    placing = slot_matrix(pos[...])
+    column = lax.broadcasted_iota(jnp.int32, (NEAR, COLS), 1)
+    reach = (adj[...] - column).astype(F32)
+    pad = jnp.zeros((2, COLS), F32)
+    both = jnp.concatenate([reach, pad, coef[...], pad], axis=0)
+    table[...] = both
+    right[BODY : BODY + 16, :] = both[:, COLS - REACH :]
+    left[BODY : BODY + 16, :] = both[:, :REACH]
+    copies[2].wait()
     for l in range(LEV):
         bundle[BASE + SPECIES * l : BASE + SPECIES * (l + 1), :] = tracers[l]
+    right[0:BODY, :] = bundle[BASE:FEAT, COLS - REACH :]
+    left[0:BODY, :] = bundle[BASE:FEAT, :REACH]
+    for i in (1, 2, 3):
+        stores[i].start()
+    for i in (0, 1, 3, 4, 5):
+        copies[i].wait()
+    bundle[0:LEV, :] = temp[...]
+    bundle[ROW : ROW + LEV, :] = thick[...]
     sunny = sun[...]
     bundle[LEV : LEV + 1, :] = ground[...]
     bundle[LEV + 1 : LEV + 2, :] = sunny
@@ -66,7 +92,6 @@
     tail = bundle[256:288, :]
     for k in range(1, 4):
         bundle[256 + 32 * k : 288 + 32 * k, :] = tail
-    placing = slot_matrix(pos[...])
     hi, lo = split(bundle[...])
     packed = dot(placing, hi, NT) + dot(placing, lo, NT)
     lane = lax.broadcasted_iota(jnp.int32, (PEERS, 128), 1) >> 5
@@ -77,15 +102,9 @@
         send[pl.ds(2 * m + 1, PEERS, CHUNK), :] = block[:, 128:256]
         last = jnp.where(lane == m, block[:, 256:384], last)
     send[pl.ds(CHUNK - 1, PEERS, CHUNK), :] = last
-    right[0:BODY, :] = bundle[BASE:FEAT, COLS - REACH :]
-    left[0:BODY, :] = bundle[BASE:FEAT, :REACH]
-    column = lax.broadcasted_iota(jnp.int32, (NEAR, COLS), 1)
-    reach = (adj[...] - column).astype(F32)
-    pad = jnp.zeros((2, COLS), F32)
-    both = jnp.concatenate([reach, pad, coef[...], pad], axis=0)
-    table[...] = both
-    right[BODY : BODY + 16, :] = both[:, COLS - REACH :]
-    left[BODY : BODY + 16, :] = both[:, :REACH]
+    stores[0].start()
+    for store in stores:
+        store.wait()
 
 
 def pool_kernel(arrived, member, pooled, stage):
@@ -109,7 +128,36 @@
     pooled[256:288, :] = tail[0:32] + tail[32:64] + tail[64:96] + tail[96:128]
 
 
-def flux_kernel(side, own, other, opacity, emission, sunshine, mine, theirs, fields, warm, kept, sums, net):
+def weight_kernel(opacity, weights):
+    rows = lax.broadcasted_iota(jnp.int32, (128, 128), 0)
+    lanes = lax.broadcasted_iota(jnp.int32, (128, 128), 1)
+    picks = []
+    for s in range(SPECIES):
+        lane = jnp.where(rows < BLOCK, SPECIES * rows + s, -1)
+        picks.append((lanes == lane) | (lanes == jnp.where(lane < 0, -1, lane + 2 * PART)))
+    for s in range(SPECIES):
+        lane = jnp.where(rows < BLOCK, SPECIES * rows + s + PART, -1)
+        picks.append(lanes == lane)
+    picker = jnp.concatenate([jnp.where(p, 1.0, 0.0).astype(BF) for p in picks], axis=0)
+    group = lax.broadcasted_iota(jnp.int32, (TALL, 128), 1)
+    group = jnp.where(group >= 2 * PART, group - 2 * PART, jnp.where(group >= PART, group - PART, group)) >> 2
+    pad = jnp.zeros((TALL - GH, 128), F32)
+    for b in range(BLOCKS):
+        his, los = [], []
+        for s in range(SPECIES):
+            level = opacity[s]
+            if b:
+                level = pltpu.roll(level, 128 - b * BLOCK, 1)
+            hi, lo = split(jnp.concatenate([level, pad], axis=0))
+            his.append(hi)
+            los.append(lo)
+        wide = dot(jnp.concatenate(his + los, axis=1), picker, NN)
+        for i in range(BLOCK):
+            start = (b * BLOCK + i) * TALL
+            weights[start : start + TALL, :] = jnp.where(group == i, wide, 0.0).astype(BF)
+
+
+def flux_kernel(side, own, other, weights, emission, sunshine, mine, theirs, fields, warm, taus, sums, net):
     me = side[0]
     fields[pl.ds(me, 1)] = own[...][None]
     fields[pl.ds(1 - me, 1)] = other[...][None]
@@ -122,49 +170,42 @@
     slant = jnp.broadcast_to(slant, (GH, RAD))
     insolation = surface[7:8, :]
     emit = jnp.broadcast_to(emission[...], (GH, RAD))
+    pad = jnp.zeros((128 - 3 * PART, RAD), F32)
+    tall = BLOCK * TALL
+    for b in range(BLOCKS):
+        h, inner = divmod(b * BLOCK, LEV)
+        start = BASE + SPECIES * inner
+        part = fields[h, start : start + PART, :]
+        hi = part.astype(BF).astype(F32)
+        amounts = jnp.concatenate([hi, hi, part - hi, pad], axis=0).astype(BF)
+        taus[b * tall : (b + 1) * tall, :] = dot(weights[b * tall : (b + 1) * tall, :], amounts, NN)
 
     def fold(x):
         return jnp.sum(x.reshape(GH // 8, 8, RAD), axis=0)
 
-    def down(h, block, carry):
-        thermal, direct = carry
-        start = h * LEV + block * UNROLL
-        shift = lax.rem(128 - start, 128)
-        coeffs = [pltpu.roll(opacity[s], shift, 1) for s in range(SPECIES)]
-        for i in range(UNROLL):
-            inner = block * UNROLL + i
-            tau = None
-            for s in range(SPECIES):
-                amount = fields[h, pl.ds(BASE + SPECIES * inner + s, 1), :]
-                term = jnp.broadcast_to(coeffs[s][:, i : i + 1], (GH, RAD)) * amount
-                tau = term if tau is None else tau + term
-            opaque = 1.0 - jnp.exp2(tau)
-            kept[start + i] = opaque
-            source = emit * warm[h, pl.ds(inner, 1), :]
-            gain = opaque * (thermal - source)
-            thermal = thermal - gain
-            passed = direct * jnp.exp2(tau * slant)
-            sums[pl.ds(8 * (start + i), 8), :] = fold(gain + (direct - passed))
-            direct = passed
-        return thermal, direct
-
-    def up(h, block, upward):
-        start = h * LEV + block * UNROLL
-        for i in range(UNROLL - 1, -1, -1):
-            source = emit * warm[h, pl.ds(block * UNROLL + i, 1), :]
-            gain = kept[start + i] * (upward - source)
-            upward = upward - gain
-            rows = pl.ds(8 * (start + i), 8)
-            sums[rows, :] = sums[rows, :] + fold(gain)
-        return upward
-
-    blocks = LEV // UNROLL
-    carry = (jnp.zeros((GH, RAD), F32), sunshine[...] * insolation)
-    for h in range(2):
-        carry = lax.fori_loop(0, blocks, functools.partial(down, h), carry)
+    thermal = jnp.zeros((GH, RAD), F32)
+    direct = sunshine[...] * insolation
+    beam = fold(direct)
+    for l in range(2 * LEV):
+        h, inner = divmod(l, LEV)
+        rows = slice(l * TALL, l * TALL + GH)
+        tau = taus[rows, :]
+        opaque = 1.0 - jnp.exp2(tau)
+        taus[rows, :] = opaque
+        source = emit * warm[h, inner : inner + 1, :]
+        gain = opaque * (thermal - source)
+        thermal = thermal - gain
+        direct = direct * jnp.exp2(tau * slant)
+        below = fold(direct)
+        sums[8 * l : 8 * l + 8, :] = fold(gain) + (beam - below)
+        beam = below
     upward = emit * ground4
-    for h in (1, 0):
-        upward = lax.fori_loop(0, blocks, lambda b, u, h=h: up(h, blocks - 1 - b, u), upward)
+    for l in range(2 * LEV - 1, -1, -1):
+        h, inner = divmod(l, LEV)
+        source = emit * warm[h, inner : inner + 1, :]
+        gain = taus[l * TALL : l * TALL + GH, :] * (upward - source)
+        upward = upward - gain
+        sums[8 * l : 8 * l + 8, :] = sums[8 * l : 8 * l + 8, :] + fold(gain)
     for h in range(2):
         total = None
         for k in range(8):
@@ -254,13 +295,12 @@
     return jax.ShapeDtypeStruct(dims, F32)
 
 
-def call(kernel, out_shape, scratch, in_specs=None, grant=16):
-    specs = {} if in_specs is None else {"in_specs": in_specs}
+def call(kernel, out_shape, scratch, vmem_limit_bytes=16 << 20, **specs):
     return pl.pallas_call(
         kernel,
         out_shape=out_shape,
         scratch_shapes=scratch,
-        compiler_params=pltpu.CompilerParams(vmem_limit_bytes=grant << 20),
+        compiler_params=pltpu.CompilerParams(vmem_limit_bytes=vmem_limit_bytes),
         **specs,
     )
 
@@ -287,11 +327,20 @@
     halo_rows = BODY + 16
     tracers = jnp.transpose(absorber_amounts, (1, 0, 2))
 
+    hbm = pl.BlockSpec(memory_space=pltpu.HBM)
+    packed = (shape(PEERS * CHUNK, 128), shape(halo_rows, REACH), shape(halo_rows, REACH), shape(16, COLS))
+    given = ((LEV, COLS), (LEV, COLS), (LEV, SPECIES, COLS), (1, COLS), (1, COLS))
     send, right, left, table = call(
         pack_kernel,
-        (shape(PEERS * CHUNK, 128), shape(halo_rows, REACH), shape(halo_rows, REACH), shape(16, COLS)),
-        [pltpu.VMEM((384, COLS), F32)],
-        grant=60,
+        packed,
+        [pltpu.VMEM(dims, F32) for dims in given]
+        + [pltpu.VMEM((rows, COLS), jnp.int32) for rows in (1, 1, NEAR)]
+        + [pltpu.VMEM((NEAR, COLS), F32)]
+        + [pltpu.VMEM(out.shape, F32) for out in packed]
+        + [pltpu.VMEM((384, COLS), F32), pltpu.SemaphoreType.DMA((9,)), pltpu.SemaphoreType.DMA((4,))],
+        in_specs=[hbm] * 9,
+        out_specs=[hbm] * 4,
+        vmem_limit_bytes=60 << 20,
     )(
         stratum_warmth_anomaly,
         pressure_depth,
@@ -318,9 +367,10 @@
     )(tracers, table, from_left, from_right)
     members = arrival_membership.reshape(PEERS, SLOTS)
     opacity = jnp.pad(opacity_table, ((0, 0), (0, 0), (0, 128 - 2 * LEV)))
+    weights = call(weight_kernel, jax.ShapeDtypeStruct((2 * LEV * TALL, 128), BF), [])(opacity)
     side = lax.axis_index("sec").astype(jnp.int32)[None]
-    arrived, mixed, members, members_t, opacity, emission, sunshine, side = lax.optimization_barrier(
-        (arrived, mixed, members, members.T, opacity, emission_share[:, None], sunshine_share[:, None], side)
+    arrived, mixed, members, members_t, weights, emission, sunshine, side = lax.optimization_barrier(
+        (arrived, mixed, members, members.T, weights, emission_share[:, None], sunshine_share[:, None], side)
     )
 
     pooled = call(pool_kernel, shape(FEAT, RAD), [pltpu.VMEM((COLS, 384), F32)])(
@@ -333,12 +383,12 @@
         [
             pltpu.VMEM((2, FEAT, RAD), F32),
             pltpu.VMEM((2, ROW, RAD), F32),
-            pltpu.VMEM((2 * LEV, GH, RAD), F32),
+            pltpu.VMEM((2 * LEV * TALL, RAD), F32),
             pltpu.VMEM((2 * LEV * 8, RAD), F32),
             pltpu.VMEM((2, ROW, RAD), F32),
         ],
-        [pl.BlockSpec(memory_space=pltpu.SMEM)] + [pl.BlockSpec(memory_space=pltpu.VMEM)] * 5,
-    )(side, pooled, other, opacity, emission, sunshine)
+        in_specs=[pl.BlockSpec(memory_space=pltpu.SMEM)] + [pl.BlockSpec(memory_space=pltpu.VMEM)] * 5,
+    )(side, pooled, other, weights, emission, sunshine)
     gotten = lax.ppermute(theirs, "sec", swap)
     back = call(spread_kernel, shape(PEERS * 2, 128), [])(mine, gotten, pooled, members)
     returned = lax.all_to_all(

time: 75.7 us -> 72.7 us (0.960)
  Pallas kernels: 13.7 us -> 11.3 us
    pallas_call x1, Pallas kernels: 4.99 us -> 1.89 us  [per_device(): call(flux_kernel, (shape(ROW, RAD), shape(ROW, RAD)), [pltpu.VMEM((2, FEA...]
    pallas_call x1 -> x2, Pallas kernels: 2.76 us -> 3.45 us  [the longest x1 2.86 us: per_device(): call(pack_kernel, packed, [pltpu.VMEM(dims, F32) for dims in given] + [pl...]
  transfers between devices with their start and end apart: 5 -> 5, of which waited for: 3 -> 3; matrix products, arithmetic and copies ran while one was open for 2% -> 2% of each run, Pallas kernels for 6% -> 7%
where the time goes in v4:
time: 72.7 us; the launch traced here: 72.5 us
  starting transfers between devices  25.3 us (35%)
  blocking collectives  17.3 us (24%)
  waiting for transfers between devices  16.1 us (22%)
  Pallas kernels  11.3 us (16%)
  local copies, waits for them, and re-layouts  1.01 us (1%)
  between operations  0.74 us (1%)
    all_to_all x1, blocking collectives, per_device(): lax.all_to_all(back.reshape(PEERS * 2, 1, 128), 'grp', split_axis=0, conc...  17.3 us
    all_to_all x1, starting transfers between devices, per_device(): lax.all_to_all(send.reshape(PEERS * CHUNK, 1, 128), 'grp', split_axis=0,...  16.5 us
    ppermute x1, waiting for transfers between devices, per_device(): from_left = lax.ppermute(right, 'grp', up)  14.5 us
    ppermute x1, starting transfers between devices, per_device(): from_right = lax.ppermute(left, 'grp', down)  6.32 us
    pallas_call x1, Pallas kernels, per_device(): call(mix_kernel, shape(LEV, SPECIES, COLS), [pltpu.VMEM((2, BODY, WIDE),...  4.18 us
    pallas_call x1, Pallas kernels, per_device(): call(pack_kernel, packed, [pltpu.VMEM(dims, F32) for dims in given] + [pl...  2.86 us
    pallas_call x1, Pallas kernels, per_device(): call(flux_kernel, (shape(ROW, RAD), shape(ROW, RAD)), [pltpu.VMEM((2, FEA...  1.89 us
  transfers between devices with their start and end apart: 5, of which 3 were waited for; matrix products, arithmetic and copies ran while one was open for 2% of the time, Pallas kernels for 7%

profile of v4, /device:TPU:1, one launch (start us, length us, event | category | flops | bytes accessed | tf_op | source)
XLA Modules:
  0.0 72.5 jit_solution(17321892052389156260)
XLA Ops:
  0.6 0.0 copy-start.4
  0.6 0.0 copy-start.3
  0.7 2.9 %shard_map.140 = (f32[1152,128]{1,0:T(8,128)}, f32[208,256]{1,0:T(8,128)}, f32[208,256]{1,0:T(8,128)}, f32[16,512]{1,0:T(8,128)}) custom-call(f32[45,512]{1,0:T(8,128)} %refs_0_.1, f32[45,512]{1,0:T(8,128)} %refs_1_.1, f32[45,4,512]{2,1,0:T(4,128)} %bitcast.18, f32[1,512]{1,0:T(1,128)} %bitcast.25, f32[1,512]{1,0:T(1,128)} %bitcast.26, s32[1,512]{1,0:T(1,128)} %bitcast.27, ...), custom_call_target="tpu_custom_call" | custom-call | tf_op jit(solution)/shard_map/pallas_call | solution.py:333
  3.5 0.0 copy-start
  3.5 0.0 copy-start.1
  3.5 16.5 %all-to-all-start = ((f32[1152,1,128]{2,1,0:T(1,128)}), f32[1152,1,128]{2,1,0:T(1,128)S(1)}, u32[]{:S(2)}, u32[]{:S(2)}) async-start(f32[1152,1,128]{2,1,0:T(1,128)} %bitcast.23), calls=%async_computation | async-start | bytes 1179648 | tf_op jit(solution)/shard_map/all_to_all | solution.py:357
  20.0 0.7 collective-permute-start
  20.7 6.3 %collective-permute-start.1 = (f32[208,256]{1,0:T(8,128)}, f32[208,256]{1,0:T(8,128)S(1)}, u32[]{:S(2)}, u32[]{:S(2)}) collective-permute-start(f32[208,256]{1,0:T(8,128)} %get-tuple-element.19), channel_id=1, source_target_pairs={{1,0},{2,1},{3,2},{4,3},{5,4},{6,5},{7,6},{8,7},{9,8},{10,9},{11,1... | collective-permute-start | bytes 638984 | tf_op jit(solution)/shard_map/ppermute | solution.py:356
  27.0 0.6 broadcast.5
  27.6 0.0 copy-done.4
  27.6 0.7 reduce.3
  28.3 0.1 reshape.20.member
  28.4 0.1 copy.22
  28.5 0.0 copy-done.3
  28.5 0.0 copy-start.5
  28.5 0.0 copy-start.6
  28.5 0.6 shard_map.142.weights
  29.1 14.5 %collective-permute-done.from_left = f32[208,256]{1,0:T(8,128)S(1)} collective-permute-done((f32[208,256]{1,0:T(8,128)}, f32[208,256]{1,0:T(8,128)S(1)}, u32[]{:S(2)}, u32[]{:S(2)}) %collective-permute-start) | collective-permute-done | bytes 213024 | tf_op jit(solution)/shard_map/ppermute | solution.py:355
  43.6 0.0 collective-permute-done.1.from_right
  43.6 0.0 copy-done
  43.6 0.0 copy-done.1
  43.6 4.2 %shard_map.141 = f32[45,4,512]{2,1,0:T(4,128)} custom-call(f32[45,4,512]{2,1,0:T(4,128)S(1)} %bitcast.19, f32[16,512]{1,0:T(8,128)S(1)} %copy-done.1, f32[208,256]{1,0:T(8,128)S(1)} %collective-permute-done.from_left, f32[208,256]{1,0:T(8,128)S(1)} %collective-permute-done.1.from_right), custom_call_target="tpu_custom_call" | custom-call | tf_op jit(solution)/shard_map/pallas_call | solution.py:358
  47.8 0.0 all-to-all-done
  47.8 0.0 copy-start.2
  47.8 0.4 shard_map.143.own
  48.2 1.5 %collective-permute-start.2 = (f32[288,128]{1,0:T(8,128)S(1)}, f32[288,128]{1,0:T(8,128)S(1)}, u32[]{:S(2)}, u32[]{:S(2)}) collective-permute-start(f32[288,128]{1,0:T(8,128)S(1)} %shard_map.143.own), channel_id=1, source_target_pairs={{0,128},{128,0},{1,129},{129,1},{2,130},{130,2},{3,131},{131,3},{4... | collective-permute-start | bytes 442376 | tf_op jit(solution)/shard_map/ppermute | solution.py:379
  49.7 0.0 copy-done.5
  49.7 0.1 copy.23.emission
  49.8 0.0 copy-done.6
  49.8 0.1 copy.24.sunshine
  49.9 0.8 %collective-permute-done.2.other = f32[288,128]{1,0:T(8,128)S(1)} collective-permute-done((f32[288,128]{1,0:T(8,128)S(1)}, f32[288,128]{1,0:T(8,128)S(1)}, u32[]{:S(2)}, u32[]{:S(2)}) %collective-permute-start.2) | collective-permute-done | bytes 147488 | tf_op jit(solution)/shard_map/ppermute | solution.py:379
  50.7 1.9 %shard_map.144 = (f32[48,128]{1,0:T(8,128)S(1)}, f32[48,128]{1,0:T(8,128)S(1)}) custom-call(s32[1]{0:T(128)} %bitcast.9.side, f32[288,128]{1,0:T(8,128)S(1)} %shard_map.143.own, f32[288,128]{1,0:T(8,128)S(1)} %collective-permute-done.2.other, bf16[5760,128]{1,0:T(8,128)(2,1)S(1)} %shard_map.142.weights, f32[56,1]{1,0:T(8,128)S(1)} %copy.23.emission, ...), custom_call_target="tpu_custom_call" | custom-call | tf_op jit(solution)/shard_map/pallas_call | solution.py:380
  52.6 0.4 collective-permute-start.3
  53.0 0.8 %collective-permute-done.3.gotten = f32[48,128]{1,0:T(8,128)S(1)} collective-permute-done((f32[48,128]{1,0:T(8,128)S(1)}, f32[48,128]{1,0:T(8,128)S(1)}, u32[]{:S(2)}, u32[]{:S(2)}) %collective-permute-start.3) | collective-permute-done | bytes 24608 | tf_op jit(solution)/shard_map/ppermute | solution.py:392
  53.9 0.3 shard_map.145
  54.2 17.3 %all_to_all.10 = f32[256,1,128]{2,1,0:T(1,128)S(1)} all-to-all(f32[256,1,128]{2,1,0:T(1,128)S(1)} %bitcast.20), channel_id=1, replica_groups=mesh['sec'=2,'grp'=128] {'grp'}, dimensions={0} | all-to-all | bytes 262144 | tf_op jit(solution)/shard_map/all_to_all | solution.py:394
  71.5 0.0 copy-done.2
  71.5 1.0 %shard_map.146 = f32[45,512]{1,0:T(8,128)} custom-call(f32[256,128]{1,0:T(8,128)S(1)} %bitcast.21, s32[1,512]{1,0:T(1,128)S(1)} %copy-done.2), custom_call_target="tpu_custom_call" | custom-call | tf_op jit(solution)/shard_map/pallas_call | solution.py:397
  (1 shorter events, 0.0 us)
Async XLA Ops:
  0.6 27.0 %copy-start.4 = (s32[1,512]{1,0:T(1,128)S(1)}, s32[1,512]{1,0:T(1,128)}, u32[]{:S(2)}) copy-start(s32[1,512]{1,0:T(1,128)} %param.20) | copy-start | bytes 6148
  0.6 27.8 %copy-start.3 = (f32[4,56,90]{2,1,0:T(8,128)S(1)}, f32[4,56,90]{2,1,0:T(8,128)}, u32[]{:S(2)}) copy-start(f32[4,56,90]{2,1,0:T(8,128)} %param.23) | copy-start | bytes 241924
  3.5 40.1 %copy-start = (f32[4,45,512]{2,0,1:T(4,128)S(1)}, f32[4,45,512]{2,0,1:T(4,128)}, u32[]{:S(2)}) copy-start(f32[4,45,512]{2,0,1:T(4,128)} %param.15) | copy-start | bytes 1105924
  3.5 40.1 %copy-start.1 = (f32[16,512]{1,0:T(8,128)S(1)}, f32[16,512]{1,0:T(8,128)}, u32[]{:S(2)}) copy-start(f32[16,512]{1,0:T(8,128)} %get-tuple-element.17.table) | copy-start | bytes 98308
  3.5 44.2 %all-to-all-start = ((f32[1152,1,128]{2,1,0:T(1,128)}), f32[1152,1,128]{2,1,0:T(1,128)S(1)}, u32[]{:S(2)}, u32[]{:S(2)}) async-start(f32[1152,1,128]{2,1,0:T(1,128)} %bitcast.23), calls=%async_computation | async-start | bytes 1179648 | tf_op jit(solution)/shard_map/all_to_all | solution.py:357
  20.0 23.6 %collective-permute-start = (f32[208,256]{1,0:T(8,128)}, f32[208,256]{1,0:T(8,128)S(1)}, u32[]{:S(2)}, u32[]{:S(2)}) collective-permute-start(f32[208,256]{1,0:T(8,128)} %get-tuple-element.18), channel_id=1, source_target_pairs={{0,1},{1,2},{2,3},{3,4},{4,5},{5,6},{6,7},{7,8},{8,9},{9,10},{10,1... | collective-permute-start | bytes 638984 | tf_op jit(solution)/shard_map/ppermute | solution.py:355
  20.7 22.9 %collective-permute-start.1 = (f32[208,256]{1,0:T(8,128)}, f32[208,256]{1,0:T(8,128)S(1)}, u32[]{:S(2)}, u32[]{:S(2)}) collective-permute-start(f32[208,256]{1,0:T(8,128)} %get-tuple-element.19), channel_id=1, source_target_pairs={{1,0},{2,1},{3,2},{4,3},{5,4},{6,5},{7,6},{8,7},{9,8},{10,9},{11,1... | collective-permute-start | bytes 638984 | tf_op jit(solution)/shard_map/ppermute | solution.py:356
  28.5 21.2 %copy-start.5 = (f32[56]{0:T(128)S(1)}, f32[56]{0:T(128)}, u32[]{:S(2)}) copy-start(f32[56]{0:T(128)} %param.24) | copy-start | bytes 676
  28.5 21.2 %copy-start.6 = (f32[56]{0:T(128)S(1)}, f32[56]{0:T(128)}, u32[]{:S(2)}) copy-start(f32[56]{0:T(128)} %param.25) | copy-start | bytes 676
  47.8 23.7 %copy-start.2 = (s32[1,512]{1,0:T(1,128)S(1)}, s32[1,512]{1,0:T(1,128)}, u32[]{:S(2)}) copy-start(s32[1,512]{1,0:T(1,128)} %pos.1) | copy-start | bytes 6148
  48.2 2.5 %collective-permute-start.2 = (f32[288,128]{1,0:T(8,128)S(1)}, f32[288,128]{1,0:T(8,128)S(1)}, u32[]{:S(2)}, u32[]{:S(2)}) collective-permute-start(f32[288,128]{1,0:T(8,128)S(1)} %shard_map.143.own), channel_id=1, source_target_pairs={{0,128},{128,0},{1,129},{129,1},{2,130},{130,2},{3,131},{131,3},{4... | collective-permute-start | bytes 442376 | tf_op jit(solution)/shard_map/ppermute | solution.py:379
  52.6 1.3 %collective-permute-start.3 = (f32[48,128]{1,0:T(8,128)S(1)}, f32[48,128]{1,0:T(8,128)S(1)}, u32[]{:S(2)}, u32[]{:S(2)}) collective-permute-start(f32[48,128]{1,0:T(8,128)S(1)} %get-tuple-element.27), channel_id=1, source_target_pairs={{0,128},{128,0},{1,129},{129,1},{2,130},{130,2},{3,131},{131,3},{4... | collective-permute-start | bytes 73736 | tf_op jit(solution)/shard_map/ppermute | solution.py:392

commit v5 on v4

--- a/solution.py
+++ b/solution.py
@@ -352,25 +352,15 @@
         adjacency_table,
         blending_coefficient,
     )
-    from_left = lax.ppermute(right, "grp", up)
-    from_right = lax.ppermute(left, "grp", down)
-    arrived = lax.all_to_all(send.reshape(PEERS * CHUNK, 1, 128), "grp", split_axis=0, concat_axis=0, tiled=True)
-    mixed = call(
-        mix_kernel,
-        shape(LEV, SPECIES, COLS),
-        [
-            pltpu.VMEM((2, BODY, WIDE), BF),
-            pltpu.VMEM((2, BODY, WIDE), BF),
-            pltpu.VMEM((2, 2, 7, 256, 128), BF),
-            pltpu.VMEM((BODY, COLS), F32),
-        ],
-    )(tracers, table, from_left, from_right)
+    arrived = lax.all_to_all(
+        send.reshape(PEERS * CHUNK, 1, 128), "grp", split_axis=0, concat_axis=0, tiled=True
+    )
     members = arrival_membership.reshape(PEERS, SLOTS)
     opacity = jnp.pad(opacity_table, ((0, 0), (0, 0), (0, 128 - 2 * LEV)))
     weights = call(weight_kernel, jax.ShapeDtypeStruct((2 * LEV * TALL, 128), BF), [])(opacity)
     side = lax.axis_index("sec").astype(jnp.int32)[None]
-    arrived, mixed, members, members_t, weights, emission, sunshine, side = lax.optimization_barrier(
-        (arrived, mixed, members, members.T, weights, emission_share[:, None], sunshine_share[:, None], side)
+    arrived, members, members_t, weights, emission, sunshine, side = lax.optimization_barrier(
+        (arrived, members, members.T, weights, emission_share[:, None], sunshine_share[:, None], side)
     )
 
     pooled = call(pool_kernel, shape(FEAT, RAD), [pltpu.VMEM((COLS, 384), F32)])(
@@ -389,11 +379,25 @@
         ],
         in_specs=[pl.BlockSpec(memory_space=pltpu.SMEM)] + [pl.BlockSpec(memory_space=pltpu.VMEM)] * 5,
     )(side, pooled, other, weights, emission, sunshine)
+    mine, theirs, right, left = lax.optimization_barrier((mine, theirs, right, left))
     gotten = lax.ppermute(theirs, "sec", swap)
+    from_left = lax.ppermute(right, "grp", up)
+    from_right = lax.ppermute(left, "grp", down)
     back = call(spread_kernel, shape(PEERS * 2, 128), [])(mine, gotten, pooled, members)
     returned = lax.all_to_all(
         back.reshape(PEERS * 2, 1, 128), "grp", split_axis=0, concat_axis=0, tiled=True
     ).reshape(PEERS * 2, 128)
+    mixed = call(
+        mix_kernel,
+        shape(LEV, SPECIES, COLS),
+        [
+            pltpu.VMEM((2, BODY, WIDE), BF),
+            pltpu.VMEM((2, BODY, WIDE), BF),
+            pltpu.VMEM((2, 2, 7, 256, 128), BF),
+            pltpu.VMEM((BODY, COLS), F32),
+        ],
+    )(tracers, table, from_left, from_right)
+    returned, mixed = lax.optimization_barrier((returned, mixed))
     heating = call(unplace_kernel, shape(LEV, COLS), [])(returned, dispatch_position)
     return (heating, jnp.transpose(mixed, (1, 0, 2)))
 

time: 72.7 us -> 73.9 us (1.017)
  blocking collectives: 17.3 us -> 0 us
  starting transfers between devices: 25.3 us -> 34.3 us
  waiting for transfers between devices: 16.1 us -> 25 us
    all_to_all x1 -> x0, blocking collectives: 17.3 us -> none  [per_device(): lax.all_to_all(back.reshape(PEERS * 2, 1, 128), 'grp', split_axis=0, conc...]
    all_to_all x1, waiting for transfers between devices: 0.01 us -> 16 us  [per_device(): lax.all_to_all(send.reshape(PEERS * CHUNK, 1, 128), 'grp', split_axis=0,...]
    ppermute x1, waiting for transfers between devices: 14.5 us -> 7.38 us  [per_device(): from_left = lax.ppermute(right, 'grp', up)]
    all_to_all x0 -> x1, starting transfers between devices: none -> 6.94 us  [per_device(): lax.all_to_all(back.reshape(PEERS * 2, 1, 128), 'grp', split_axis=0, conc...]
    ppermute x1, starting transfers between devices: 1.45 us -> 3.46 us  [per_device(): other = lax.ppermute(pooled, 'sec', swap)]
  transfers between devices with their start and end apart: 5 -> 6, of which waited for: 3 -> 4; matrix products, arithmetic and copies ran while one was open for 2% -> 2% of each run, Pallas kernels for 7% -> 6%
where the time goes in v5:
time: 73.9 us; the launch traced here: 73.6 us
  starting transfers between devices  34.3 us (46%)
  waiting for transfers between devices  25 us (34%)
  Pallas kernels  11.9 us (16%)
  local copies, waits for them, and re-layouts  1 us (1%)
  between operations  0.75 us (1%)
    all_to_all x1, starting transfers between devices, per_device(): lax.all_to_all(send.reshape(PEERS * CHUNK, 1, 128), 'grp', split_axis=0,...  16.3 us
    all_to_all x1, waiting for transfers between devices, per_device(): lax.all_to_all(send.reshape(PEERS * CHUNK, 1, 128), 'grp', split_axis=0,...  16 us
    ppermute x1, waiting for transfers between devices, per_device(): from_left = lax.ppermute(right, 'grp', up)  7.38 us
    all_to_all x1, starting transfers between devices, per_device(): lax.all_to_all(back.reshape(PEERS * 2, 1, 128), 'grp', split_axis=0, conc...  6.94 us
    ppermute x1, starting transfers between devices, per_device(): from_right = lax.ppermute(left, 'grp', down)  6.46 us
    pallas_call x1, Pallas kernels, per_device(): call(mix_kernel, shape(LEV, SPECIES, COLS), [pltpu.VMEM((2, BODY, WIDE),...  4.17 us
    ppermute x1, starting transfers between devices, per_device(): other = lax.ppermute(pooled, 'sec', swap)  3.46 us
    pallas_call x1, Pallas kernels, per_device(): call(pack_kernel, packed, [pltpu.VMEM(dims, F32) for dims in given] + [pl...  2.84 us
  transfers between devices with their start and end apart: 6, of which 4 were waited for; matrix products, arithmetic and copies ran while one was open for 2% of the time, Pallas kernels for 6%

profile of v5, /device:TPU:1, one launch (start us, length us, event | category | flops | bytes accessed | tf_op | source)
XLA Modules:
  0.0 73.6 jit_solution(14401140213837164982)
XLA Ops:
  0.6 0.0 copy-start.4
  0.6 0.0 copy-start.3
  0.7 2.8 %shard_map.140 = (f32[1152,128]{1,0:T(8,128)}, f32[208,256]{1,0:T(8,128)}, f32[208,256]{1,0:T(8,128)}, f32[16,512]{1,0:T(8,128)}) custom-call(f32[45,512]{1,0:T(8,128)} %refs_0_.1, f32[45,512]{1,0:T(8,128)} %refs_1_.1, f32[45,4,512]{2,1,0:T(4,128)} %bitcast.18, f32[1,512]{1,0:T(1,128)} %bitcast.24, f32[1,512]{1,0:T(1,128)} %bitcast.25, s32[1,512]{1,0:T(1,128)} %bitcast.26, ...), custom_call_target="tpu_custom_call" | custom-call | tf_op jit(solution)/shard_map/pallas_call | solution.py:333
  3.5 16.3 %all-to-all-start = ((f32[1152,1,128]{2,1,0:T(1,128)}), f32[1152,1,128]{2,1,0:T(1,128)S(1)}, u32[]{:S(2)}, u32[]{:S(2)}) async-start(f32[1152,1,128]{2,1,0:T(1,128)} %bitcast.22), calls=%async_computation | async-start | bytes 1179648 | tf_op jit(solution)/shard_map/all_to_all | solution.py:355
  19.9 0.0 copy-start.5
  19.9 0.0 copy-start.6
  19.9 0.6 broadcast.5
  20.5 0.0 copy-done.4
  20.5 0.6 reduce.3
  21.1 0.1 reshape.20.member
  21.2 0.1 copy.22
  21.3 0.0 copy-done.3
  21.3 0.6 shard_map.141.weights
  21.9 16.0 %all-to-all-done = f32[1152,1,128]{2,1,0:T(1,128)S(1)} async-done(((f32[1152,1,128]{2,1,0:T(1,128)}), f32[1152,1,128]{2,1,0:T(1,128)S(1)}, u32[]{:S(2)}, u32[]{:S(2)}) %all-to-all-start) | async-done | bytes 589856 | tf_op jit(solution)/shard_map/all_to_all | solution.py:355
  37.9 0.0 copy-start.8
  37.9 0.0 copy-start.7
  37.9 0.0 copy-start
  37.9 0.0 copy-start.1
  37.9 0.4 shard_map.142.own
  38.3 3.5 %collective-permute-start = (f32[288,128]{1,0:T(8,128)S(1)}, f32[288,128]{1,0:T(8,128)S(1)}, u32[]{:S(2)}, u32[]{:S(2)}) collective-permute-start(f32[288,128]{1,0:T(8,128)S(1)} %shard_map.142.own), channel_id=1, source_target_pairs={{0,128},{128,0},{1,129},{129,1},{2,130},{130,2},{3,131},{131,3},{4... | collective-permute-start | bytes 442376 | tf_op jit(solution)/shard_map/ppermute | solution.py:369
  41.8 0.0 copy-done.5
  41.8 0.1 copy.23.emission
  41.9 0.0 copy-done.6
  41.9 0.1 copy.24.sunshine
  42.0 0.0 copy-start.2
  42.0 0.8 %collective-permute-done.other = f32[288,128]{1,0:T(8,128)S(1)} collective-permute-done((f32[288,128]{1,0:T(8,128)S(1)}, f32[288,128]{1,0:T(8,128)S(1)}, u32[]{:S(2)}, u32[]{:S(2)}) %collective-permute-start) | collective-permute-done | bytes 147488 | tf_op jit(solution)/shard_map/ppermute | solution.py:369
  42.8 1.9 %shard_map.143 = (f32[48,128]{1,0:T(8,128)S(1)}, f32[48,128]{1,0:T(8,128)S(1)}) custom-call(s32[1]{0:T(128)} %bitcast.9.side, f32[288,128]{1,0:T(8,128)S(1)} %shard_map.142.own, f32[288,128]{1,0:T(8,128)S(1)} %collective-permute-done.other, bf16[5760,128]{1,0:T(8,128)(2,1)S(1)} %shard_map.141.weights, f32[56,1]{1,0:T(8,128)S(1)} %copy.23.emission, ...), custom_call_target="tpu_custom_call" | custom-call | tf_op jit(solution)/shard_map/pallas_call | solution.py:370
  44.7 0.5 collective-permute-start.1
  45.2 0.8 %collective-permute-done.1.gotten = f32[48,128]{1,0:T(8,128)S(1)} collective-permute-done((f32[48,128]{1,0:T(8,128)S(1)}, f32[48,128]{1,0:T(8,128)S(1)}, u32[]{:S(2)}, u32[]{:S(2)}) %collective-permute-start.1) | collective-permute-done | bytes 24608 | tf_op jit(solution)/shard_map/ppermute | solution.py:383
  46.0 1.0 %shard_map.144 = f32[256,128]{1,0:T(8,128)} custom-call(f32[48,128]{1,0:T(8,128)S(1)} %get-tuple-element.32.mine, f32[48,128]{1,0:T(8,128)S(1)} %collective-permute-done.1.gotten, f32[288,128]{1,0:T(8,128)S(1)} %shard_map.142.own, s32[128,4]{1,0:T(8,128)S(1)} %reshape.20.member), custom_call_target="tpu_custom_call" | custom-call | tf_op jit(solution)/shard_map/pallas_call | solution.py:386
  47.0 6.9 %all-to-all-start.1 = ((f32[256,1,128]{2,1,0:T(1,128)}), f32[256,1,128]{2,1,0:T(1,128)S(1)}, u32[]{:S(2)}, u32[]{:S(2)}) async-start(f32[256,1,128]{2,1,0:T(1,128)} %bitcast.12), calls=%async_computation.1 | async-start | bytes 262144 | tf_op jit(solution)/shard_map/all_to_all | solution.py:387
  53.9 0.0 copy-done.8
  54.0 0.7 collective-permute-start.2
  54.6 0.0 copy-done.7
  54.6 6.5 %collective-permute-start.3 = (f32[208,256]{1,0:T(8,128)S(1)}, f32[208,256]{1,0:T(8,128)S(1)}, u32[]{:S(2)}, u32[]{:S(2)}) collective-permute-start(f32[208,256]{1,0:T(8,128)S(1)} %copy-done.7), channel_id=1, source_target_pairs={{1,0},{2,1},{3,2},{4,3},{5,4},{6,5},{7,6},{8,7},{9,8},{10,9},{11,1... | collective-permute-start | bytes 638984 | tf_op jit(solution)/shard_map/ppermute | solution.py:385
  61.1 7.4 %collective-permute-done.2.from_left = f32[208,256]{1,0:T(8,128)S(1)} collective-permute-done((f32[208,256]{1,0:T(8,128)S(1)}, f32[208,256]{1,0:T(8,128)S(1)}, u32[]{:S(2)}, u32[]{:S(2)}) %collective-permute-start.2) | collective-permute-done | bytes 213024 | tf_op jit(solution)/shard_map/ppermute | solution.py:384
  68.4 0.0 collective-permute-done.3.from_right
  68.4 0.0 copy-done
  68.4 0.0 copy-done.1
  68.5 4.2 %shard_map.145 = f32[45,4,512]{2,1,0:T(4,128)} custom-call(f32[45,4,512]{2,1,0:T(4,128)S(1)} %bitcast.19, f32[16,512]{1,0:T(8,128)S(1)} %copy-done.1, f32[208,256]{1,0:T(8,128)S(1)} %collective-permute-done.2.from_left, f32[208,256]{1,0:T(8,128)S(1)} %collective-permute-done.3.from_right), custom_call_target="tpu_custom_call" | custom-call | tf_op jit(solution)/shard_map/pallas_call | solution.py:390
  72.6 0.0 all-to-all-done.1
  72.6 0.0 copy-done.2
  72.6 1.0 %shard_map.146 = f32[45,512]{1,0:T(8,128)} custom-call(f32[256,128]{1,0:T(8,128)S(1)} %bitcast.20, s32[1,512]{1,0:T(1,128)S(1)} %copy-done.2), custom_call_target="tpu_custom_call" | custom-call | tf_op jit(solution)/shard_map/pallas_call | solution.py:401
  (1 shorter events, 0.0 us)
Async XLA Ops:
  0.6 19.8 %copy-start.4 = (s32[1,512]{1,0:T(1,128)S(1)}, s32[1,512]{1,0:T(1,128)}, u32[]{:S(2)}) copy-start(s32[1,512]{1,0:T(1,128)} %param.20) | copy-start | bytes 6148
  0.6 20.6 %copy-start.3 = (f32[4,56,90]{2,1,0:T(8,128)S(1)}, f32[4,56,90]{2,1,0:T(8,128)}, u32[]{:S(2)}) copy-start(f32[4,56,90]{2,1,0:T(8,128)} %param.23) | copy-start | bytes 241924
  3.5 34.4 %all-to-all-start = ((f32[1152,1,128]{2,1,0:T(1,128)}), f32[1152,1,128]{2,1,0:T(1,128)S(1)}, u32[]{:S(2)}, u32[]{:S(2)}) async-start(f32[1152,1,128]{2,1,0:T(1,128)} %bitcast.22), calls=%async_computation | async-start | bytes 1179648 | tf_op jit(solution)/shard_map/all_to_all | solution.py:355
  19.9 21.9 %copy-start.5 = (f32[56]{0:T(128)S(1)}, f32[56]{0:T(128)}, u32[]{:S(2)}) copy-start(f32[56]{0:T(128)} %param.24) | copy-start | bytes 676
  19.9 22.0 %copy-start.6 = (f32[56]{0:T(128)S(1)}, f32[56]{0:T(128)}, u32[]{:S(2)}) copy-start(f32[56]{0:T(128)} %param.25) | copy-start | bytes 676
  37.9 16.1 %copy-start.8 = (f32[208,256]{1,0:T(8,128)S(1)}, f32[208,256]{1,0:T(8,128)}, u32[]{:S(2)}) copy-start(f32[208,256]{1,0:T(8,128)} %get-tuple-element.36) | copy-start | bytes 638980
  37.9 16.7 %copy-start.7 = (f32[208,256]{1,0:T(8,128)S(1)}, f32[208,256]{1,0:T(8,128)}, u32[]{:S(2)}) copy-start(f32[208,256]{1,0:T(8,128)} %get-tuple-element.37) | copy-start | bytes 638980
  37.9 30.5 %copy-start = (f32[4,45,512]{2,0,1:T(4,128)S(1)}, f32[4,45,512]{2,0,1:T(4,128)}, u32[]{:S(2)}) copy-start(f32[4,45,512]{2,0,1:T(4,128)} %param.15) | copy-start | bytes 1105924
  37.9 30.5 %copy-start.1 = (f32[16,512]{1,0:T(8,128)S(1)}, f32[16,512]{1,0:T(8,128)}, u32[]{:S(2)}) copy-start(f32[16,512]{1,0:T(8,128)} %get-tuple-element.35.table) | copy-start | bytes 98308
  38.3 4.5 %collective-permute-start = (f32[288,128]{1,0:T(8,128)S(1)}, f32[288,128]{1,0:T(8,128)S(1)}, u32[]{:S(2)}, u32[]{:S(2)}) collective-permute-start(f32[288,128]{1,0:T(8,128)S(1)} %shard_map.142.own), channel_id=1, source_target_pairs={{0,128},{128,0},{1,129},{129,1},{2,130},{130,2},{3,131},{131,3},{4... | collective-permute-start | bytes 442376 | tf_op jit(solution)/shard_map/ppermute | solution.py:369
  42.0 30.6 %copy-start.2 = (s32[1,512]{1,0:T(1,128)S(1)}, s32[1,512]{1,0:T(1,128)}, u32[]{:S(2)}) copy-start(s32[1,512]{1,0:T(1,128)} %pos.1) | copy-start | bytes 6148
  44.7 1.3 %collective-permute-start.1 = (f32[48,128]{1,0:T(8,128)S(1)}, f32[48,128]{1,0:T(8,128)S(1)}, u32[]{:S(2)}, u32[]{:S(2)}) collective-permute-start(f32[48,128]{1,0:T(8,128)S(1)} %get-tuple-element.33), channel_id=1, source_target_pairs={{0,128},{128,0},{1,129},{129,1},{2,130},{130,2},{3,131},{131,3},{4... | collective-permute-start | bytes 73736 | tf_op jit(solution)/shard_map/ppermute | solution.py:383
  47.0 25.6 %all-to-all-start.1 = ((f32[256,1,128]{2,1,0:T(1,128)}), f32[256,1,128]{2,1,0:T(1,128)S(1)}, u32[]{:S(2)}, u32[]{:S(2)}) async-start(f32[256,1,128]{2,1,0:T(1,128)} %bitcast.12), calls=%async_computation.1 | async-start | bytes 262144 | tf_op jit(solution)/shard_map/all_to_all | solution.py:387
  54.0 14.5 %collective-permute-start.2 = (f32[208,256]{1,0:T(8,128)S(1)}, f32[208,256]{1,0:T(8,128)S(1)}, u32[]{:S(2)}, u32[]{:S(2)}) collective-permute-start(f32[208,256]{1,0:T(8,128)S(1)} %copy-done.8), channel_id=1, source_target_pairs={{0,1},{1,2},{2,3},{3,4},{4,5},{5,6},{6,7},{7,8},{8,9},{9,10},{10,1... | collective-permute-start | bytes 638984 | tf_op jit(solution)/shard_map/ppermute | solution.py:384
  54.6 13.8 %collective-permute-start.3 = (f32[208,256]{1,0:T(8,128)S(1)}, f32[208,256]{1,0:T(8,128)S(1)}, u32[]{:S(2)}, u32[]{:S(2)}) collective-permute-start(f32[208,256]{1,0:T(8,128)S(1)} %copy-done.7), channel_id=1, source_target_pairs={{1,0},{2,1},{3,2},{4,3},{5,4},{6,5},{7,6},{8,7},{9,8},{10,9},{11,1... | collective-permute-start | bytes 638984 | tf_op jit(solution)/shard_map/ppermute | solution.py:385

commit v6 on v4

--- a/solution.py
+++ b/solution.py
@@ -31,8 +31,8 @@
 SPECIES = 4
 NEAR = 6
 BLOCK = 9
-BLOCKS = 2 * LEV // BLOCK
-TALL = 64
+BLOCKS = LEV // BLOCK
+GALL = 2 * GH
 PART = 40
 NT = (((1,), (1,)), ((), ()))
 NN = (((1,), (0,)), ((), ()))
@@ -89,46 +89,34 @@
     bundle[LEV : LEV + 1, :] = ground[...]
     bundle[LEV + 1 : LEV + 2, :] = sunny
     bundle[LEV + 2 : LEV + 3, :] = day[...].astype(F32) * sunny
+    hi, lo = split(bundle[0:256, :])
+    packed = dot(placing, hi, NT) + dot(placing, lo, NT)
     tail = bundle[256:288, :]
-    for k in range(1, 4):
-        bundle[256 + 32 * k : 288 + 32 * k, :] = tail
-    hi, lo = split(bundle[...])
-    packed = dot(placing, hi, NT) + dot(placing, lo, NT)
+    hi = tail.astype(BF).astype(F32)
+    tails = dot(placing, jnp.concatenate([hi] * SLOTS + [tail - hi] * SLOTS, axis=0).astype(BF), NT)
+    tails = tails[:, 0:128] + tails[:, 128:256]
     lane = lax.broadcasted_iota(jnp.int32, (PEERS, 128), 1) >> 5
     last = jnp.zeros((PEERS, 128), F32)
     for m in range(SLOTS):
         block = packed[m * PEERS : (m + 1) * PEERS, :]
         send[pl.ds(2 * m, PEERS, CHUNK), :] = block[:, 0:128]
         send[pl.ds(2 * m + 1, PEERS, CHUNK), :] = block[:, 128:256]
-        last = jnp.where(lane == m, block[:, 256:384], last)
+        last = jnp.where(lane == m, tails[m * PEERS : (m + 1) * PEERS, :], last)
     send[pl.ds(CHUNK - 1, PEERS, CHUNK), :] = last
     stores[0].start()
     for store in stores:
         store.wait()
 
 
-def pool_kernel(arrived, member, pooled, stage):
-    ids = member[...] >> 2
-    rows = lax.broadcasted_iota(jnp.int32, (RAD, 128), 0)
-    lane = lax.broadcasted_iota(jnp.int32, (PEERS, 128), 1) >> 5
-    last = arrived[pl.ds(CHUNK - 1, PEERS, CHUNK), :]
-    chosen = []
-    for m in range(SLOTS):
-        chosen.append(jnp.where(rows == ids[m : m + 1, :], 0.25, 0.0).astype(BF))
-        span = slice(m * PEERS, (m + 1) * PEERS)
-        stage[span, 0:128] = arrived[pl.ds(2 * m, PEERS, CHUNK), :]
-        stage[span, 128:256] = arrived[pl.ds(2 * m + 1, PEERS, CHUNK), :]
-        stage[span, 256:384] = jnp.where(lane == m, last, 0.0)
-    selector = jnp.concatenate(chosen, axis=1)
-    hi, lo = split(stage[...])
-    total = dot(selector, hi, NN) + dot(selector, lo, NN)
-    pooled[0:128, :] = total[:, 0:128].T
-    pooled[128:256, :] = total[:, 128:256].T
-    tail = total[:, 256:384].T
-    pooled[256:288, :] = tail[0:32] + tail[32:64] + tail[64:96] + tail[96:128]
-
-
-def weight_kernel(opacity, weights):
+def weight_kernel(side, own, other, weights, emit, shine, full):
+    me = side[0]
+    full[pl.ds(me, 1)] = own[...][None]
+    full[pl.ds(1 - me, 1)] = other[...][None]
+    shift = lax.rem(128 - LEV * me, 128)
+    tables = [jnp.concatenate([full[0, s], full[1, s]], axis=0) for s in range(SPECIES)]
+    emit[...] = jnp.broadcast_to(tables[0][:, 2 * LEV : 2 * LEV + 1], (GALL, RAD))
+    shine[...] = jnp.broadcast_to(tables[0][:, 2 * LEV + 1 : 2 * LEV + 2], (GALL, RAD))
+    tables = [pltpu.roll(table, shift, 1) for table in tables]
     rows = lax.broadcasted_iota(jnp.int32, (128, 128), 0)
     lanes = lax.broadcasted_iota(jnp.int32, (128, 128), 1)
     picks = []
@@ -139,88 +127,138 @@
         lane = jnp.where(rows < BLOCK, SPECIES * rows + s + PART, -1)
         picks.append(lanes == lane)
     picker = jnp.concatenate([jnp.where(p, 1.0, 0.0).astype(BF) for p in picks], axis=0)
-    group = lax.broadcasted_iota(jnp.int32, (TALL, 128), 1)
+    group = lax.broadcasted_iota(jnp.int32, (GALL, 128), 1)
     group = jnp.where(group >= 2 * PART, group - 2 * PART, jnp.where(group >= PART, group - PART, group)) >> 2
-    pad = jnp.zeros((TALL - GH, 128), F32)
     for b in range(BLOCKS):
         his, los = [], []
-        for s in range(SPECIES):
-            level = opacity[s]
-            if b:
-                level = pltpu.roll(level, 128 - b * BLOCK, 1)
-            hi, lo = split(jnp.concatenate([level, pad], axis=0))
+        for table in tables:
+            hi, lo = split(pltpu.roll(table, 128 - b * BLOCK, 1) if b else table)
             his.append(hi)
             los.append(lo)
         wide = dot(jnp.concatenate(his + los, axis=1), picker, NN)
         for i in range(BLOCK):
-            start = (b * BLOCK + i) * TALL
-            weights[start : start + TALL, :] = jnp.where(group == i, wide, 0.0).astype(BF)
-
-
-def flux_kernel(side, own, other, weights, emission, sunshine, mine, theirs, fields, warm, taus, sums, net):
-    me = side[0]
-    fields[pl.ds(me, 1)] = own[...][None]
-    fields[pl.ds(1 - me, 1)] = other[...][None]
-    for h in range(2):
-        warm[h] = jnp.square(jnp.square(fields[h, 0:ROW, :]))
-        fields[h, BASE:FEAT, :] = fields[h, BASE:FEAT, :] * (-DIFFUSE * LOG2E)
-    surface = own[40:48, :]
-    ground4 = jnp.square(jnp.square(surface[5:6, :]))
-    slant = 1.0 / (DIFFUSE * surface[6:7, :])
-    slant = jnp.broadcast_to(slant, (GH, RAD))
-    insolation = surface[7:8, :]
-    emit = jnp.broadcast_to(emission[...], (GH, RAD))
+            start = (b * BLOCK + i) * GALL
+            weights[start : start + GALL, :] = jnp.where(group == i, wide, 0.0).astype(BF)
+
+
+def fold(x):
+    return jnp.sum(x.reshape(GH // 8, 8, RAD), axis=0)
+
+
+def span(level, half):
+    return slice(level * GALL + half * GH, level * GALL + (half + 1) * GH)
+
+
+def first_kernel(side, arrived, member, weights, emit, shine, opaque, passing, warm, thick, sums, edge, stage, pooled):
+    ids = member[...] >> 2
+    rows = lax.broadcasted_iota(jnp.int32, (RAD, 128), 0)
+    lane = lax.broadcasted_iota(jnp.int32, (PEERS, 128), 1) >> 5
+    last = arrived[pl.ds(CHUNK - 1, PEERS, CHUNK), :]
+    chosen = []
+    for m in range(SLOTS):
+        chosen.append(jnp.where(rows == ids[m : m + 1, :], 0.25, 0.0).astype(BF))
+        part = slice(m * PEERS, (m + 1) * PEERS)
+        stage[part, 0:128] = arrived[pl.ds(2 * m, PEERS, CHUNK), :]
+        stage[part, 128:256] = arrived[pl.ds(2 * m + 1, PEERS, CHUNK), :]
+        stage[part, 256:384] = jnp.where(lane == m, last, 0.0)
+    selector = jnp.concatenate(chosen, axis=1)
+    hi, lo = split(stage[...])
+    total = dot(selector, hi, NN) + dot(selector, lo, NN)
+    pooled[0:128, :] = total[:, 0:128].T
+    pooled[128:256, :] = total[:, 128:256].T
+    tail = total[:, 256:384].T
+    pooled[256:288, :] = tail[0:32] + tail[32:64] + tail[64:96] + tail[96:128]
+    surface = pooled[40:48, :]
+    slant = jnp.broadcast_to(1.0 / (DIFFUSE * surface[6:7, :]), (GH, RAD))
+    warm[...] = jnp.square(jnp.square(pooled[0:ROW, :]))
+    thick[...] = pooled[ROW:BASE, :]
+    pooled[BASE:FEAT, :] = pooled[BASE:FEAT, :] * (-DIFFUSE * LOG2E)
     pad = jnp.zeros((128 - 3 * PART, RAD), F32)
-    tall = BLOCK * TALL
+    tall = BLOCK * GALL
     for b in range(BLOCKS):
-        h, inner = divmod(b * BLOCK, LEV)
-        start = BASE + SPECIES * inner
-        part = fields[h, start : start + PART, :]
+        start = BASE + SPECIES * BLOCK * b
+        part = pooled[start : start + PART, :]
         hi = part.astype(BF).astype(F32)
         amounts = jnp.concatenate([hi, hi, part - hi, pad], axis=0).astype(BF)
-        taus[b * tall : (b + 1) * tall, :] = dot(weights[b * tall : (b + 1) * tall, :], amounts, NN)
-
-    def fold(x):
-        return jnp.sum(x.reshape(GH // 8, 8, RAD), axis=0)
-
-    thermal = jnp.zeros((GH, RAD), F32)
-    direct = sunshine[...] * insolation
-    beam = fold(direct)
-    for l in range(2 * LEV):
-        h, inner = divmod(l, LEV)
-        rows = slice(l * TALL, l * TALL + GH)
-        tau = taus[rows, :]
-        opaque = 1.0 - jnp.exp2(tau)
-        taus[rows, :] = opaque
-        source = emit * warm[h, inner : inner + 1, :]
-        gain = opaque * (thermal - source)
-        thermal = thermal - gain
-        direct = direct * jnp.exp2(tau * slant)
-        below = fold(direct)
-        sums[8 * l : 8 * l + 8, :] = fold(gain) + (beam - below)
-        beam = below
-    upward = emit * ground4
-    for l in range(2 * LEV - 1, -1, -1):
-        h, inner = divmod(l, LEV)
-        source = emit * warm[h, inner : inner + 1, :]
-        gain = taus[l * TALL : l * TALL + GH, :] * (upward - source)
-        upward = upward - gain
-        sums[8 * l : 8 * l + 8, :] = sums[8 * l : 8 * l + 8, :] + fold(gain)
-    for h in range(2):
-        total = None
-        for k in range(8):
-            part = sums[pl.ds(8 * LEV * h + k, LEV, 8), :]
-            total = part if total is None else total + part
-        net[h, 0:LEV, :] = total
-        net[h, LEV:ROW, :] = jnp.zeros((ROW - LEV, RAD), F32)
-    mine[...] = net[pl.ds(me, 1)][0]
-    theirs[...] = net[pl.ds(1 - me, 1)][0]
-
-
-def spread_kernel(mine, gotten, own, member, send):
-    heat = (mine[...] + gotten[...]) / own[ROW:BASE, :]
-    rows = lax.broadcasted_iota(jnp.int32, (ROW, RAD), 0)
-    heat = jnp.where(rows < LEV, heat, 0.0)
+        passing[b * tall : (b + 1) * tall, :] = dot(weights[b * tall : (b + 1) * tall, :], amounts, NN)
+    me = side[0]
+
+    @pl.when(me == 0)
+    def _():
+        for half in range(2):
+            part = slice(half * GH, (half + 1) * GH)
+            thermal = jnp.zeros((GH, RAD), F32)
+            direct = shine[part, :] * surface[7:8, :]
+            beam = fold(direct)
+            for l in range(LEV):
+                tau = passing[span(l, half), :]
+                kept = 1.0 - jnp.exp2(tau)
+                opaque[span(l, half), :] = kept
+                gain = kept * (thermal - emit[part, :] * warm[l : l + 1, :])
+                thermal = thermal - gain
+                direct = direct * jnp.exp2(tau * slant)
+                below = fold(direct)
+                change = fold(gain) + (beam - below)
+                beam = below
+                row = slice(8 * l, 8 * l + 8)
+                sums[row, :] = sums[row, :] + change if half else change
+            edge[part, :] = thermal
+            edge[GALL + half * GH : GALL + (half + 1) * GH, :] = direct
+
+    @pl.when(me == 1)
+    def _():
+        ground = jnp.square(jnp.square(surface[5:6, :]))
+        for half in range(2):
+            part = slice(half * GH, (half + 1) * GH)
+            upward = emit[part, :] * ground
+            for l in range(LEV - 1, -1, -1):
+                tau = passing[span(l, half), :]
+                kept = 1.0 - jnp.exp2(tau)
+                opaque[span(l, half), :] = kept
+                passing[span(l, half), :] = jnp.exp2(tau * slant)
+                gain = kept * (upward - emit[part, :] * warm[l : l + 1, :])
+                upward = upward - gain
+                row = slice(8 * l, 8 * l + 8)
+                sums[row, :] = sums[row, :] + fold(gain) if half else fold(gain)
+            edge[part, :] = upward
+        edge[GALL:, :] = jnp.zeros((GALL, RAD), F32)
+
+
+def second_kernel(side, gotten, opaque, passing, warm, thick, sums, emit, member, send, net):
+    me = side[0]
+
+    @pl.when(me == 0)
+    def _():
+        for half in range(2):
+            part = slice(half * GH, (half + 1) * GH)
+            upward = gotten[part, :]
+            for l in range(LEV - 1, -1, -1):
+                gain = opaque[span(l, half), :] * (upward - emit[part, :] * warm[l : l + 1, :])
+                upward = upward - gain
+                row = slice(8 * l, 8 * l + 8)
+                net[row, :] = (net if half else sums)[row, :] + fold(gain)
+
+    @pl.when(me == 1)
+    def _():
+        for half in range(2):
+            part = slice(half * GH, (half + 1) * GH)
+            thermal = gotten[part, :]
+            direct = gotten[GALL + half * GH : GALL + (half + 1) * GH, :]
+            beam = fold(direct)
+            for l in range(LEV):
+                gain = opaque[span(l, half), :] * (thermal - emit[part, :] * warm[l : l + 1, :])
+                thermal = thermal - gain
+                direct = direct * passing[span(l, half), :]
+                below = fold(direct)
+                row = slice(8 * l, 8 * l + 8)
+                net[row, :] = (net if half else sums)[row, :] + fold(gain) + (beam - below)
+                beam = below
+
+    total = None
+    for k in range(8):
+        part = net[pl.ds(k, LEV, 8), :]
+        total = part if total is None else total + part
+    heat = jnp.concatenate([total / thick[0:LEV, :], jnp.zeros((ROW - LEV, RAD), F32)], axis=0)
     gap = jnp.zeros((16, RAD), F32)
     hi, lo = split(jnp.concatenate([heat, gap, heat, gap], axis=0))
     ids = member[...] >> 2
@@ -337,7 +375,7 @@
         + [pltpu.VMEM((rows, COLS), jnp.int32) for rows in (1, 1, NEAR)]
         + [pltpu.VMEM((NEAR, COLS), F32)]
         + [pltpu.VMEM(out.shape, F32) for out in packed]
-        + [pltpu.VMEM((384, COLS), F32), pltpu.SemaphoreType.DMA((9,)), pltpu.SemaphoreType.DMA((4,))],
+        + [pltpu.VMEM((FEAT, COLS), F32), pltpu.SemaphoreType.DMA((9,)), pltpu.SemaphoreType.DMA((4,))],
         in_specs=[hbm] * 9,
         out_specs=[hbm] * 4,
         vmem_limit_bytes=60 << 20,
@@ -366,31 +404,39 @@
         ],
     )(tracers, table, from_left, from_right)
     members = arrival_membership.reshape(PEERS, SLOTS)
-    opacity = jnp.pad(opacity_table, ((0, 0), (0, 0), (0, 128 - 2 * LEV)))
-    weights = call(weight_kernel, jax.ShapeDtypeStruct((2 * LEV * TALL, 128), BF), [])(opacity)
     side = lax.axis_index("sec").astype(jnp.int32)[None]
-    arrived, mixed, members, members_t, weights, emission, sunshine, side = lax.optimization_barrier(
-        (arrived, mixed, members, members.T, weights, emission_share[:, None], sunshine_share[:, None], side)
+    shares = jnp.stack([emission_share, sunshine_share], axis=-1)[None]
+    spare = 128 - 2 * LEV
+    opacity = jnp.concatenate([opacity_table, jnp.pad(shares, ((0, SPECIES - 1), (0, 0), (0, spare - 2)))], axis=2)
+    whole = pl.BlockSpec(memory_space=pltpu.VMEM)
+    scalar = pl.BlockSpec(memory_space=pltpu.SMEM)
+    rows = LEV * GALL
+    weights, emit, shine = call(
+        weight_kernel,
+        (jax.ShapeDtypeStruct((rows, 128), BF), shape(GALL, RAD), shape(GALL, RAD)),
+        [pltpu.VMEM((2, SPECIES, GH, 128), F32)],
+        in_specs=[scalar] + [whole] * 2,
+    )(side, opacity, lax.ppermute(opacity, "sec", swap))
+    arrived, mixed, members, members_t, weights, emit, shine, side = lax.optimization_barrier(
+        (arrived, mixed, members, members.T, weights, emit, shine, side)
     )
-
-    pooled = call(pool_kernel, shape(FEAT, RAD), [pltpu.VMEM((COLS, 384), F32)])(
-        arrived.reshape(PEERS * CHUNK, 128), members_t
-    )
-    other = lax.ppermute(pooled, "sec", swap)
-    mine, theirs = call(
-        flux_kernel,
-        (shape(ROW, RAD), shape(ROW, RAD)),
-        [
-            pltpu.VMEM((2, FEAT, RAD), F32),
-            pltpu.VMEM((2, ROW, RAD), F32),
-            pltpu.VMEM((2 * LEV * TALL, RAD), F32),
-            pltpu.VMEM((2 * LEV * 8, RAD), F32),
-            pltpu.VMEM((2, ROW, RAD), F32),
-        ],
-        in_specs=[pl.BlockSpec(memory_space=pltpu.SMEM)] + [pl.BlockSpec(memory_space=pltpu.VMEM)] * 5,
-    )(side, pooled, other, weights, emission, sunshine)
-    gotten = lax.ppermute(theirs, "sec", swap)
-    back = call(spread_kernel, shape(PEERS * 2, 128), [])(mine, gotten, pooled, members)
+    opaque, passing, warm, thick, sums, edge = call(
+        first_kernel,
+        (
+            shape(rows, RAD),
+            shape(rows, RAD),
+            shape(ROW, RAD),
+            shape(ROW, RAD),
+            shape(8 * LEV, RAD),
+            shape(2 * GALL, RAD),
+        ),
+        [pltpu.VMEM((COLS, 384), F32), pltpu.VMEM((FEAT, RAD), F32)],
+        in_specs=[scalar] + [whole] * 5,
+    )(side, arrived.reshape(PEERS * CHUNK, 128), members_t, weights, emit, shine)
+    gotten = lax.ppermute(edge, "sec", swap)
+    back = call(
+        second_kernel, shape(PEERS * 2, 128), [pltpu.VMEM((8 * LEV, RAD), F32)], in_specs=[scalar] + [whole] * 8
+    )(side, gotten, opaque, passing, warm, thick, sums, emit, members)
     returned = lax.all_to_all(
         back.reshape(PEERS * 2, 1, 128), "grp", split_axis=0, concat_axis=0, tiled=True
     ).reshape(PEERS * 2, 128)

time: 72.7 us -> 72.8 us (level)
  waiting for transfers between devices: 16.1 us -> 11.5 us
  other arithmetic: 0.71 us -> 3.03 us
  starting transfers between devices: 25.3 us -> 26.5 us
    ppermute x1, waiting for transfers between devices: 14.5 us -> 10.5 us  [per_device(): from_left = lax.ppermute(right, 'grp', up)]
    ppermute x2, starting transfers between devices: 1.9 us -> 3.17 us  [the longest x1 1.62 us: per_device(): gotten = lax.ppermute(edge, 'sec', swap)]
    concatenate x0 -> x1, other arithmetic: none -> 0.98 us  [per_device(): jnp.concatenate([opacity_table, jnp.pad(shares, ((0, SPECIES - 1), (0, 0)...]
    pallas_call x4 -> x3, Pallas kernels: 3.24 us -> 3.61 us  [the longest x1 1.96 us: per_device(): call(first_kernel, (shape(rows, RAD), shape(rows, RAD), shape(ROW, RAD),...]
  transfers between devices with their start and end apart: 5 -> 5, of which waited for: 3 -> 2; matrix products, arithmetic and copies ran while one was open for 2% -> 5% of each run, Pallas kernels for 7% -> 7%
where the time goes in v6:
time: 72.8 us; the launch traced here: 72.4 us
  starting transfers between devices  26.5 us (36%)
  blocking collectives  17.6 us (24%)
  Pallas kernels  11.5 us (16%)
  waiting for transfers between devices  11.5 us (16%)
  other arithmetic  3.03 us (4%)
  local copies, waits for them, and re-layouts  1.6 us (2%)
    all_to_all x1, blocking collectives, per_device(): lax.all_to_all(back.reshape(PEERS * 2, 1, 128), 'grp', split_axis=0, conc...  17.6 us
    all_to_all x1, starting transfers between devices, per_device(): lax.all_to_all(send.reshape(PEERS * CHUNK, 1, 128), 'grp', split_axis=0,...  16.3 us
    ppermute x1, waiting for transfers between devices, per_device(): from_left = lax.ppermute(right, 'grp', up)  10.5 us
    ppermute x1, starting transfers between devices, per_device(): from_right = lax.ppermute(left, 'grp', down)  6.32 us
    pallas_call x1, Pallas kernels, per_device(): call(mix_kernel, shape(LEV, SPECIES, COLS), [pltpu.VMEM((2, BODY, WIDE),...  4.17 us
    pallas_call x1, Pallas kernels, per_device(): call(pack_kernel, packed, [pltpu.VMEM(dims, F32) for dims in given] + [pl...  2.73 us
    pallas_call x1, Pallas kernels, per_device(): call(first_kernel, (shape(rows, RAD), shape(rows, RAD), shape(ROW, RAD),...  1.96 us
    ppermute x1, starting transfers between devices, per_device(): gotten = lax.ppermute(edge, 'sec', swap)  1.62 us
  transfers between devices with their start and end apart: 5, of which 2 were waited for; matrix products, arithmetic and copies ran while one was open for 5% of the time, Pallas kernels for 7%

profile of v6, /device:TPU:1, one launch (start us, length us, event | category | flops | bytes accessed | tf_op | source)
XLA Modules:
  0.0 72.4 jit_solution(5495164079099074051)
XLA Ops:
  0.6 0.0 copy-start
  0.6 2.7 %shard_map.140 = (f32[1152,128]{1,0:T(8,128)}, f32[208,256]{1,0:T(8,128)}, f32[208,256]{1,0:T(8,128)}, f32[16,512]{1,0:T(8,128)}) custom-call(f32[45,512]{1,0:T(8,128)} %refs_0_.1, f32[45,512]{1,0:T(8,128)} %refs_1_.1, f32[45,4,512]{2,1,0:T(4,128)} %bitcast.20, f32[1,512]{1,0:T(1,128)} %bitcast.27, f32[1,512]{1,0:T(1,128)} %bitcast.28, s32[1,512]{1,0:T(1,128)} %bitcast.29, ...), custom_call_target="tpu_custom_call" | custom-call | tf_op jit(solution)/shard_map/pallas_call | solution.py:371
  3.4 16.3 %all-to-all-start = ((f32[1152,1,128]{2,1,0:T(1,128)}), f32[1152,1,128]{2,1,0:T(1,128)S(1)}, u32[]{:S(2)}, u32[]{:S(2)}) async-start(f32[1152,1,128]{2,1,0:T(1,128)} %bitcast.25), calls=%async_computation | async-start | bytes 1179648 | tf_op jit(solution)/shard_map/all_to_all | solution.py:395
  19.7 0.7 collective-permute-start
  20.4 6.3 %collective-permute-start.1 = (f32[208,256]{1,0:T(8,128)}, f32[208,256]{1,0:T(8,128)S(1)}, u32[]{:S(2)}, u32[]{:S(2)}) collective-permute-start(f32[208,256]{1,0:T(8,128)} %get-tuple-element.26), channel_id=1, source_target_pairs={{1,0},{2,1},{3,2},{4,3},{5,4},{6,5},{7,6},{8,7},{9,8},{10,9},{11,1... | collective-permute-start | bytes 638984 | tf_op jit(solution)/shard_map/ppermute | solution.py:394
  26.7 0.7 maximum_bitcast_fusion
  27.4 0.1 copy.21
  27.5 1.0 %select_maximum_fusion.own = f32[4,56,128]{2,1,0:T(8,128)S(1)} fusion(f32[1,56,2]{2,1,0:T(8,128)S(1)} %copy.21, f32[4,56,90]{2,1,0:T(8,128)} %param.23), kind=kLoop, calls=%fused_computation | loop fusion | flops 86016 | bytes 195776 | tf_op jit(solution)/shard_map/concatenate | solution.py:410
  28.5 1.5 %collective-permute-start.2 = (f32[4,56,128]{2,1,0:T(8,128)S(1)}, f32[4,56,128]{2,1,0:T(8,128)S(1)}, u32[]{:S(2)}, u32[]{:S(2)}) collective-permute-start(f32[4,56,128]{2,1,0:T(8,128)S(1)} %select_maximum_fusion.own), channel_id=1, source_target_pairs={{0,128},{128,0},{1,129},{129,1},{2,130},{130,2},{3,131},{131,3},{4... | collective-permute-start | bytes 344072 | tf_op jit(solution)/shard_map/ppermute | solution.py:419
  30.0 0.6 broadcast.9
  30.6 1.4 %reduce.3 = s32[512]{0:T(512)S(1)} reduce(s32[1,512]{1,0:T(1,128)} %param.20, s32[]{:T(128)} %broadcast.9), dimensions={0}, to_apply=%param.20.reduce_sub_computation.3 | reduce | bytes 4100 | tf_op args[7]
  31.9 0.1 reshape.20.member
  32.1 0.1 copy.20
  32.1 0.0 collective-permute-done.2.other
  32.1 0.7 shard_map.142
  32.8 10.5 %collective-permute-done.from_left = f32[208,256]{1,0:T(8,128)S(1)} collective-permute-done((f32[208,256]{1,0:T(8,128)}, f32[208,256]{1,0:T(8,128)S(1)}, u32[]{:S(2)}, u32[]{:S(2)}) %collective-permute-start) | collective-permute-done | bytes 213024 | tf_op jit(solution)/shard_map/ppermute | solution.py:393
  43.3 0.0 collective-permute-done.1.from_right
  43.3 0.0 copy-done
  43.3 0.0 copy-start.1
  43.3 0.8 %copy-done.1 = f32[16,512]{1,0:T(8,128)S(1)} copy-done((f32[16,512]{1,0:T(8,128)S(1)}, f32[16,512]{1,0:T(8,128)}, u32[]{:S(2)}) %copy-start.1) | copy-done | bytes 32792
  44.1 4.2 %shard_map.141 = f32[45,4,512]{2,1,0:T(4,128)} custom-call(f32[45,4,512]{2,1,0:T(4,128)S(1)} %bitcast.21, f32[16,512]{1,0:T(8,128)S(1)} %copy-done.1, f32[208,256]{1,0:T(8,128)S(1)} %collective-permute-done.from_left, f32[208,256]{1,0:T(8,128)S(1)} %collective-permute-done.1.from_right), custom_call_target="tpu_custom_call" | custom-call | tf_op jit(solution)/shard_map/pallas_call | solution.py:396
  48.2 0.0 all-to-all-done
  48.2 2.0 %shard_map.143 = (f32[5040,128]{1,0:T(8,128)S(1)}, f32[5040,128]{1,0:T(8,128)S(1)}, f32[48,128]{1,0:T(8,128)S(1)}, f32[48,128]{1,0:T(8,128)S(1)}, f32[360,128]{1,0:T(8,128)S(1)}, /*index=5*/f32[224,128]{1,0:T(8,128)S(1)}) custom-call(s32[1]{0:T(128)} %bitcast.7.side, f32[1152,128]{1,0:T(8,128)S(1)} %bitcast.19, s32[4,128]{1,0:T(4,128)S(1)} %bitcast.24, ...), custom_call_target="tpu_custom_call" | custom-call | tf_op jit(solution)/shard_map/pallas_call | solution.py:423
  50.2 1.6 %collective-permute-start.3 = (f32[224,128]{1,0:T(8,128)S(1)}, f32[224,128]{1,0:T(8,128)S(1)}, u32[]{:S(2)}, u32[]{:S(2)}) collective-permute-start(f32[224,128]{1,0:T(8,128)S(1)} %get-tuple-element.36), channel_id=1, source_target_pairs={{0,128},{128,0},{1,129},{129,1},{2,130},{130,2},{3,131},{131,3},{4... | collective-permute-start | bytes 344072 | tf_op jit(solution)/shard_map/ppermute | solution.py:436
  51.8 1.0 %collective-permute-done.3.gotten = f32[224,128]{1,0:T(8,128)S(1)} collective-permute-done((f32[224,128]{1,0:T(8,128)S(1)}, f32[224,128]{1,0:T(8,128)S(1)}, u32[]{:S(2)}, u32[]{:S(2)}) %collective-permute-start.3) | collective-permute-done | bytes 114720 | tf_op jit(solution)/shard_map/ppermute | solution.py:436
  52.8 0.0 copy-start.2
  52.8 1.0 %shard_map.144 = f32[256,128]{1,0:T(8,128)S(1)} custom-call(s32[1]{0:T(128)} %bitcast.7.side, f32[224,128]{1,0:T(8,128)S(1)} %collective-permute-done.3.gotten, f32[5040,128]{1,0:T(8,128)S(1)} %get-tuple-element.37.opaque, f32[5040,128]{1,0:T(8,128)S(1)} %get-tuple-element.38.passing, f32[48,128]{1,0:T(8,128)S(1)} %get-tuple-element.39.warm, ...), custom_call_target="tpu_custom_call" | custom-call | tf_op jit(solution)/shard_map/pallas_call | solution.py:437
  53.8 17.6 %all_to_all.10 = f32[256,1,128]{2,1,0:T(1,128)S(1)} all-to-all(f32[256,1,128]{2,1,0:T(1,128)S(1)} %bitcast.22), channel_id=1, replica_groups=mesh['sec'=2,'grp'=128] {'grp'}, dimensions={0} | all-to-all | bytes 262144 | tf_op jit(solution)/shard_map/all_to_all | solution.py:440
  71.4 0.0 copy-done.2
  71.4 1.0 %shard_map.145 = f32[45,512]{1,0:T(8,128)} custom-call(f32[256,128]{1,0:T(8,128)S(1)} %bitcast.23, s32[1,512]{1,0:T(1,128)S(1)} %copy-done.2), custom_call_target="tpu_custom_call" | custom-call | tf_op jit(solution)/shard_map/pallas_call | solution.py:443
Async XLA Ops:
  0.6 42.7 %copy-start = (f32[4,45,512]{2,0,1:T(4,128)S(1)}, f32[4,45,512]{2,0,1:T(4,128)}, u32[]{:S(2)}) copy-start(f32[4,45,512]{2,0,1:T(4,128)} %param.15) | copy-start | bytes 1105924
  3.4 44.9 %all-to-all-start = ((f32[1152,1,128]{2,1,0:T(1,128)}), f32[1152,1,128]{2,1,0:T(1,128)S(1)}, u32[]{:S(2)}, u32[]{:S(2)}) async-start(f32[1152,1,128]{2,1,0:T(1,128)} %bitcast.25), calls=%async_computation | async-start | bytes 1179648 | tf_op jit(solution)/shard_map/all_to_all | solution.py:395
  19.7 23.6 %collective-permute-start = (f32[208,256]{1,0:T(8,128)}, f32[208,256]{1,0:T(8,128)S(1)}, u32[]{:S(2)}, u32[]{:S(2)}) collective-permute-start(f32[208,256]{1,0:T(8,128)} %get-tuple-element.25), channel_id=1, source_target_pairs={{0,1},{1,2},{2,3},{3,4},{4,5},{5,6},{6,7},{7,8},{8,9},{9,10},{10,1... | collective-permute-start | bytes 638984 | tf_op jit(solution)/shard_map/ppermute | solution.py:393
  20.4 22.9 %collective-permute-start.1 = (f32[208,256]{1,0:T(8,128)}, f32[208,256]{1,0:T(8,128)S(1)}, u32[]{:S(2)}, u32[]{:S(2)}) collective-permute-start(f32[208,256]{1,0:T(8,128)} %get-tuple-element.26), channel_id=1, source_target_pairs={{1,0},{2,1},{3,2},{4,3},{5,4},{6,5},{7,6},{8,7},{9,8},{10,9},{11,1... | collective-permute-start | bytes 638984 | tf_op jit(solution)/shard_map/ppermute | solution.py:394
  28.5 3.7 %collective-permute-start.2 = (f32[4,56,128]{2,1,0:T(8,128)S(1)}, f32[4,56,128]{2,1,0:T(8,128)S(1)}, u32[]{:S(2)}, u32[]{:S(2)}) collective-permute-start(f32[4,56,128]{2,1,0:T(8,128)S(1)} %select_maximum_fusion.own), channel_id=1, source_target_pairs={{0,128},{128,0},{1,129},{129,1},{2,130},{130,2},{3,131},{131,3},{4... | collective-permute-start | bytes 344072 | tf_op jit(solution)/shard_map/ppermute | solution.py:419
  43.3 0.8 %copy-start.1 = (f32[16,512]{1,0:T(8,128)S(1)}, f32[16,512]{1,0:T(8,128)}, u32[]{:S(2)}) copy-start(f32[16,512]{1,0:T(8,128)} %get-tuple-element.24.table) | copy-start | bytes 98308
  50.2 2.6 %collective-permute-start.3 = (f32[224,128]{1,0:T(8,128)S(1)}, f32[224,128]{1,0:T(8,128)S(1)}, u32[]{:S(2)}, u32[]{:S(2)}) collective-permute-start(f32[224,128]{1,0:T(8,128)S(1)} %get-tuple-element.36), channel_id=1, source_target_pairs={{0,128},{128,0},{1,129},{129,1},{2,130},{130,2},{3,131},{131,3},{4... | collective-permute-start | bytes 344072 | tf_op jit(solution)/shard_map/ppermute | solution.py:436
  52.8 18.6 %copy-start.2 = (s32[1,512]{1,0:T(1,128)S(1)}, s32[1,512]{1,0:T(1,128)}, u32[]{:S(2)}) copy-start(s32[1,512]{1,0:T(1,128)} %pos.1) | copy-start | bytes 6148

commit v7 on v6

--- a/solution.py
+++ b/solution.py
@@ -53,25 +53,27 @@
     return jnp.where(slot == position, 1.0, 0.0).astype(BF)
 
 
+def mixing_table(adj, coef):
+    column = lax.broadcasted_iota(jnp.int32, (NEAR, COLS), 1)
+    pad = jnp.zeros((2, COLS), F32)
+    return jnp.concatenate([(adj[...] - column).astype(F32), pad, coef[...], pad], axis=0)
+
+
 def pack_kernel(*refs):
-    sources, outs, scratch = refs[:9], refs[9:13], refs[13:]
+    sources, outs, scratch = refs[:9], refs[9:12], refs[12:]
     temp, thick, tracers, ground, sun, day, pos, adj, coef = scratch[:9]
-    send, right, left, table, bundle, sems, done = scratch[9:]
+    send, right, left, bundle, sems, done = scratch[9:]
     copies = [pltpu.make_async_copy(a, b, sems.at[i]) for i, (a, b) in enumerate(zip(sources, scratch))]
     for i in (6, 7, 8, 2, 0, 1, 3, 4, 5):
         copies[i].start()
-    stores = [pltpu.make_async_copy(a, b, done.at[i]) for i, (a, b) in enumerate(zip((send, right, left, table), outs))]
+    stores = [pltpu.make_async_copy(a, b, done.at[i]) for i, (a, b) in enumerate(zip((send, right, left), outs))]
     bundle[ROW + LEV : BASE, :] = jnp.zeros((ROW - LEV, COLS), F32)
     spare = BASE + LEV * SPECIES
     bundle[spare:FEAT, :] = jnp.zeros((FEAT - spare, COLS), F32)
     for i in (6, 7, 8):
         copies[i].wait()
     placing = slot_matrix(pos[...])
-    column = lax.broadcasted_iota(jnp.int32, (NEAR, COLS), 1)
-    reach = (adj[...] - column).astype(F32)
-    pad = jnp.zeros((2, COLS), F32)
-    both = jnp.concatenate([reach, pad, coef[...], pad], axis=0)
-    table[...] = both
+    both = mixing_table(adj, coef)
     right[BODY : BODY + 16, :] = both[:, COLS - REACH :]
     left[BODY : BODY + 16, :] = both[:, :REACH]
     copies[2].wait()
@@ -79,7 +81,7 @@
         bundle[BASE + SPECIES * l : BASE + SPECIES * (l + 1), :] = tracers[l]
     right[0:BODY, :] = bundle[BASE:FEAT, COLS - REACH :]
     left[0:BODY, :] = bundle[BASE:FEAT, :REACH]
-    for i in (1, 2, 3):
+    for i in (1, 2):
         stores[i].start()
     for i in (0, 1, 3, 4, 5):
         copies[i].wait()
@@ -108,7 +110,24 @@
         store.wait()
 
 
-def weight_kernel(side, own, other, weights, emit, shine, full):
+def join_kernel(opacity, emission, sunshine, joined):
+    rows = lax.broadcasted_iota(jnp.int32, (GH, GH), 0)
+    lanes = lax.broadcasted_iota(jnp.int32, (GH, GH), 1)
+    for s in range(SPECIES):
+        joined[s] = jnp.zeros((GH, 128), F32)
+        joined[s, :, 0 : 2 * LEV] = opacity[s]
+    for k, share in enumerate((emission, sunshine)):
+        square = jnp.where(rows == lanes, jnp.broadcast_to(share[...], (GH, GH)), 0.0)
+        joined[0, :, 2 * LEV + k : 2 * LEV + k + 1] = jnp.sum(square, axis=1, keepdims=True)
+
+
+def weight_kernel(side, own, other, member, weights, emit, shine, spread, full):
+    ids = (member[...] >> 2).astype(F32)
+    spots = lax.broadcasted_iota(jnp.int32, (128, RAD), 1).astype(F32)
+    for k in range(SLOTS):
+        part = slice(k * 128, (k + 1) * 128)
+        column = jnp.broadcast_to(ids[:, part], (128, 128)).T
+        spread[part, :] = jnp.where(column == spots, 1.0, 0.0).astype(BF)
     me = side[0]
     full[pl.ds(me, 1)] = own[...][None]
     full[pl.ds(1 - me, 1)] = other[...][None]
@@ -149,20 +168,17 @@
     return slice(level * GALL + half * GH, level * GALL + (half + 1) * GH)
 
 
-def first_kernel(side, arrived, member, weights, emit, shine, opaque, passing, warm, thick, sums, edge, stage, pooled):
-    ids = member[...] >> 2
-    rows = lax.broadcasted_iota(jnp.int32, (RAD, 128), 0)
+def first_kernel(side, arrived, member, weights, emit, shine, trans, glow, passing, thick, sums, edge, stage, pooled, warm):
     lane = lax.broadcasted_iota(jnp.int32, (PEERS, 128), 1) >> 5
     last = arrived[pl.ds(CHUNK - 1, PEERS, CHUNK), :]
-    chosen = []
     for m in range(SLOTS):
-        chosen.append(jnp.where(rows == ids[m : m + 1, :], 0.25, 0.0).astype(BF))
-        part = slice(m * PEERS, (m + 1) * PEERS)
-        stage[part, 0:128] = arrived[pl.ds(2 * m, PEERS, CHUNK), :]
-        stage[part, 128:256] = arrived[pl.ds(2 * m + 1, PEERS, CHUNK), :]
-        stage[part, 256:384] = jnp.where(lane == m, last, 0.0)
-    selector = jnp.concatenate(chosen, axis=1)
-    hi, lo = split(stage[...])
+        part = pl.ds(m, PEERS, SLOTS)
+        stage[0, part, :] = arrived[pl.ds(2 * m, PEERS, CHUNK), :]
+        stage[1, part, :] = arrived[pl.ds(2 * m + 1, PEERS, CHUNK), :]
+        stage[2, part, :] = jnp.where(lane == m, last, 0.0)
+    rows = lax.broadcasted_iota(jnp.int32, (RAD, COLS), 0)
+    selector = jnp.where(rows == member[...] >> 2, 0.25, 0.0).astype(BF)
+    hi, lo = split(jnp.concatenate([stage[k] for k in range(3)], axis=1))
     total = dot(selector, hi, NN) + dot(selector, lo, NN)
     pooled[0:128, :] = total[:, 0:128].T
     pooled[128:256, :] = total[:, 128:256].T
@@ -183,25 +199,33 @@
         passing[b * tall : (b + 1) * tall, :] = dot(weights[b * tall : (b + 1) * tall, :], amounts, NN)
     me = side[0]
 
+    def optics(l, half):
+        tau = passing[span(l, half), :]
+        kept = jnp.exp2(tau)
+        source = emit[half * GH : (half + 1) * GH, :] * warm[l : l + 1, :]
+        added = source - kept * source
+        trans[span(l, half), :] = kept
+        glow[span(l, half), :] = added
+        return kept, added, jnp.exp2(tau * slant)
+
+    def note(l, half, change):
+        row = slice(8 * l, 8 * l + 8)
+        sums[row, :] = sums[row, :] + change if half else change
+
     @pl.when(me == 0)
     def _():
         for half in range(2):
             part = slice(half * GH, (half + 1) * GH)
             thermal = jnp.zeros((GH, RAD), F32)
             direct = shine[part, :] * surface[7:8, :]
-            beam = fold(direct)
+            above = fold(direct)
             for l in range(LEV):
-                tau = passing[span(l, half), :]
-                kept = 1.0 - jnp.exp2(tau)
-                opaque[span(l, half), :] = kept
-                gain = kept * (thermal - emit[part, :] * warm[l : l + 1, :])
-                thermal = thermal - gain
-                direct = direct * jnp.exp2(tau * slant)
-                below = fold(direct)
-                change = fold(gain) + (beam - below)
-                beam = below
-                row = slice(8 * l, 8 * l + 8)
-                sums[row, :] = sums[row, :] + change if half else change
+                kept, added, passed = optics(l, half)
+                thermal = kept * thermal + added
+                direct = direct * passed
+                below = fold(thermal + direct)
+                note(l, half, above - below)
+                above = below
             edge[part, :] = thermal
             edge[GALL + half * GH : GALL + (half + 1) * GH, :] = direct
 
@@ -211,48 +235,46 @@
         for half in range(2):
             part = slice(half * GH, (half + 1) * GH)
             upward = emit[part, :] * ground
+            below = fold(upward)
             for l in range(LEV - 1, -1, -1):
-                tau = passing[span(l, half), :]
-                kept = 1.0 - jnp.exp2(tau)
-                opaque[span(l, half), :] = kept
-                passing[span(l, half), :] = jnp.exp2(tau * slant)
-                gain = kept * (upward - emit[part, :] * warm[l : l + 1, :])
-                upward = upward - gain
-                row = slice(8 * l, 8 * l + 8)
-                sums[row, :] = sums[row, :] + fold(gain) if half else fold(gain)
+                kept, added, passed = optics(l, half)
+                passing[span(l, half), :] = passed
+                upward = kept * upward + added
+                above = fold(upward)
+                note(l, half, below - above)
+                below = above
             edge[part, :] = upward
         edge[GALL:, :] = jnp.zeros((GALL, RAD), F32)
 
 
-def second_kernel(side, gotten, opaque, passing, warm, thick, sums, emit, member, send, net):
+def second_kernel(side, gotten, trans, glow, passing, thick, sums, spread, send, net, slots):
     me = side[0]
 
     @pl.when(me == 0)
     def _():
         for half in range(2):
-            part = slice(half * GH, (half + 1) * GH)
-            upward = gotten[part, :]
+            upward = gotten[half * GH : (half + 1) * GH, :]
+            below = fold(upward)
             for l in range(LEV - 1, -1, -1):
-                gain = opaque[span(l, half), :] * (upward - emit[part, :] * warm[l : l + 1, :])
-                upward = upward - gain
+                upward = trans[span(l, half), :] * upward + glow[span(l, half), :]
+                above = fold(upward)
                 row = slice(8 * l, 8 * l + 8)
-                net[row, :] = (net if half else sums)[row, :] + fold(gain)
+                net[row, :] = (net if half else sums)[row, :] + (below - above)
+                below = above
 
     @pl.when(me == 1)
     def _():
         for half in range(2):
-            part = slice(half * GH, (half + 1) * GH)
-            thermal = gotten[part, :]
+            thermal = gotten[half * GH : (half + 1) * GH, :]
             direct = gotten[GALL + half * GH : GALL + (half + 1) * GH, :]
-            beam = fold(direct)
+            above = fold(thermal + direct)
             for l in range(LEV):
-                gain = opaque[span(l, half), :] * (thermal - emit[part, :] * warm[l : l + 1, :])
-                thermal = thermal - gain
+                thermal = trans[span(l, half), :] * thermal + glow[span(l, half), :]
                 direct = direct * passing[span(l, half), :]
-                below = fold(direct)
+                below = fold(thermal + direct)
                 row = slice(8 * l, 8 * l + 8)
-                net[row, :] = (net if half else sums)[row, :] + fold(gain) + (beam - below)
-                beam = below
+                net[row, :] = (net if half else sums)[row, :] + (above - below)
+                above = below
 
     total = None
     for k in range(8):
@@ -261,14 +283,11 @@
     heat = jnp.concatenate([total / thick[0:LEV, :], jnp.zeros((ROW - LEV, RAD), F32)], axis=0)
     gap = jnp.zeros((16, RAD), F32)
     hi, lo = split(jnp.concatenate([heat, gap, heat, gap], axis=0))
-    ids = member[...] >> 2
+    slots[...] = dot(spread[...], hi, NT) + dot(spread[...], lo, NT)
     lanes = lax.broadcasted_iota(jnp.int32, (PEERS, RAD), 1)
     for h in range(2):
-        parts = []
-        for m in (2 * h, 2 * h + 1):
-            selector = jnp.where(lanes == ids[:, m : m + 1], 1.0, 0.0).astype(BF)
-            parts.append(dot(selector, hi, NT) + dot(selector, lo, NT))
-        send[pl.ds(h, PEERS, 2), :] = jnp.where(lanes < 64, parts[0], parts[1])
+        even, odd = slots[pl.ds(2 * h, PEERS, SLOTS), :], slots[pl.ds(2 * h + 1, PEERS, SLOTS), :]
+        send[pl.ds(h, PEERS, 2), :] = jnp.where(lanes < 64, even, odd)
 
 
 def unplace_kernel(returned, pos, heating):
@@ -281,7 +300,7 @@
     heating[...] = (dot(hi, placing, NN) + dot(lo, placing, NN))[0:LEV, :]
 
 
-def mix_kernel(tracers, table, from_left, from_right, mixed, high, low, band, stage):
+def mix_kernel(tracers, adj, coef, from_left, from_right, mixed, high, low, band, stage):
     spare = LEV * SPECIES
     stage[spare:BODY, :] = jnp.zeros((BODY - spare, COLS), F32)
     for l in range(LEV):
@@ -291,7 +310,7 @@
         hi, lo = split(part)
         high[0, :, start : start + part.shape[1]] = hi
         low[0, :, start : start + part.shape[1]] = lo
-    tables = jnp.concatenate([from_left[BODY:, :], table[...], from_right[BODY:, :]], axis=1)
+    tables = jnp.concatenate([from_left[BODY:, :], mixing_table(adj, coef), from_right[BODY:, :]], axis=1)
     shifted = pltpu.roll(tables, WIDE - HALO, 1)
     rows = lax.broadcasted_iota(jnp.int32, (256, 128), 0).astype(F32)
     lanes = lax.broadcasted_iota(jnp.int32, (1, 128), 1).astype(F32)
@@ -333,12 +352,16 @@
     return jax.ShapeDtypeStruct(dims, F32)
 
 
-def call(kernel, out_shape, scratch, vmem_limit_bytes=16 << 20, **specs):
+LENGTH = {"pack": 27, "join": 5, "weight": 7, "mix": 42, "first": 20, "second": 9, "unplace": 10}
+
+
+def call(kernel, name, out_shape, scratch, vmem_limit_bytes=16 << 20, **specs):
     return pl.pallas_call(
         kernel,
         out_shape=out_shape,
         scratch_shapes=scratch,
         compiler_params=pltpu.CompilerParams(vmem_limit_bytes=vmem_limit_bytes),
+        cost_estimate=pl.CostEstimate(flops=LENGTH[name] * 10**8, bytes_accessed=1 << 18, transcendentals=0),
         **specs,
     )
 
@@ -366,18 +389,19 @@
     tracers = jnp.transpose(absorber_amounts, (1, 0, 2))
 
     hbm = pl.BlockSpec(memory_space=pltpu.HBM)
-    packed = (shape(PEERS * CHUNK, 128), shape(halo_rows, REACH), shape(halo_rows, REACH), shape(16, COLS))
+    packed = (shape(PEERS * CHUNK, 128), shape(halo_rows, REACH), shape(halo_rows, REACH))
     given = ((LEV, COLS), (LEV, COLS), (LEV, SPECIES, COLS), (1, COLS), (1, COLS))
-    send, right, left, table = call(
+    send, right, left = call(
         pack_kernel,
+        "pack",
         packed,
         [pltpu.VMEM(dims, F32) for dims in given]
         + [pltpu.VMEM((rows, COLS), jnp.int32) for rows in (1, 1, NEAR)]
         + [pltpu.VMEM((NEAR, COLS), F32)]
         + [pltpu.VMEM(out.shape, F32) for out in packed]
-        + [pltpu.VMEM((FEAT, COLS), F32), pltpu.SemaphoreType.DMA((9,)), pltpu.SemaphoreType.DMA((4,))],
+        + [pltpu.VMEM((FEAT, COLS), F32), pltpu.SemaphoreType.DMA((9,)), pltpu.SemaphoreType.DMA((3,))],
         in_specs=[hbm] * 9,
-        out_specs=[hbm] * 4,
+        out_specs=[hbm] * 3,
         vmem_limit_bytes=60 << 20,
     )(
         stratum_warmth_anomaly,
@@ -395,6 +419,7 @@
     arrived = lax.all_to_all(send.reshape(PEERS * CHUNK, 1, 128), "grp", split_axis=0, concat_axis=0, tiled=True)
     mixed = call(
         mix_kernel,
+        "mix",
         shape(LEV, SPECIES, COLS),
         [
             pltpu.VMEM((2, BODY, WIDE), BF),
@@ -402,45 +427,55 @@
             pltpu.VMEM((2, 2, 7, 256, 128), BF),
             pltpu.VMEM((BODY, COLS), F32),
         ],
-    )(tracers, table, from_left, from_right)
-    members = arrival_membership.reshape(PEERS, SLOTS)
+    )(tracers, adjacency_table, blending_coefficient, from_left, from_right)
     side = lax.axis_index("sec").astype(jnp.int32)[None]
-    shares = jnp.stack([emission_share, sunshine_share], axis=-1)[None]
-    spare = 128 - 2 * LEV
-    opacity = jnp.concatenate([opacity_table, jnp.pad(shares, ((0, SPECIES - 1), (0, 0), (0, spare - 2)))], axis=2)
+    opacity = call(join_kernel, "join", shape(SPECIES, GH, 128), [])(
+        opacity_table, emission_share[None], sunshine_share[None]
+    )
     whole = pl.BlockSpec(memory_space=pltpu.VMEM)
     scalar = pl.BlockSpec(memory_space=pltpu.SMEM)
     rows = LEV * GALL
-    weights, emit, shine = call(
+    weights, emit, shine, spread = call(
         weight_kernel,
-        (jax.ShapeDtypeStruct((rows, 128), BF), shape(GALL, RAD), shape(GALL, RAD)),
+        "weight",
+        (
+            jax.ShapeDtypeStruct((rows, 128), BF),
+            shape(GALL, RAD),
+            shape(GALL, RAD),
+            jax.ShapeDtypeStruct((COLS, RAD), BF),
+        ),
         [pltpu.VMEM((2, SPECIES, GH, 128), F32)],
-        in_specs=[scalar] + [whole] * 2,
-    )(side, opacity, lax.ppermute(opacity, "sec", swap))
-    arrived, mixed, members, members_t, weights, emit, shine, side = lax.optimization_barrier(
-        (arrived, mixed, members, members.T, weights, emit, shine, side)
+        in_specs=[scalar] + [whole] * 3,
+    )(side, opacity, lax.ppermute(opacity, "sec", swap), arrival_membership)
+    arrived, mixed, weights, emit, shine, spread, side = lax.optimization_barrier(
+        (arrived, mixed, weights, emit, shine, spread, side)
     )
-    opaque, passing, warm, thick, sums, edge = call(
+    trans, glow, passing, thick, sums, edge = call(
         first_kernel,
+        "first",
         (
             shape(rows, RAD),
             shape(rows, RAD),
-            shape(ROW, RAD),
+            shape(rows, RAD),
             shape(ROW, RAD),
             shape(8 * LEV, RAD),
             shape(2 * GALL, RAD),
         ),
-        [pltpu.VMEM((COLS, 384), F32), pltpu.VMEM((FEAT, RAD), F32)],
+        [pltpu.VMEM((3, COLS, 128), F32), pltpu.VMEM((FEAT, RAD), F32), pltpu.VMEM((ROW, RAD), F32)],
         in_specs=[scalar] + [whole] * 5,
-    )(side, arrived.reshape(PEERS * CHUNK, 128), members_t, weights, emit, shine)
+    )(side, arrived.reshape(PEERS * CHUNK, 128), arrival_membership, weights, emit, shine)
     gotten = lax.ppermute(edge, "sec", swap)
     back = call(
-        second_kernel, shape(PEERS * 2, 128), [pltpu.VMEM((8 * LEV, RAD), F32)], in_specs=[scalar] + [whole] * 8
-    )(side, gotten, opaque, passing, warm, thick, sums, emit, members)
+        second_kernel,
+        "second",
+        shape(PEERS * 2, 128),
+        [pltpu.VMEM((8 * LEV, RAD), F32), pltpu.VMEM((COLS, RAD), F32)],
+        in_specs=[scalar] + [whole] * 7,
+    )(side, gotten, trans, glow, passing, thick, sums, spread)
     returned = lax.all_to_all(
         back.reshape(PEERS * 2, 1, 128), "grp", split_axis=0, concat_axis=0, tiled=True
     ).reshape(PEERS * 2, 128)
-    heating = call(unplace_kernel, shape(LEV, COLS), [])(returned, dispatch_position)
+    heating = call(unplace_kernel, "unplace", shape(LEV, COLS), [])(returned, dispatch_position)
     return (heating, jnp.transpose(mixed, (1, 0, 2)))
 
 

time: 72.8 us -> 72 us (0.989)
  waiting for transfers between devices: 11.5 us -> 15.2 us
  other arithmetic: 3.03 us -> 0 us
  local copies, waits for them, and re-layouts: 1.6 us -> 0.04 us
    ppermute x1, waiting for transfers between devices: 10.5 us -> 13.3 us  [per_device(): from_left = lax.ppermute(right, 'grp', up)]
    unnamed x1 -> x0, other arithmetic: 1.37 us -> none
    unnamed x7 -> x16, local copies, waits for them, and re-layouts: 1.34 us -> 0.04 us
    concatenate x1 -> x0, other arithmetic: 0.98 us -> none  [per_device(): jnp.concatenate([opacity_table, jnp.pad(shares, ((0, SPECIES - 1), (0, 0)...]
    ppermute x1, waiting for transfers between devices: 0.01 us -> 0.97 us  [per_device(): lax.ppermute(opacity, 'sec', swap)]
    pallas_call x6 -> x7, Pallas kernels: 11.5 us -> 11.5 us  [the longest x1 4.24 us: per_device(): call(mix_kernel, 'mix', shape(LEV, SPECIES, COLS), [pltpu.VMEM((2, BODY,...]
  transfers between devices with their start and end apart: 5 -> 5, of which waited for: 2 -> 3; matrix products, arithmetic and copies ran while one was open for 5% -> 0% of each run, Pallas kernels for 7% -> 7%
where the time goes in v7:
time: 72 us; the launch traced here: 71.8 us
  starting transfers between devices  26.7 us (37%)
  blocking collectives  17.6 us (24%)
  waiting for transfers between devices  15.2 us (21%)
  Pallas kernels  11.5 us (16%)
  between operations  0.75 us (1%)
    all_to_all x1, blocking collectives, per_device(): lax.all_to_all(back.reshape(PEERS * 2, 1, 128), 'grp', split_axis=0, conc...  17.6 us
    all_to_all x1, starting transfers between devices, per_device(): lax.all_to_all(send.reshape(PEERS * CHUNK, 1, 128), 'grp', split_axis=0,...  16.5 us
    ppermute x1, waiting for transfers between devices, per_device(): from_left = lax.ppermute(right, 'grp', up)  13.3 us
    ppermute x1, starting transfers between devices, per_device(): from_right = lax.ppermute(left, 'grp', down)  6.32 us
    pallas_call x1, Pallas kernels, per_device(): call(mix_kernel, 'mix', shape(LEV, SPECIES, COLS), [pltpu.VMEM((2, BODY,...  4.24 us
    pallas_call x1, Pallas kernels, per_device(): call(pack_kernel, 'pack', packed, [pltpu.VMEM(dims, F32) for dims in give...  2.73 us
    pallas_call x1, Pallas kernels, per_device(): call(first_kernel, 'first', (shape(rows, RAD), shape(rows, RAD), shape(ro...  2.03 us
    ppermute x1, starting transfers between devices, per_device(): gotten = lax.ppermute(edge, 'sec', swap)  1.63 us
  transfers between devices with their start and end apart: 5, of which 3 were waited for; matrix products, arithmetic and copies ran while one was open for 0% of the time, Pallas kernels for 7%

profile of v7, /device:TPU:1, one launch (start us, length us, event | category | flops | bytes accessed | tf_op | source)
XLA Modules:
  0.0 71.8 jit_solution(17586054797060149781)
XLA Ops:
  0.6 0.0 copy-start.1
  0.6 0.0 copy-start.6
  0.7 0.0 copy-start.7
  0.7 2.7 %shard_map.140 = (f32[1152,128]{1,0:T(8,128)}, f32[208,256]{1,0:T(8,128)}, f32[208,256]{1,0:T(8,128)}) custom-call(f32[45,512]{1,0:T(8,128)} %refs_0_.1, f32[45,512]{1,0:T(8,128)} %refs_1_.1, f32[45,4,512]{2,1,0:T(4,128)} %bitcast.19, f32[1,512]{1,0:T(1,128)} %bitcast.24, f32[1,512]{1,0:T(1,128)} %bitcast.25, s32[1,512]{1,0:T(1,128)} %bitcast.26, ...), custom_call_target="tpu_custom_call" | custom-call | flops 2700000000 | bytes 262144 | tf_op jit(solution)/shard_map/pallas_call | solution.py:394
  3.4 0.0 copy-start.4
  3.4 0.0 copy-start
  3.4 0.0 copy-start.2
  3.4 0.0 copy-start.3
  3.4 16.5 %all-to-all-start = ((f32[1152,1,128]{2,1,0:T(1,128)}), f32[1152,1,128]{2,1,0:T(1,128)S(1)}, u32[]{:S(2)}, u32[]{:S(2)}) async-start(f32[1152,1,128]{2,1,0:T(1,128)} %bitcast.23), calls=%async_computation | async-start | bytes 1179648 | tf_op jit(solution)/shard_map/all_to_all | solution.py:419
  19.9 0.7 collective-permute-start
  20.6 6.3 %collective-permute-start.1 = (f32[208,256]{1,0:T(8,128)}, f32[208,256]{1,0:T(8,128)S(1)}, u32[]{:S(2)}, u32[]{:S(2)}) collective-permute-start(f32[208,256]{1,0:T(8,128)} %get-tuple-element.24), channel_id=1, source_target_pairs={{1,0},{2,1},{3,2},{4,3},{5,4},{6,5},{7,6},{8,7},{9,8},{10,9},{11,1... | collective-permute-start | bytes 638984 | tf_op jit(solution)/shard_map/ppermute | solution.py:418
  26.9 0.0 copy-done.1
  26.9 0.0 copy-done.6
  26.9 0.0 copy-done.7
  26.9 0.1 shard_map.142.own
  27.0 1.6 %collective-permute-start.2 = (f32[4,56,128]{2,1,0:T(8,128)S(1)}, f32[4,56,128]{2,1,0:T(8,128)S(1)}, u32[]{:S(2)}, u32[]{:S(2)}) collective-permute-start(f32[4,56,128]{2,1,0:T(8,128)S(1)} %shard_map.142.own), channel_id=1, source_target_pairs={{0,128},{128,0},{1,129},{129,1},{2,130},{130,2},{3,131},{131,3},{4... | collective-permute-start | bytes 344072 | tf_op jit(solution)/shard_map/ppermute | solution.py:449
  28.6 1.0 %collective-permute-done.2.other = f32[4,56,128]{2,1,0:T(8,128)S(1)} collective-permute-done((f32[4,56,128]{2,1,0:T(8,128)S(1)}, f32[4,56,128]{2,1,0:T(8,128)S(1)}, u32[]{:S(2)}, u32[]{:S(2)}) %collective-permute-start.2) | collective-permute-done | bytes 114720 | tf_op jit(solution)/shard_map/ppermute | solution.py:449
  29.6 0.0 copy-done.4
  29.6 0.7 shard_map.143
  30.2 13.3 %collective-permute-done.from_left = f32[208,256]{1,0:T(8,128)S(1)} collective-permute-done((f32[208,256]{1,0:T(8,128)}, f32[208,256]{1,0:T(8,128)S(1)}, u32[]{:S(2)}, u32[]{:S(2)}) %collective-permute-start) | collective-permute-done | bytes 213024 | tf_op jit(solution)/shard_map/ppermute | solution.py:417
  43.5 0.0 collective-permute-done.1.from_right
  43.5 0.0 copy-done
  43.5 0.0 copy-done.2
  43.5 0.0 copy-done.3
  43.5 4.2 %shard_map.141 = f32[45,4,512]{2,1,0:T(4,128)} custom-call(f32[45,4,512]{2,1,0:T(4,128)S(1)} %bitcast.20, s32[6,512]{1,0:T(8,128)S(1)} %copy-done.2, f32[6,512]{1,0:T(8,128)S(1)} %copy-done.3, f32[208,256]{1,0:T(8,128)S(1)} %collective-permute-done.from_left, f32[208,256]{1,0:T(8,128)S(1)} %collective-permute-done.1.from_right), custom_call_target="tpu_custom_call" | custom-call | flops 4200000000 | bytes 262144 | tf_op jit(solution)/shard_map/pallas_call | solution.py:420
  47.7 0.0 all-to-all-done
  47.8 2.0 %shard_map.144 = (f32[5040,128]{1,0:T(8,128)S(1)}, f32[5040,128]{1,0:T(8,128)S(1)}, f32[5040,128]{1,0:T(8,128)S(1)}, f32[48,128]{1,0:T(8,128)S(1)}, f32[360,128]{1,0:T(8,128)S(1)}, /*index=5*/f32[224,128]{1,0:T(8,128)S(1)}) custom-call(s32[1]{0:T(128)} %bitcast.6.side, f32[1152,128]{1,0:T(8,128)S(1)} %bitcast.16, s32[1,512]{1,0:T(1,128)S(1)} %copy-done.4, ...), custom_call_target="tpu_custom_call" | custom-call | flops 2000000000 | bytes 262144 | tf_op jit(solution)/shard_map/pallas_call | solution.py:453
  49.8 1.6 %collective-permute-start.3 = (f32[224,128]{1,0:T(8,128)S(1)}, f32[224,128]{1,0:T(8,128)S(1)}, u32[]{:S(2)}, u32[]{:S(2)}) collective-permute-start(f32[224,128]{1,0:T(8,128)S(1)} %get-tuple-element.34), channel_id=1, source_target_pairs={{0,128},{128,0},{1,129},{129,1},{2,130},{130,2},{3,131},{131,3},{4... | collective-permute-start | bytes 344072 | tf_op jit(solution)/shard_map/ppermute | solution.py:467
  51.4 1.0 %collective-permute-done.3.gotten = f32[224,128]{1,0:T(8,128)S(1)} collective-permute-done((f32[224,128]{1,0:T(8,128)S(1)}, f32[224,128]{1,0:T(8,128)S(1)}, u32[]{:S(2)}, u32[]{:S(2)}) %collective-permute-start.3) | collective-permute-done | bytes 114720 | tf_op jit(solution)/shard_map/ppermute | solution.py:467
  52.4 0.0 copy-start.5
  52.4 0.8 %shard_map.145 = f32[256,128]{1,0:T(8,128)S(1)} custom-call(s32[1]{0:T(128)} %bitcast.6.side, f32[224,128]{1,0:T(8,128)S(1)} %collective-permute-done.3.gotten, f32[5040,128]{1,0:T(8,128)S(1)} %get-tuple-element.35.trans, f32[5040,128]{1,0:T(8,128)S(1)} %get-tuple-element.36.glow, f32[5040,128]{1,0:T(8,128)S(1)} %get-tuple-element.37.passing, ...), custom_call_target="tpu_custom_call" | custom-call | flops 900000000 | bytes 262144 | tf_op jit(solution)/shard_map/pallas_call | solution.py:468
  53.2 17.6 %all_to_all.10 = f32[256,1,128]{2,1,0:T(1,128)S(1)} all-to-all(f32[256,1,128]{2,1,0:T(1,128)S(1)} %bitcast.17), channel_id=1, replica_groups=mesh['sec'=2,'grp'=128] {'grp'}, dimensions={0} | all-to-all | bytes 262144 | tf_op jit(solution)/shard_map/all_to_all | solution.py:475
  70.8 0.0 copy-done.5
  70.8 1.0 %shard_map.146 = f32[45,512]{1,0:T(8,128)} custom-call(f32[256,128]{1,0:T(8,128)S(1)} %bitcast.18, s32[1,512]{1,0:T(1,128)S(1)} %copy-done.5), custom_call_target="tpu_custom_call" | custom-call | flops 1000000000 | bytes 262144 | tf_op jit(solution)/shard_map/pallas_call | solution.py:478
Async XLA Ops:
  0.6 26.3 %copy-start.1 = (f32[4,56,90]{2,1,0:T(8,128)S(1)}, f32[4,56,90]{2,1,0:T(8,128)}, u32[]{:S(2)}) copy-start(f32[4,56,90]{2,1,0:T(8,128)} %opacity.1) | copy-start | bytes 241924
  0.6 26.3 %copy-start.6 = (f32[56]{0:T(128)S(1)}, f32[56]{0:T(128)}, u32[]{:S(2)}) copy-start(f32[56]{0:T(128)} %param.24) | copy-start | bytes 676
  0.7 26.2 %copy-start.7 = (f32[56]{0:T(128)S(1)}, f32[56]{0:T(128)}, u32[]{:S(2)}) copy-start(f32[56]{0:T(128)} %param.25) | copy-start | bytes 676
  3.4 26.2 %copy-start.4 = (s32[1,512]{1,0:T(1,128)S(1)}, s32[1,512]{1,0:T(1,128)}, u32[]{:S(2)}) copy-start(s32[1,512]{1,0:T(1,128)} %member.3) | copy-start | bytes 6148
  3.4 40.1 %copy-start = (f32[4,45,512]{2,0,1:T(4,128)S(1)}, f32[4,45,512]{2,0,1:T(4,128)}, u32[]{:S(2)}) copy-start(f32[4,45,512]{2,0,1:T(4,128)} %param.15) | copy-start | bytes 1105924
  3.4 40.1 %copy-start.2 = (s32[6,512]{1,0:T(8,128)S(1)}, s32[6,512]{1,0:T(8,128)}, u32[]{:S(2)}) copy-start(s32[6,512]{1,0:T(8,128)} %adj.1) | copy-start | bytes 36868
  3.4 40.1 %copy-start.3 = (f32[6,512]{1,0:T(8,128)S(1)}, f32[6,512]{1,0:T(8,128)}, u32[]{:S(2)}) copy-start(f32[6,512]{1,0:T(8,128)} %coef.1) | copy-start | bytes 36868
  3.4 44.3 %all-to-all-start = ((f32[1152,1,128]{2,1,0:T(1,128)}), f32[1152,1,128]{2,1,0:T(1,128)S(1)}, u32[]{:S(2)}, u32[]{:S(2)}) async-start(f32[1152,1,128]{2,1,0:T(1,128)} %bitcast.23), calls=%async_computation | async-start | bytes 1179648 | tf_op jit(solution)/shard_map/all_to_all | solution.py:419
  19.9 23.6 %collective-permute-start = (f32[208,256]{1,0:T(8,128)}, f32[208,256]{1,0:T(8,128)S(1)}, u32[]{:S(2)}, u32[]{:S(2)}) collective-permute-start(f32[208,256]{1,0:T(8,128)} %get-tuple-element.23), channel_id=1, source_target_pairs={{0,1},{1,2},{2,3},{3,4},{4,5},{5,6},{6,7},{7,8},{8,9},{9,10},{10,1... | collective-permute-start | bytes 638984 | tf_op jit(solution)/shard_map/ppermute | solution.py:417
  20.6 22.9 %collective-permute-start.1 = (f32[208,256]{1,0:T(8,128)}, f32[208,256]{1,0:T(8,128)S(1)}, u32[]{:S(2)}, u32[]{:S(2)}) collective-permute-start(f32[208,256]{1,0:T(8,128)} %get-tuple-element.24), channel_id=1, source_target_pairs={{1,0},{2,1},{3,2},{4,3},{5,4},{6,5},{7,6},{8,7},{9,8},{10,9},{11,1... | collective-permute-start | bytes 638984 | tf_op jit(solution)/shard_map/ppermute | solution.py:418
  27.0 2.6 %collective-permute-start.2 = (f32[4,56,128]{2,1,0:T(8,128)S(1)}, f32[4,56,128]{2,1,0:T(8,128)S(1)}, u32[]{:S(2)}, u32[]{:S(2)}) collective-permute-start(f32[4,56,128]{2,1,0:T(8,128)S(1)} %shard_map.142.own), channel_id=1, source_target_pairs={{0,128},{128,0},{1,129},{129,1},{2,130},{130,2},{3,131},{131,3},{4... | collective-permute-start | bytes 344072 | tf_op jit(solution)/shard_map/ppermute | solution.py:449
  49.8 2.6 %collective-permute-start.3 = (f32[224,128]{1,0:T(8,128)S(1)}, f32[224,128]{1,0:T(8,128)S(1)}, u32[]{:S(2)}, u32[]{:S(2)}) collective-permute-start(f32[224,128]{1,0:T(8,128)S(1)} %get-tuple-element.34), channel_id=1, source_target_pairs={{0,128},{128,0},{1,129},{129,1},{2,130},{130,2},{3,131},{131,3},{4... | collective-permute-start | bytes 344072 | tf_op jit(solution)/shard_map/ppermute | solution.py:467
  52.4 18.4 %copy-start.5 = (s32[1,512]{1,0:T(1,128)S(1)}, s32[1,512]{1,0:T(1,128)}, u32[]{:S(2)}) copy-start(s32[1,512]{1,0:T(1,128)} %pos.1) | copy-start | bytes 6148

commit v8 on v7

--- a/solution.py
+++ b/solution.py
@@ -33,6 +33,8 @@
 BLOCK = 9
 BLOCKS = LEV // BLOCK
 GALL = 2 * GH
+TALL = 512
+DEEP = 2 * BLOCKS * TALL
 PART = 40
 NT = (((1,), (1,)), ((), ()))
 NN = (((1,), (0,)), ((), ()))
@@ -121,7 +123,8 @@
         joined[0, :, 2 * LEV + k : 2 * LEV + k + 1] = jnp.sum(square, axis=1, keepdims=True)
 
 
-def weight_kernel(side, own, other, member, weights, emit, shine, spread, full):
+def weight_kernel(side, own, other, member, pos, weights, emit, shine, spread, placing, full):
+    placing[...] = slot_matrix(pos[...])
     ids = (member[...] >> 2).astype(F32)
     spots = lax.broadcasted_iota(jnp.int32, (128, RAD), 1).astype(F32)
     for k in range(SLOTS):
@@ -146,8 +149,9 @@
         lane = jnp.where(rows < BLOCK, SPECIES * rows + s + PART, -1)
         picks.append(lanes == lane)
     picker = jnp.concatenate([jnp.where(p, 1.0, 0.0).astype(BF) for p in picks], axis=0)
-    group = lax.broadcasted_iota(jnp.int32, (GALL, 128), 1)
+    group = lax.broadcasted_iota(jnp.int32, (GH, 128), 1)
     group = jnp.where(group >= 2 * PART, group - 2 * PART, jnp.where(group >= PART, group - PART, group)) >> 2
+    pad = jnp.zeros((TALL - BLOCK * GH, 128), F32)
     for b in range(BLOCKS):
         his, los = [], []
         for table in tables:
@@ -155,9 +159,11 @@
             his.append(hi)
             los.append(lo)
         wide = dot(jnp.concatenate(his + los, axis=1), picker, NN)
-        for i in range(BLOCK):
-            start = (b * BLOCK + i) * GALL
-            weights[start : start + GALL, :] = jnp.where(group == i, wide, 0.0).astype(BF)
+        for half in range(2):
+            part = wide[half * GH : (half + 1) * GH, :]
+            block = jnp.concatenate([jnp.where(group == i, part, 0.0) for i in range(BLOCK)] + [pad], axis=0)
+            start = (half * BLOCKS + b) * TALL
+            weights[start : start + TALL, :] = block.astype(BF)
 
 
 def fold(x):
@@ -165,10 +171,11 @@
 
 
 def span(level, half):
-    return slice(level * GALL + half * GH, level * GALL + (half + 1) * GH)
-
-
-def first_kernel(side, arrived, member, weights, emit, shine, trans, glow, passing, thick, sums, edge, stage, pooled, warm):
+    start = (half * BLOCKS + level // BLOCK) * TALL + level % BLOCK * GH
+    return slice(start, start + GH)
+
+
+def first_kernel(side, arrived, member, weights, emit, shine, trans, glow, passing, thick, sums, edge, stage, pooled, warm, amounts):
     lane = lax.broadcasted_iota(jnp.int32, (PEERS, 128), 1) >> 5
     last = arrived[pl.ds(CHUNK - 1, PEERS, CHUNK), :]
     for m in range(SLOTS):
@@ -190,13 +197,22 @@
     thick[...] = pooled[ROW:BASE, :]
     pooled[BASE:FEAT, :] = pooled[BASE:FEAT, :] * (-DIFFUSE * LOG2E)
     pad = jnp.zeros((128 - 3 * PART, RAD), F32)
-    tall = BLOCK * GALL
     for b in range(BLOCKS):
         start = BASE + SPECIES * BLOCK * b
         part = pooled[start : start + PART, :]
         hi = part.astype(BF).astype(F32)
-        amounts = jnp.concatenate([hi, hi, part - hi, pad], axis=0).astype(BF)
-        passing[b * tall : (b + 1) * tall, :] = dot(weights[b * tall : (b + 1) * tall, :], amounts, NN)
+        amounts[b * 128 : (b + 1) * 128, :] = jnp.concatenate([hi, hi, part - hi, pad], axis=0).astype(BF)
+
+    def depths(half, b):
+        rows = slice((half * BLOCKS + b) * TALL, (half * BLOCKS + b + 1) * TALL)
+        passing[rows, :] = dot(weights[rows, :], amounts[b * 128 : (b + 1) * 128, :], NN)
+
+    def ahead(order, place):
+        if place == 0:
+            depths(*order[0])
+        if place + 1 < len(order):
+            depths(*order[place + 1])
+
     me = side[0]
 
     def optics(l, half):
@@ -214,12 +230,15 @@
 
     @pl.when(me == 0)
     def _():
+        order = [(half, b) for half in range(2) for b in range(BLOCKS)]
         for half in range(2):
             part = slice(half * GH, (half + 1) * GH)
             thermal = jnp.zeros((GH, RAD), F32)
             direct = shine[part, :] * surface[7:8, :]
             above = fold(direct)
             for l in range(LEV):
+                if l % BLOCK == 0:
+                    ahead(order, half * BLOCKS + l // BLOCK)
                 kept, added, passed = optics(l, half)
                 thermal = kept * thermal + added
                 direct = direct * passed
@@ -232,11 +251,14 @@
     @pl.when(me == 1)
     def _():
         ground = jnp.square(jnp.square(surface[5:6, :]))
+        order = [(half, BLOCKS - 1 - b) for half in range(2) for b in range(BLOCKS)]
         for half in range(2):
             part = slice(half * GH, (half + 1) * GH)
             upward = emit[part, :] * ground
             below = fold(upward)
             for l in range(LEV - 1, -1, -1):
+                if l % BLOCK == BLOCK - 1:
+                    ahead(order, half * BLOCKS + BLOCKS - 1 - l // BLOCK)
                 kept, added, passed = optics(l, half)
                 passing[span(l, half), :] = passed
                 upward = kept * upward + added
@@ -290,14 +312,13 @@
         send[pl.ds(h, PEERS, 2), :] = jnp.where(lanes < 64, even, odd)
 
 
-def unplace_kernel(returned, pos, heating):
+def unplace_kernel(returned, placing, heating):
     parts = []
     for h in range(2):
         turned = returned[pl.ds(h, PEERS, 2), :].T
         parts += [turned[0:ROW, :], turned[64 : 64 + ROW, :]]
     hi, lo = split(jnp.concatenate(parts, axis=1))
-    placing = slot_matrix(pos[...])
-    heating[...] = (dot(hi, placing, NN) + dot(lo, placing, NN))[0:LEV, :]
+    heating[...] = (dot(hi, placing[...], NN) + dot(lo, placing[...], NN))[0:LEV, :]
 
 
 def mix_kernel(tracers, adj, coef, from_left, from_right, mixed, high, low, band, stage):
@@ -434,34 +455,39 @@
     )
     whole = pl.BlockSpec(memory_space=pltpu.VMEM)
     scalar = pl.BlockSpec(memory_space=pltpu.SMEM)
-    rows = LEV * GALL
-    weights, emit, shine, spread = call(
+    weights, emit, shine, spread, placing = call(
         weight_kernel,
         "weight",
         (
-            jax.ShapeDtypeStruct((rows, 128), BF),
+            jax.ShapeDtypeStruct((DEEP, 128), BF),
             shape(GALL, RAD),
             shape(GALL, RAD),
             jax.ShapeDtypeStruct((COLS, RAD), BF),
+            jax.ShapeDtypeStruct((COLS, COLS), BF),
         ),
         [pltpu.VMEM((2, SPECIES, GH, 128), F32)],
-        in_specs=[scalar] + [whole] * 3,
-    )(side, opacity, lax.ppermute(opacity, "sec", swap), arrival_membership)
-    arrived, mixed, weights, emit, shine, spread, side = lax.optimization_barrier(
-        (arrived, mixed, weights, emit, shine, spread, side)
+        in_specs=[scalar] + [whole] * 4,
+    )(side, opacity, lax.ppermute(opacity, "sec", swap), arrival_membership, dispatch_position)
+    arrived, mixed, weights, emit, shine, spread, placing, side = lax.optimization_barrier(
+        (arrived, mixed, weights, emit, shine, spread, placing, side)
     )
     trans, glow, passing, thick, sums, edge = call(
         first_kernel,
         "first",
         (
-            shape(rows, RAD),
-            shape(rows, RAD),
-            shape(rows, RAD),
+            shape(DEEP, RAD),
+            shape(DEEP, RAD),
+            shape(DEEP, RAD),
             shape(ROW, RAD),
             shape(8 * LEV, RAD),
             shape(2 * GALL, RAD),
         ),
-        [pltpu.VMEM((3, COLS, 128), F32), pltpu.VMEM((FEAT, RAD), F32), pltpu.VMEM((ROW, RAD), F32)],
+        [
+            pltpu.VMEM((3, COLS, 128), F32),
+            pltpu.VMEM((FEAT, RAD), F32),
+            pltpu.VMEM((ROW, RAD), F32),
+            pltpu.VMEM((BLOCKS * 128, RAD), BF),
+        ],
         in_specs=[scalar] + [whole] * 5,
     )(side, arrived.reshape(PEERS * CHUNK, 128), arrival_membership, weights, emit, shine)
     gotten = lax.ppermute(edge, "sec", swap)
@@ -475,7 +501,7 @@
     returned = lax.all_to_all(
         back.reshape(PEERS * 2, 1, 128), "grp", split_axis=0, concat_axis=0, tiled=True
     ).reshape(PEERS * 2, 128)
-    heating = call(unplace_kernel, "unplace", shape(LEV, COLS), [])(returned, dispatch_position)
+    heating = call(unplace_kernel, "unplace", shape(LEV, COLS), [])(returned, placing)
     return (heating, jnp.transpose(mixed, (1, 0, 2)))
 
 

time: 72 us -> 71.4 us (level)
  waiting for transfers between devices: 15.2 us -> 14.3 us
  local copies, waits for them, and re-layouts: 0.04 us -> 0.84 us
    ppermute x1, waiting for transfers between devices: 13.3 us -> 12.3 us  [per_device(): from_left = lax.ppermute(right, 'grp', up)]
    unnamed x16 -> x20, local copies, waits for them, and re-layouts: 0.04 us -> 0.84 us
where the time goes in v8:
time: 71.4 us; the launch traced here: 71.2 us
  starting transfers between devices  26.6 us (37%)
  blocking collectives  17.6 us (25%)
  waiting for transfers between devices  14.3 us (20%)
  Pallas kernels  11.1 us (16%)
  local copies, waits for them, and re-layouts  0.84 us (1%)
  between operations  0.76 us (1%)
    all_to_all x1, blocking collectives, per_device(): lax.all_to_all(back.reshape(PEERS * 2, 1, 128), 'grp', split_axis=0, conc...  17.6 us
    all_to_all x1, starting transfers between devices, per_device(): lax.all_to_all(send.reshape(PEERS * CHUNK, 1, 128), 'grp', split_axis=0,...  16.5 us
    ppermute x1, waiting for transfers between devices, per_device(): from_left = lax.ppermute(right, 'grp', up)  12.3 us
    ppermute x1, starting transfers between devices, per_device(): from_right = lax.ppermute(left, 'grp', down)  6.32 us
    pallas_call x1, Pallas kernels, per_device(): call(mix_kernel, 'mix', shape(LEV, SPECIES, COLS), [pltpu.VMEM((2, BODY,...  4.22 us
    pallas_call x1, Pallas kernels, per_device(): call(pack_kernel, 'pack', packed, [pltpu.VMEM(dims, F32) for dims in give...  2.74 us
    pallas_call x1, Pallas kernels, per_device(): call(first_kernel, 'first', (shape(DEEP, RAD), shape(DEEP, RAD), shape(DE...  1.62 us
    ppermute x1, starting transfers between devices, per_device(): lax.ppermute(opacity, 'sec', swap)  1.6 us
  transfers between devices with their start and end apart: 5, of which 3 were waited for; matrix products, arithmetic and copies ran while one was open for 0% of the time, Pallas kernels for 7%

profile of v8, /device:TPU:1, one launch (start us, length us, event | category | flops | bytes accessed | tf_op | source)
XLA Modules:
  0.0 71.2 jit_solution(13575191764477489761)
XLA Ops:
  0.6 0.0 copy-start.1
  0.6 0.0 copy-start.6
  0.7 0.0 copy-start.7
  0.7 2.7 %shard_map.140 = (f32[1152,128]{1,0:T(8,128)}, f32[208,256]{1,0:T(8,128)}, f32[208,256]{1,0:T(8,128)}) custom-call(f32[45,512]{1,0:T(8,128)} %refs_0_.1, f32[45,512]{1,0:T(8,128)} %refs_1_.1, f32[45,4,512]{2,1,0:T(4,128)} %bitcast.19, f32[1,512]{1,0:T(1,128)} %bitcast.24, f32[1,512]{1,0:T(1,128)} %bitcast.25, s32[1,512]{1,0:T(1,128)} %bitcast.26, ...), custom_call_target="tpu_custom_call" | custom-call | flops 2700000000 | bytes 262144 | tf_op jit(solution)/shard_map/pallas_call | solution.py:415
  3.4 0.0 copy-start.4
  3.4 0.0 copy-start.5
  3.4 0.0 copy-start
  3.4 0.0 copy-start.2
  3.5 0.0 copy-start.3
  3.5 16.5 %all-to-all-start = ((f32[1152,1,128]{2,1,0:T(1,128)}), f32[1152,1,128]{2,1,0:T(1,128)S(1)}, u32[]{:S(2)}, u32[]{:S(2)}) async-start(f32[1152,1,128]{2,1,0:T(1,128)} %bitcast.23), calls=%async_computation | async-start | bytes 1179648 | tf_op jit(solution)/shard_map/all_to_all | solution.py:440
  19.9 0.7 collective-permute-start
  20.6 6.3 %collective-permute-start.1 = (f32[208,256]{1,0:T(8,128)}, f32[208,256]{1,0:T(8,128)S(1)}, u32[]{:S(2)}, u32[]{:S(2)}) collective-permute-start(f32[208,256]{1,0:T(8,128)} %get-tuple-element.26), channel_id=1, source_target_pairs={{1,0},{2,1},{3,2},{4,3},{5,4},{6,5},{7,6},{8,7},{9,8},{10,9},{11,1... | collective-permute-start | bytes 638984 | tf_op jit(solution)/shard_map/ppermute | solution.py:439
  26.9 0.0 copy-done.1
  26.9 0.0 copy-done.6
  26.9 0.0 copy-done.7
  26.9 0.1 shard_map.142.own
  27.0 1.6 %collective-permute-start.2 = (f32[4,56,128]{2,1,0:T(8,128)S(1)}, f32[4,56,128]{2,1,0:T(8,128)S(1)}, u32[]{:S(2)}, u32[]{:S(2)}) collective-permute-start(f32[4,56,128]{2,1,0:T(8,128)S(1)} %shard_map.142.own), channel_id=1, source_target_pairs={{0,128},{128,0},{1,129},{129,1},{2,130},{130,2},{3,131},{131,3},{4... | collective-permute-start | bytes 344072 | tf_op jit(solution)/shard_map/ppermute | solution.py:470
  28.6 1.0 %collective-permute-done.2.other = f32[4,56,128]{2,1,0:T(8,128)S(1)} collective-permute-done((f32[4,56,128]{2,1,0:T(8,128)S(1)}, f32[4,56,128]{2,1,0:T(8,128)S(1)}, u32[]{:S(2)}, u32[]{:S(2)}) %collective-permute-start.2) | collective-permute-done | bytes 114720 | tf_op jit(solution)/shard_map/ppermute | solution.py:470
  29.6 0.0 copy-done.4
  29.6 0.0 copy-done.5
  29.6 0.8 %shard_map.143 = (bf16[5120,128]{1,0:T(8,128)(2,1)S(1)}, f32[112,128]{1,0:T(8,128)S(1)}, f32[112,128]{1,0:T(8,128)S(1)}, bf16[512,128]{1,0:T(8,128)(2,1)S(1)}, bf16[512,512]{1,0:T(8,128)(2,1)S(1)}) custom-call(s32[1]{0:T(128)} %bitcast.6.side, f32[4,56,128]{2,1,0:T(8,128)S(1)} %shard_map.142.own, f32[4,56,128]{2,1,0:T(8,128)S(1)} %collective-permute-done.2.other, ...), custom_call_target="tpu_custom_call" | custom-call | flops 700000000 | bytes 262144 | tf_op jit(solution)/shard_map/pallas_call | solution.py:458
  30.4 0.0 copy-start.8
  30.4 0.8 %copy-done.8 = bf16[512,512]{1,0:T(8,128)(2,1)} copy-done((bf16[512,512]{1,0:T(8,128)(2,1)}, bf16[512,512]{1,0:T(8,128)(2,1)S(1)}, u32[]{:S(2)}) %copy-start.8) | copy-done | bytes 524312
  31.2 12.3 %collective-permute-done.from_left = f32[208,256]{1,0:T(8,128)S(1)} collective-permute-done((f32[208,256]{1,0:T(8,128)}, f32[208,256]{1,0:T(8,128)S(1)}, u32[]{:S(2)}, u32[]{:S(2)}) %collective-permute-start) | collective-permute-done | bytes 213024 | tf_op jit(solution)/shard_map/ppermute | solution.py:438
  43.5 0.0 collective-permute-done.1.from_right
  43.5 0.0 copy-done
  43.5 0.0 copy-done.2
  43.5 0.0 copy-done.3
  43.5 4.2 %shard_map.141 = f32[45,4,512]{2,1,0:T(4,128)} custom-call(f32[45,4,512]{2,1,0:T(4,128)S(1)} %bitcast.20, s32[6,512]{1,0:T(8,128)S(1)} %copy-done.2, f32[6,512]{1,0:T(8,128)S(1)} %copy-done.3, f32[208,256]{1,0:T(8,128)S(1)} %collective-permute-done.from_left, f32[208,256]{1,0:T(8,128)S(1)} %collective-permute-done.1.from_right), custom_call_target="tpu_custom_call" | custom-call | flops 4200000000 | bytes 262144 | tf_op jit(solution)/shard_map/pallas_call | solution.py:441
  47.7 0.0 all-to-all-done
  47.8 1.6 %shard_map.144 = (f32[5120,128]{1,0:T(8,128)S(1)}, f32[5120,128]{1,0:T(8,128)S(1)}, f32[5120,128]{1,0:T(8,128)S(1)}, f32[48,128]{1,0:T(8,128)S(1)}, f32[360,128]{1,0:T(8,128)S(1)}, /*index=5*/f32[224,128]{1,0:T(8,128)S(1)}) custom-call(s32[1]{0:T(128)} %bitcast.6.side, f32[1152,128]{1,0:T(8,128)S(1)} %bitcast.16, s32[1,512]{1,0:T(1,128)S(1)} %copy-done.5, ...), custom_call_target="tpu_custom_call" | custom-call | flops 2000000000 | bytes 262144 | tf_op jit(solution)/shard_map/pallas_call | solution.py:474
  49.4 1.5 %collective-permute-start.3 = (f32[224,128]{1,0:T(8,128)S(1)}, f32[224,128]{1,0:T(8,128)S(1)}, u32[]{:S(2)}, u32[]{:S(2)}) collective-permute-start(f32[224,128]{1,0:T(8,128)S(1)} %get-tuple-element.37), channel_id=1, source_target_pairs={{0,128},{128,0},{1,129},{129,1},{2,130},{130,2},{3,131},{131,3},{4... | collective-permute-start | bytes 344072 | tf_op jit(solution)/shard_map/ppermute | solution.py:493
  50.9 1.0 %collective-permute-done.3.gotten = f32[224,128]{1,0:T(8,128)S(1)} collective-permute-done((f32[224,128]{1,0:T(8,128)S(1)}, f32[224,128]{1,0:T(8,128)S(1)}, u32[]{:S(2)}, u32[]{:S(2)}) %collective-permute-start.3) | collective-permute-done | bytes 114720 | tf_op jit(solution)/shard_map/ppermute | solution.py:493
  51.9 0.0 copy-start.9
  51.9 0.7 %shard_map.145 = f32[256,128]{1,0:T(8,128)S(1)} custom-call(s32[1]{0:T(128)} %bitcast.6.side, f32[224,128]{1,0:T(8,128)S(1)} %collective-permute-done.3.gotten, f32[5120,128]{1,0:T(8,128)S(1)} %get-tuple-element.38.trans, f32[5120,128]{1,0:T(8,128)S(1)} %get-tuple-element.39.glow, f32[5120,128]{1,0:T(8,128)S(1)} %get-tuple-element.40.passing, ...), custom_call_target="tpu_custom_call" | custom-call | flops 900000000 | bytes 262144 | tf_op jit(solution)/shard_map/pallas_call | solution.py:494
  52.6 17.6 %all_to_all.10 = f32[256,1,128]{2,1,0:T(1,128)S(1)} all-to-all(f32[256,1,128]{2,1,0:T(1,128)S(1)} %bitcast.17), channel_id=1, replica_groups=mesh['sec'=2,'grp'=128] {'grp'}, dimensions={0} | all-to-all | bytes 262144 | tf_op jit(solution)/shard_map/all_to_all | solution.py:501
  70.2 0.0 copy-done.9
  70.2 1.0 %shard_map.146 = f32[45,512]{1,0:T(8,128)} custom-call(f32[256,128]{1,0:T(8,128)S(1)} %bitcast.18, bf16[512,512]{1,0:T(8,128)(2,1)S(1)} %copy-done.9), custom_call_target="tpu_custom_call" | custom-call | flops 1000000000 | bytes 262144 | tf_op jit(solution)/shard_map/pallas_call | solution.py:504
Async XLA Ops:
  0.6 26.3 %copy-start.1 = (f32[4,56,90]{2,1,0:T(8,128)S(1)}, f32[4,56,90]{2,1,0:T(8,128)}, u32[]{:S(2)}) copy-start(f32[4,56,90]{2,1,0:T(8,128)} %opacity.1) | copy-start | bytes 241924
  0.6 26.3 %copy-start.6 = (f32[56]{0:T(128)S(1)}, f32[56]{0:T(128)}, u32[]{:S(2)}) copy-start(f32[56]{0:T(128)} %param.24) | copy-start | bytes 676
  0.7 26.3 %copy-start.7 = (f32[56]{0:T(128)S(1)}, f32[56]{0:T(128)}, u32[]{:S(2)}) copy-start(f32[56]{0:T(128)} %param.25) | copy-start | bytes 676
  3.4 26.2 %copy-start.4 = (s32[1,512]{1,0:T(1,128)S(1)}, s32[1,512]{1,0:T(1,128)}, u32[]{:S(2)}) copy-start(s32[1,512]{1,0:T(1,128)} %pos.1) | copy-start | bytes 6148
  3.4 26.2 %copy-start.5 = (s32[1,512]{1,0:T(1,128)S(1)}, s32[1,512]{1,0:T(1,128)}, u32[]{:S(2)}) copy-start(s32[1,512]{1,0:T(1,128)} %member.3) | copy-start | bytes 6148
  3.4 40.1 %copy-start = (f32[4,45,512]{2,0,1:T(4,128)S(1)}, f32[4,45,512]{2,0,1:T(4,128)}, u32[]{:S(2)}) copy-start(f32[4,45,512]{2,0,1:T(4,128)} %param.15) | copy-start | bytes 1105924
  3.4 40.1 %copy-start.2 = (s32[6,512]{1,0:T(8,128)S(1)}, s32[6,512]{1,0:T(8,128)}, u32[]{:S(2)}) copy-start(s32[6,512]{1,0:T(8,128)} %adj.1) | copy-start | bytes 36868
  3.5 40.1 %copy-start.3 = (f32[6,512]{1,0:T(8,128)S(1)}, f32[6,512]{1,0:T(8,128)}, u32[]{:S(2)}) copy-start(f32[6,512]{1,0:T(8,128)} %coef.1) | copy-start | bytes 36868
  3.5 44.3 %all-to-all-start = ((f32[1152,1,128]{2,1,0:T(1,128)}), f32[1152,1,128]{2,1,0:T(1,128)S(1)}, u32[]{:S(2)}, u32[]{:S(2)}) async-start(f32[1152,1,128]{2,1,0:T(1,128)} %bitcast.23), calls=%async_computation | async-start | bytes 1179648 | tf_op jit(solution)/shard_map/all_to_all | solution.py:440
  19.9 23.6 %collective-permute-start = (f32[208,256]{1,0:T(8,128)}, f32[208,256]{1,0:T(8,128)S(1)}, u32[]{:S(2)}, u32[]{:S(2)}) collective-permute-start(f32[208,256]{1,0:T(8,128)} %get-tuple-element.25), channel_id=1, source_target_pairs={{0,1},{1,2},{2,3},{3,4},{4,5},{5,6},{6,7},{7,8},{8,9},{9,10},{10,1... | collective-permute-start | bytes 638984 | tf_op jit(solution)/shard_map/ppermute | solution.py:438
  20.6 22.9 %collective-permute-start.1 = (f32[208,256]{1,0:T(8,128)}, f32[208,256]{1,0:T(8,128)S(1)}, u32[]{:S(2)}, u32[]{:S(2)}) collective-permute-start(f32[208,256]{1,0:T(8,128)} %get-tuple-element.26), channel_id=1, source_target_pairs={{1,0},{2,1},{3,2},{4,3},{5,4},{6,5},{7,6},{8,7},{9,8},{10,9},{11,1... | collective-permute-start | bytes 638984 | tf_op jit(solution)/shard_map/ppermute | solution.py:439
  27.0 2.6 %collective-permute-start.2 = (f32[4,56,128]{2,1,0:T(8,128)S(1)}, f32[4,56,128]{2,1,0:T(8,128)S(1)}, u32[]{:S(2)}, u32[]{:S(2)}) collective-permute-start(f32[4,56,128]{2,1,0:T(8,128)S(1)} %shard_map.142.own), channel_id=1, source_target_pairs={{0,128},{128,0},{1,129},{129,1},{2,130},{130,2},{3,131},{131,3},{4... | collective-permute-start | bytes 344072 | tf_op jit(solution)/shard_map/ppermute | solution.py:470
  30.4 0.8 %copy-start.8 = (bf16[512,512]{1,0:T(8,128)(2,1)}, bf16[512,512]{1,0:T(8,128)(2,1)S(1)}, u32[]{:S(2)}) copy-start(bf16[512,512]{1,0:T(8,128)(2,1)S(1)} %get-tuple-element.44.placing) | copy-start | bytes 1572868
  49.4 2.5 %collective-permute-start.3 = (f32[224,128]{1,0:T(8,128)S(1)}, f32[224,128]{1,0:T(8,128)S(1)}, u32[]{:S(2)}, u32[]{:S(2)}) collective-permute-start(f32[224,128]{1,0:T(8,128)S(1)} %get-tuple-element.37), channel_id=1, source_target_pairs={{0,128},{128,0},{1,129},{129,1},{2,130},{130,2},{3,131},{131,3},{4... | collective-permute-start | bytes 344072 | tf_op jit(solution)/shard_map/ppermute | solution.py:493
  51.9 18.3 %copy-start.9 = (bf16[512,512]{1,0:T(8,128)(2,1)S(1)}, bf16[512,512]{1,0:T(8,128)(2,1)}, u32[]{:S(2)}) copy-start(bf16[512,512]{1,0:T(8,128)(2,1)} %copy-done.8) | copy-start | bytes 1572868

commit v9 on v8

--- a/solution.py
+++ b/solution.py
@@ -68,7 +68,10 @@
     copies = [pltpu.make_async_copy(a, b, sems.at[i]) for i, (a, b) in enumerate(zip(sources, scratch))]
     for i in (6, 7, 8, 2, 0, 1, 3, 4, 5):
         copies[i].start()
-    stores = [pltpu.make_async_copy(a, b, done.at[i]) for i, (a, b) in enumerate(zip((send, right, left), outs))]
+    middle = PEERS * CHUNK // 2
+    pairs = [(send.at[0:middle, :], outs[0].at[0:middle, :]), (right, outs[1]), (left, outs[2])]
+    pairs.append((send.at[middle : 2 * middle, :], outs[0].at[middle : 2 * middle, :]))
+    stores = [pltpu.make_async_copy(a, b, done.at[i]) for i, (a, b) in enumerate(pairs)]
     bundle[ROW + LEV : BASE, :] = jnp.zeros((ROW - LEV, COLS), F32)
     spare = BASE + LEV * SPECIES
     bundle[spare:FEAT, :] = jnp.zeros((FEAT - spare, COLS), F32)
@@ -93,21 +96,19 @@
     bundle[LEV : LEV + 1, :] = ground[...]
     bundle[LEV + 1 : LEV + 2, :] = sunny
     bundle[LEV + 2 : LEV + 3, :] = day[...].astype(F32) * sunny
-    hi, lo = split(bundle[0:256, :])
-    packed = dot(placing, hi, NT) + dot(placing, lo, NT)
-    tail = bundle[256:288, :]
-    hi = tail.astype(BF).astype(F32)
-    tails = dot(placing, jnp.concatenate([hi] * SLOTS + [tail - hi] * SLOTS, axis=0).astype(BF), NT)
-    tails = tails[:, 0:128] + tails[:, 128:256]
-    lane = lax.broadcasted_iota(jnp.int32, (PEERS, 128), 1) >> 5
-    last = jnp.zeros((PEERS, 128), F32)
+    hi, lo = split(bundle[...])
+    tails = []
     for m in range(SLOTS):
-        block = packed[m * PEERS : (m + 1) * PEERS, :]
-        send[pl.ds(2 * m, PEERS, CHUNK), :] = block[:, 0:128]
-        send[pl.ds(2 * m + 1, PEERS, CHUNK), :] = block[:, 128:256]
-        last = jnp.where(lane == m, tails[m * PEERS : (m + 1) * PEERS, :], last)
-    send[pl.ds(CHUNK - 1, PEERS, CHUNK), :] = last
+        if m % 2 == 0:
+            pair = placing[m * PEERS : (m + 2) * PEERS, :]
+            packed = dot(hi, pair, NT) + dot(lo, pair, NT)
+        block = packed[:, m % 2 * PEERS : (m % 2 + 1) * PEERS]
+        send[pl.ds(2 * m, PEERS, CHUNK), :] = block[0:128, :].T
+        send[pl.ds(2 * m + 1, PEERS, CHUNK), :] = block[128:256, :].T
+        tails.append(block[256:288, :])
+    send[pl.ds(CHUNK - 1, PEERS, CHUNK), :] = jnp.concatenate(tails, axis=0).T
     stores[0].start()
+    stores[3].start()
     for store in stores:
         store.wait()
 
@@ -192,7 +193,7 @@
     tail = total[:, 256:384].T
     pooled[256:288, :] = tail[0:32] + tail[32:64] + tail[64:96] + tail[96:128]
     surface = pooled[40:48, :]
-    slant = jnp.broadcast_to(1.0 / (DIFFUSE * surface[6:7, :]), (GH, RAD))
+    slant = 1.0 / (DIFFUSE * surface[6:7, :])
     warm[...] = jnp.square(jnp.square(pooled[0:ROW, :]))
     thick[...] = pooled[ROW:BASE, :]
     pooled[BASE:FEAT, :] = pooled[BASE:FEAT, :] * (-DIFFUSE * LOG2E)
@@ -200,12 +201,15 @@
     for b in range(BLOCKS):
         start = BASE + SPECIES * BLOCK * b
         part = pooled[start : start + PART, :]
-        hi = part.astype(BF).astype(F32)
-        amounts[b * 128 : (b + 1) * 128, :] = jnp.concatenate([hi, hi, part - hi, pad], axis=0).astype(BF)
+        for k, values in enumerate((part, part * slant)):
+            hi = values.astype(BF).astype(F32)
+            mixture = jnp.concatenate([hi, hi, values - hi, pad], axis=0).astype(BF)
+            amounts[k, b * 128 : (b + 1) * 128, :] = mixture
 
     def depths(half, b):
         rows = slice((half * BLOCKS + b) * TALL, (half * BLOCKS + b + 1) * TALL)
-        passing[rows, :] = dot(weights[rows, :], amounts[b * 128 : (b + 1) * 128, :], NN)
+        for k, exponent in enumerate((trans, passing)):
+            exponent[rows, :] = dot(weights[rows, :], amounts[k, b * 128 : (b + 1) * 128, :], NN)
 
     def ahead(order, place):
         if place == 0:
@@ -216,13 +220,12 @@
     me = side[0]
 
     def optics(l, half):
-        tau = passing[span(l, half), :]
-        kept = jnp.exp2(tau)
+        kept = jnp.exp2(trans[span(l, half), :])
         source = emit[half * GH : (half + 1) * GH, :] * warm[l : l + 1, :]
         added = source - kept * source
         trans[span(l, half), :] = kept
         glow[span(l, half), :] = added
-        return kept, added, jnp.exp2(tau * slant)
+        return kept, added, jnp.exp2(passing[span(l, half), :])
 
     def note(l, half, change):
         row = slice(8 * l, 8 * l + 8)
@@ -420,7 +423,7 @@
         + [pltpu.VMEM((rows, COLS), jnp.int32) for rows in (1, 1, NEAR)]
         + [pltpu.VMEM((NEAR, COLS), F32)]
         + [pltpu.VMEM(out.shape, F32) for out in packed]
-        + [pltpu.VMEM((FEAT, COLS), F32), pltpu.SemaphoreType.DMA((9,)), pltpu.SemaphoreType.DMA((3,))],
+        + [pltpu.VMEM((FEAT, COLS), F32), pltpu.SemaphoreType.DMA((9,)), pltpu.SemaphoreType.DMA((4,))],
         in_specs=[hbm] * 9,
         out_specs=[hbm] * 3,
         vmem_limit_bytes=60 << 20,
@@ -437,7 +440,9 @@
     )
     from_left = lax.ppermute(right, "grp", up)
     from_right = lax.ppermute(left, "grp", down)
-    arrived = lax.all_to_all(send.reshape(PEERS * CHUNK, 1, 128), "grp", split_axis=0, concat_axis=0, tiled=True)
+    arrived = lax.all_to_all(
+        send.reshape(PEERS * CHUNK, 1, 128), "grp", split_axis=0, concat_axis=0, tiled=True
+    )
     mixed = call(
         mix_kernel,
         "mix",
@@ -486,7 +491,7 @@
             pltpu.VMEM((3, COLS, 128), F32),
             pltpu.VMEM((FEAT, RAD), F32),
             pltpu.VMEM((ROW, RAD), F32),
-            pltpu.VMEM((BLOCKS * 128, RAD), BF),
+            pltpu.VMEM((2, BLOCKS * 128, RAD), BF),
         ],
         in_specs=[scalar] + [whole] * 5,
     )(side, arrived.reshape(PEERS * CHUNK, 128), arrival_membership, weights, emit, shine)

time: 71.4 us -> 71.4 us (level)
  no operation moved by 1% of the time
where the time goes in v9:
time: 71.4 us; the launch traced here: 71.1 us
  starting transfers between devices  26.5 us (37%)
  blocking collectives  17.6 us (25%)
  waiting for transfers between devices  14.3 us (20%)
  Pallas kernels  11.2 us (16%)
  local copies, waits for them, and re-layouts  0.84 us (1%)
  between operations  0.76 us (1%)
    all_to_all x1, blocking collectives, per_device(): lax.all_to_all(back.reshape(PEERS * 2, 1, 128), 'grp', split_axis=0, conc...  17.6 us
    all_to_all x1, starting transfers between devices, per_device(): lax.all_to_all(send.reshape(PEERS * CHUNK, 1, 128), 'grp', split_axis=0,...  16.5 us
    ppermute x1, waiting for transfers between devices, per_device(): from_left = lax.ppermute(right, 'grp', up)  12.4 us
    ppermute x1, starting transfers between devices, per_device(): from_right = lax.ppermute(left, 'grp', down)  6.32 us
    pallas_call x1, Pallas kernels, per_device(): call(mix_kernel, 'mix', shape(LEV, SPECIES, COLS), [pltpu.VMEM((2, BODY,...  4.22 us
    pallas_call x1, Pallas kernels, per_device(): call(pack_kernel, 'pack', packed, [pltpu.VMEM(dims, F32) for dims in give...  2.8 us
    pallas_call x1, Pallas kernels, per_device(): call(first_kernel, 'first', (shape(DEEP, RAD), shape(DEEP, RAD), shape(DE...  1.62 us
    ppermute x1, starting transfers between devices, per_device(): lax.ppermute(opacity, 'sec', swap)  1.6 us
  transfers between devices with their start and end apart: 5, of which 3 were waited for; matrix products, arithmetic and copies ran while one was open for 0% of the time, Pallas kernels for 7%

profile of v9, /device:TPU:1, one launch (start us, length us, event | category | flops | bytes accessed | tf_op | source)
XLA Modules:
  0.0 71.1 jit_solution(3150673401099884500)
XLA Ops:
  0.6 0.0 copy-start.1
  0.6 0.0 copy-start.6
  0.7 0.0 copy-start.7
  0.7 2.8 %shard_map.140 = (f32[1152,128]{1,0:T(8,128)}, f32[208,256]{1,0:T(8,128)}, f32[208,256]{1,0:T(8,128)}) custom-call(f32[45,512]{1,0:T(8,128)} %refs_0_.1, f32[45,512]{1,0:T(8,128)} %refs_1_.1, f32[45,4,512]{2,1,0:T(4,128)} %bitcast.19, f32[1,512]{1,0:T(1,128)} %bitcast.24, f32[1,512]{1,0:T(1,128)} %bitcast.25, s32[1,512]{1,0:T(1,128)} %bitcast.26, ...), custom_call_target="tpu_custom_call" | custom-call | flops 2700000000 | bytes 262144 | tf_op jit(solution)/shard_map/pallas_call | solution.py:418
  3.5 0.0 copy-start.4
  3.5 0.0 copy-start.5
  3.5 0.0 copy-start
  3.5 0.0 copy-start.2
  3.5 0.0 copy-start.3
  3.5 16.5 %all-to-all-start = ((f32[1152,1,128]{2,1,0:T(1,128)}), f32[1152,1,128]{2,1,0:T(1,128)S(1)}, u32[]{:S(2)}, u32[]{:S(2)}) async-start(f32[1152,1,128]{2,1,0:T(1,128)} %bitcast.23), calls=%async_computation | async-start | bytes 1179648 | tf_op jit(solution)/shard_map/all_to_all | solution.py:443
  20.0 0.7 collective-permute-start
  20.7 6.3 %collective-permute-start.1 = (f32[208,256]{1,0:T(8,128)}, f32[208,256]{1,0:T(8,128)S(1)}, u32[]{:S(2)}, u32[]{:S(2)}) collective-permute-start(f32[208,256]{1,0:T(8,128)} %get-tuple-element.26), channel_id=1, source_target_pairs={{1,0},{2,1},{3,2},{4,3},{5,4},{6,5},{7,6},{8,7},{9,8},{10,9},{11,1... | collective-permute-start | bytes 638984 | tf_op jit(solution)/shard_map/ppermute | solution.py:442
  27.0 0.0 copy-done.1
  27.0 0.0 copy-done.6
  27.0 0.0 copy-done.7
  27.0 0.1 shard_map.142.own
  27.1 1.6 %collective-permute-start.2 = (f32[4,56,128]{2,1,0:T(8,128)S(1)}, f32[4,56,128]{2,1,0:T(8,128)S(1)}, u32[]{:S(2)}, u32[]{:S(2)}) collective-permute-start(f32[4,56,128]{2,1,0:T(8,128)S(1)} %shard_map.142.own), channel_id=1, source_target_pairs={{0,128},{128,0},{1,129},{129,1},{2,130},{130,2},{3,131},{131,3},{4... | collective-permute-start | bytes 344072 | tf_op jit(solution)/shard_map/ppermute | solution.py:475
  28.7 1.0 %collective-permute-done.2.other = f32[4,56,128]{2,1,0:T(8,128)S(1)} collective-permute-done((f32[4,56,128]{2,1,0:T(8,128)S(1)}, f32[4,56,128]{2,1,0:T(8,128)S(1)}, u32[]{:S(2)}, u32[]{:S(2)}) %collective-permute-start.2) | collective-permute-done | bytes 114720 | tf_op jit(solution)/shard_map/ppermute | solution.py:475
  29.6 0.0 copy-done.4
  29.7 0.0 copy-done.5
  29.7 0.8 %shard_map.143 = (bf16[5120,128]{1,0:T(8,128)(2,1)S(1)}, f32[112,128]{1,0:T(8,128)S(1)}, f32[112,128]{1,0:T(8,128)S(1)}, bf16[512,128]{1,0:T(8,128)(2,1)S(1)}, bf16[512,512]{1,0:T(8,128)(2,1)S(1)}) custom-call(s32[1]{0:T(128)} %bitcast.6.side, f32[4,56,128]{2,1,0:T(8,128)S(1)} %shard_map.142.own, f32[4,56,128]{2,1,0:T(8,128)S(1)} %collective-permute-done.2.other, ...), custom_call_target="tpu_custom_call" | custom-call | flops 700000000 | bytes 262144 | tf_op jit(solution)/shard_map/pallas_call | solution.py:463
  30.4 0.0 copy-start.8
  30.4 0.8 %copy-done.8 = bf16[512,512]{1,0:T(8,128)(2,1)} copy-done((bf16[512,512]{1,0:T(8,128)(2,1)}, bf16[512,512]{1,0:T(8,128)(2,1)S(1)}, u32[]{:S(2)}) %copy-start.8) | copy-done | bytes 524312
  31.2 12.4 %collective-permute-done.from_left = f32[208,256]{1,0:T(8,128)S(1)} collective-permute-done((f32[208,256]{1,0:T(8,128)}, f32[208,256]{1,0:T(8,128)S(1)}, u32[]{:S(2)}, u32[]{:S(2)}) %collective-permute-start) | collective-permute-done | bytes 213024 | tf_op jit(solution)/shard_map/ppermute | solution.py:441
  43.6 0.0 collective-permute-done.1.from_right
  43.6 0.0 copy-done
  43.6 0.0 copy-done.2
  43.6 0.0 copy-done.3
  43.6 4.2 %shard_map.141 = f32[45,4,512]{2,1,0:T(4,128)} custom-call(f32[45,4,512]{2,1,0:T(4,128)S(1)} %bitcast.20, s32[6,512]{1,0:T(8,128)S(1)} %copy-done.2, f32[6,512]{1,0:T(8,128)S(1)} %copy-done.3, f32[208,256]{1,0:T(8,128)S(1)} %collective-permute-done.from_left, f32[208,256]{1,0:T(8,128)S(1)} %collective-permute-done.1.from_right), custom_call_target="tpu_custom_call" | custom-call | flops 4200000000 | bytes 262144 | tf_op jit(solution)/shard_map/pallas_call | solution.py:446
  47.8 0.0 all-to-all-done
  47.8 1.6 %shard_map.144 = (f32[5120,128]{1,0:T(8,128)S(1)}, f32[5120,128]{1,0:T(8,128)S(1)}, f32[5120,128]{1,0:T(8,128)S(1)}, f32[48,128]{1,0:T(8,128)S(1)}, f32[360,128]{1,0:T(8,128)S(1)}, /*index=5*/f32[224,128]{1,0:T(8,128)S(1)}) custom-call(s32[1]{0:T(128)} %bitcast.6.side, f32[1152,128]{1,0:T(8,128)S(1)} %bitcast.16, s32[1,512]{1,0:T(1,128)S(1)} %copy-done.5, ...), custom_call_target="tpu_custom_call" | custom-call | flops 2000000000 | bytes 262144 | tf_op jit(solution)/shard_map/pallas_call | solution.py:479
  49.4 1.4 %collective-permute-start.3 = (f32[224,128]{1,0:T(8,128)S(1)}, f32[224,128]{1,0:T(8,128)S(1)}, u32[]{:S(2)}, u32[]{:S(2)}) collective-permute-start(f32[224,128]{1,0:T(8,128)S(1)} %get-tuple-element.37), channel_id=1, source_target_pairs={{0,128},{128,0},{1,129},{129,1},{2,130},{130,2},{3,131},{131,3},{4... | collective-permute-start | bytes 344072 | tf_op jit(solution)/shard_map/ppermute | solution.py:498
  50.9 1.0 %collective-permute-done.3.gotten = f32[224,128]{1,0:T(8,128)S(1)} collective-permute-done((f32[224,128]{1,0:T(8,128)S(1)}, f32[224,128]{1,0:T(8,128)S(1)}, u32[]{:S(2)}, u32[]{:S(2)}) %collective-permute-start.3) | collective-permute-done | bytes 114720 | tf_op jit(solution)/shard_map/ppermute | solution.py:498
  51.8 0.0 copy-start.9
  51.8 0.7 %shard_map.145 = f32[256,128]{1,0:T(8,128)S(1)} custom-call(s32[1]{0:T(128)} %bitcast.6.side, f32[224,128]{1,0:T(8,128)S(1)} %collective-permute-done.3.gotten, f32[5120,128]{1,0:T(8,128)S(1)} %get-tuple-element.38.trans, f32[5120,128]{1,0:T(8,128)S(1)} %get-tuple-element.39.glow, f32[5120,128]{1,0:T(8,128)S(1)} %get-tuple-element.40.passing, ...), custom_call_target="tpu_custom_call" | custom-call | flops 900000000 | bytes 262144 | tf_op jit(solution)/shard_map/pallas_call | solution.py:499
  52.6 17.6 %all_to_all.10 = f32[256,1,128]{2,1,0:T(1,128)S(1)} all-to-all(f32[256,1,128]{2,1,0:T(1,128)S(1)} %bitcast.17), channel_id=1, replica_groups=mesh['sec'=2,'grp'=128] {'grp'}, dimensions={0} | all-to-all | bytes 262144 | tf_op jit(solution)/shard_map/all_to_all | solution.py:506
  70.1 0.0 copy-done.9
  70.1 1.0 %shard_map.146 = f32[45,512]{1,0:T(8,128)} custom-call(f32[256,128]{1,0:T(8,128)S(1)} %bitcast.18, bf16[512,512]{1,0:T(8,128)(2,1)S(1)} %copy-done.9), custom_call_target="tpu_custom_call" | custom-call | flops 1000000000 | bytes 262144 | tf_op jit(solution)/shard_map/pallas_call | solution.py:509
Async XLA Ops:
  0.6 26.3 %copy-start.1 = (f32[4,56,90]{2,1,0:T(8,128)S(1)}, f32[4,56,90]{2,1,0:T(8,128)}, u32[]{:S(2)}) copy-start(f32[4,56,90]{2,1,0:T(8,128)} %opacity.1) | copy-start | bytes 241924
  0.6 26.3 %copy-start.6 = (f32[56]{0:T(128)S(1)}, f32[56]{0:T(128)}, u32[]{:S(2)}) copy-start(f32[56]{0:T(128)} %param.24) | copy-start | bytes 676
  0.7 26.3 %copy-start.7 = (f32[56]{0:T(128)S(1)}, f32[56]{0:T(128)}, u32[]{:S(2)}) copy-start(f32[56]{0:T(128)} %param.25) | copy-start | bytes 676
  3.5 26.2 %copy-start.4 = (s32[1,512]{1,0:T(1,128)S(1)}, s32[1,512]{1,0:T(1,128)}, u32[]{:S(2)}) copy-start(s32[1,512]{1,0:T(1,128)} %pos.1) | copy-start | bytes 6148
  3.5 26.2 %copy-start.5 = (s32[1,512]{1,0:T(1,128)S(1)}, s32[1,512]{1,0:T(1,128)}, u32[]{:S(2)}) copy-start(s32[1,512]{1,0:T(1,128)} %member.3) | copy-start | bytes 6148
  3.5 40.1 %copy-start = (f32[4,45,512]{2,0,1:T(4,128)S(1)}, f32[4,45,512]{2,0,1:T(4,128)}, u32[]{:S(2)}) copy-start(f32[4,45,512]{2,0,1:T(4,128)} %param.15) | copy-start | bytes 1105924
  3.5 40.1 %copy-start.2 = (s32[6,512]{1,0:T(8,128)S(1)}, s32[6,512]{1,0:T(8,128)}, u32[]{:S(2)}) copy-start(s32[6,512]{1,0:T(8,128)} %adj.1) | copy-start | bytes 36868
  3.5 40.1 %copy-start.3 = (f32[6,512]{1,0:T(8,128)S(1)}, f32[6,512]{1,0:T(8,128)}, u32[]{:S(2)}) copy-start(f32[6,512]{1,0:T(8,128)} %coef.1) | copy-start | bytes 36868
  3.5 44.3 %all-to-all-start = ((f32[1152,1,128]{2,1,0:T(1,128)}), f32[1152,1,128]{2,1,0:T(1,128)S(1)}, u32[]{:S(2)}, u32[]{:S(2)}) async-start(f32[1152,1,128]{2,1,0:T(1,128)} %bitcast.23), calls=%async_computation | async-start | bytes 1179648 | tf_op jit(solution)/shard_map/all_to_all | solution.py:443
  20.0 23.6 %collective-permute-start = (f32[208,256]{1,0:T(8,128)}, f32[208,256]{1,0:T(8,128)S(1)}, u32[]{:S(2)}, u32[]{:S(2)}) collective-permute-start(f32[208,256]{1,0:T(8,128)} %get-tuple-element.25), channel_id=1, source_target_pairs={{0,1},{1,2},{2,3},{3,4},{4,5},{5,6},{6,7},{7,8},{8,9},{9,10},{10,1... | collective-permute-start | bytes 638984 | tf_op jit(solution)/shard_map/ppermute | solution.py:441
  20.7 22.9 %collective-permute-start.1 = (f32[208,256]{1,0:T(8,128)}, f32[208,256]{1,0:T(8,128)S(1)}, u32[]{:S(2)}, u32[]{:S(2)}) collective-permute-start(f32[208,256]{1,0:T(8,128)} %get-tuple-element.26), channel_id=1, source_target_pairs={{1,0},{2,1},{3,2},{4,3},{5,4},{6,5},{7,6},{8,7},{9,8},{10,9},{11,1... | collective-permute-start | bytes 638984 | tf_op jit(solution)/shard_map/ppermute | solution.py:442
  27.1 2.6 %collective-permute-start.2 = (f32[4,56,128]{2,1,0:T(8,128)S(1)}, f32[4,56,128]{2,1,0:T(8,128)S(1)}, u32[]{:S(2)}, u32[]{:S(2)}) collective-permute-start(f32[4,56,128]{2,1,0:T(8,128)S(1)} %shard_map.142.own), channel_id=1, source_target_pairs={{0,128},{128,0},{1,129},{129,1},{2,130},{130,2},{3,131},{131,3},{4... | collective-permute-start | bytes 344072 | tf_op jit(solution)/shard_map/ppermute | solution.py:475
  30.4 0.8 %copy-start.8 = (bf16[512,512]{1,0:T(8,128)(2,1)}, bf16[512,512]{1,0:T(8,128)(2,1)S(1)}, u32[]{:S(2)}) copy-start(bf16[512,512]{1,0:T(8,128)(2,1)S(1)} %get-tuple-element.44.placing) | copy-start | bytes 1572868
  49.4 2.4 %collective-permute-start.3 = (f32[224,128]{1,0:T(8,128)S(1)}, f32[224,128]{1,0:T(8,128)S(1)}, u32[]{:S(2)}, u32[]{:S(2)}) collective-permute-start(f32[224,128]{1,0:T(8,128)S(1)} %get-tuple-element.37), channel_id=1, source_target_pairs={{0,128},{128,0},{1,129},{129,1},{2,130},{130,2},{3,131},{131,3},{4... | collective-permute-start | bytes 344072 | tf_op jit(solution)/shard_map/ppermute | solution.py:498
  51.8 18.3 %copy-start.9 = (bf16[512,512]{1,0:T(8,128)(2,1)S(1)}, bf16[512,512]{1,0:T(8,128)(2,1)}, u32[]{:S(2)}) copy-start(bf16[512,512]{1,0:T(8,128)(2,1)} %copy-done.8) | copy-start | bytes 1572868

commit v10 on v9

--- a/solution.py
+++ b/solution.py
@@ -443,17 +443,6 @@
     arrived = lax.all_to_all(
         send.reshape(PEERS * CHUNK, 1, 128), "grp", split_axis=0, concat_axis=0, tiled=True
     )
-    mixed = call(
-        mix_kernel,
-        "mix",
-        shape(LEV, SPECIES, COLS),
-        [
-            pltpu.VMEM((2, BODY, WIDE), BF),
-            pltpu.VMEM((2, BODY, WIDE), BF),
-            pltpu.VMEM((2, 2, 7, 256, 128), BF),
-            pltpu.VMEM((BODY, COLS), F32),
-        ],
-    )(tracers, adjacency_table, blending_coefficient, from_left, from_right)
     side = lax.axis_index("sec").astype(jnp.int32)[None]
     opacity = call(join_kernel, "join", shape(SPECIES, GH, 128), [])(
         opacity_table, emission_share[None], sunshine_share[None]
@@ -473,8 +462,8 @@
         [pltpu.VMEM((2, SPECIES, GH, 128), F32)],
         in_specs=[scalar] + [whole] * 4,
     )(side, opacity, lax.ppermute(opacity, "sec", swap), arrival_membership, dispatch_position)
-    arrived, mixed, weights, emit, shine, spread, placing, side = lax.optimization_barrier(
-        (arrived, mixed, weights, emit, shine, spread, placing, side)
+    arrived, weights, emit, shine, spread, placing, side = lax.optimization_barrier(
+        (arrived, weights, emit, shine, spread, placing, side)
     )
     trans, glow, passing, thick, sums, edge = call(
         first_kernel,
@@ -506,6 +495,18 @@
     returned = lax.all_to_all(
         back.reshape(PEERS * 2, 1, 128), "grp", split_axis=0, concat_axis=0, tiled=True
     ).reshape(PEERS * 2, 128)
+    mixed = call(
+        mix_kernel,
+        "mix",
+        shape(LEV, SPECIES, COLS),
+        [
+            pltpu.VMEM((2, BODY, WIDE), BF),
+            pltpu.VMEM((2, BODY, WIDE), BF),
+            pltpu.VMEM((2, 2, 7, 256, 128), BF),
+            pltpu.VMEM((BODY, COLS), F32),
+        ],
+    )(tracers, adjacency_table, blending_coefficient, from_left, from_right)
+    returned, mixed = lax.optimization_barrier((returned, mixed))
     heating = call(unplace_kernel, "unplace", shape(LEV, COLS), [])(returned, placing)
     return (heating, jnp.transpose(mixed, (1, 0, 2)))
 

time: 71.4 us -> 64.6 us (0.905)
  blocking collectives: 17.6 us -> 0 us
  starting transfers between devices: 26.5 us -> 35.2 us
  waiting for transfers between devices: 14.3 us -> 16.4 us
  local copies, waits for them, and re-layouts: 0.84 us -> 0.04 us
    all_to_all x1 -> x0, blocking collectives: 17.6 us -> none  [per_device(): lax.all_to_all(back.reshape(PEERS * 2, 1, 128), 'grp', split_axis=0, conc...]
    ppermute x1, waiting for transfers between devices: 12.4 us -> 0.01 us  [per_device(): from_left = lax.ppermute(right, 'grp', up)]
    all_to_all x1, waiting for transfers between devices: 0.01 us -> 9.06 us  [per_device(): lax.all_to_all(send.reshape(PEERS * CHUNK, 1, 128), 'grp', split_axis=0,...]
    all_to_all x0 -> x1, starting transfers between devices: none -> 6.47 us  [per_device(): lax.all_to_all(back.reshape(PEERS * 2, 1, 128), 'grp', split_axis=0, conc...]
    all_to_all x0 -> x1, waiting for transfers between devices: none -> 6.39 us  [per_device(): lax.all_to_all(back.reshape(PEERS * 2, 1, 128), 'grp', split_axis=0, conc...]
    ppermute x1, starting transfers between devices: 1.42 us -> 4.18 us  [per_device(): gotten = lax.ppermute(edge, 'sec', swap)]
    ppermute x1, waiting for transfers between devices: 0.97 us -> 0.01 us  [per_device(): lax.ppermute(opacity, 'sec', swap)]
    unnamed x20 -> x18, local copies, waits for them, and re-layouts: 0.84 us -> 0.04 us
  transfers between devices with their start and end apart: 5 -> 6, of which waited for: 3 -> 3; matrix products, arithmetic and copies ran while one was open for 0% -> 0% of each run, Pallas kernels for 7% -> 13%
where the time goes in v10:
time: 64.6 us; the launch traced here: 64.4 us
  starting transfers between devices  35.2 us (54%)
  waiting for transfers between devices  16.4 us (25%)
  Pallas kernels  11.9 us (18%)
  between operations  0.8 us (1%)
    all_to_all x1, starting transfers between devices, per_device(): lax.all_to_all(send.reshape(PEERS * CHUNK, 1, 128), 'grp', split_axis=0,...  16.5 us
    all_to_all x1, waiting for transfers between devices, per_device(): lax.all_to_all(send.reshape(PEERS * CHUNK, 1, 128), 'grp', split_axis=0,...  9.06 us
    all_to_all x1, starting transfers between devices, per_device(): lax.all_to_all(back.reshape(PEERS * 2, 1, 128), 'grp', split_axis=0, conc...  6.47 us
    all_to_all x1, waiting for transfers between devices, per_device(): lax.all_to_all(back.reshape(PEERS * 2, 1, 128), 'grp', split_axis=0, conc...  6.39 us
    ppermute x1, starting transfers between devices, per_device(): from_right = lax.ppermute(left, 'grp', down)  6.18 us
    pallas_call x1, Pallas kernels, per_device(): call(mix_kernel, 'mix', shape(LEV, SPECIES, COLS), [pltpu.VMEM((2, BODY,...  4.22 us
    ppermute x1, starting transfers between devices, per_device(): gotten = lax.ppermute(edge, 'sec', swap)  4.18 us
    pallas_call x1, Pallas kernels, per_device(): call(pack_kernel, 'pack', packed, [pltpu.VMEM(dims, F32) for dims in give...  2.78 us
  transfers between devices with their start and end apart: 6, of which 3 were waited for; matrix products, arithmetic and copies ran while one was open for 0% of the time, Pallas kernels for 13%

profile of v10, /device:TPU:1, one launch (start us, length us, event | category | flops | bytes accessed | tf_op | source)
XLA Modules:
  0.0 64.4 jit_solution(14479068030224006947)
XLA Ops:
  0.6 0.0 copy-start.1
  0.6 0.0 copy-start.6
  0.7 0.0 copy-start.7
  0.7 2.8 %shard_map.140 = (f32[1152,128]{1,0:T(8,128)}, f32[208,256]{1,0:T(8,128)}, f32[208,256]{1,0:T(8,128)}) custom-call(f32[45,512]{1,0:T(8,128)} %refs_0_.1, f32[45,512]{1,0:T(8,128)} %refs_1_.1, f32[45,4,512]{2,1,0:T(4,128)} %bitcast.18, f32[1,512]{1,0:T(1,128)} %bitcast.23, f32[1,512]{1,0:T(1,128)} %bitcast.24, s32[1,512]{1,0:T(1,128)} %bitcast.25, ...), custom_call_target="tpu_custom_call" | custom-call | flops 2700000000 | bytes 262144 | tf_op jit(solution)/shard_map/pallas_call | solution.py:418
  3.4 0.0 copy-start.8
  3.5 0.0 copy-start.4
  3.5 0.0 copy-start.5
  3.5 16.5 %all-to-all-start = ((f32[1152,1,128]{2,1,0:T(1,128)}), f32[1152,1,128]{2,1,0:T(1,128)S(1)}, u32[]{:S(2)}, u32[]{:S(2)}) async-start(f32[1152,1,128]{2,1,0:T(1,128)} %bitcast.22), calls=%async_computation | async-start | bytes 1179648 | tf_op jit(solution)/shard_map/all_to_all | solution.py:443
  20.0 0.0 copy-done.1
  20.0 0.0 copy-done.6
  20.0 0.0 copy-done.7
  20.0 0.1 shard_map.141.own
  20.1 1.0 %collective-permute-start = (f32[4,56,128]{2,1,0:T(8,128)S(1)}, f32[4,56,128]{2,1,0:T(8,128)S(1)}, u32[]{:S(2)}, u32[]{:S(2)}) collective-permute-start(f32[4,56,128]{2,1,0:T(8,128)S(1)} %shard_map.141.own), channel_id=1, source_target_pairs={{0,128},{128,0},{1,129},{129,1},{2,130},{130,2},{3,131},{131,3},{4... | collective-permute-start | bytes 344072 | tf_op jit(solution)/shard_map/ppermute | solution.py:464
  21.1 0.9 %collective-permute-start.2 = (f32[208,256]{1,0:T(8,128)}, f32[208,256]{1,0:T(8,128)S(1)}, u32[]{:S(2)}, u32[]{:S(2)}) collective-permute-start(f32[208,256]{1,0:T(8,128)} %get-tuple-element.43), channel_id=1, source_target_pairs={{0,1},{1,2},{2,3},{3,4},{4,5},{5,6},{6,7},{7,8},{8,9},{9,10},{10,1... | collective-permute-start | bytes 638984 | tf_op jit(solution)/shard_map/ppermute | solution.py:441
  22.0 0.0 copy-done.8
  22.0 6.2 %collective-permute-start.3 = (f32[208,256]{1,0:T(8,128)S(1)}, f32[208,256]{1,0:T(8,128)S(1)}, u32[]{:S(2)}, u32[]{:S(2)}) collective-permute-start(f32[208,256]{1,0:T(8,128)S(1)} %copy-done.8), channel_id=1, source_target_pairs={{1,0},{2,1},{3,2},{4,3},{5,4},{6,5},{7,6},{8,7},{9,8},{10,9},{11,1... | collective-permute-start | bytes 638984 | tf_op jit(solution)/shard_map/ppermute | solution.py:442
  28.2 0.0 collective-permute-done.other
  28.2 0.0 copy-done.4
  28.2 0.0 copy-done.5
  28.2 0.8 %shard_map.142 = (bf16[5120,128]{1,0:T(8,128)(2,1)S(1)}, f32[112,128]{1,0:T(8,128)S(1)}, f32[112,128]{1,0:T(8,128)S(1)}, bf16[512,128]{1,0:T(8,128)(2,1)S(1)}, bf16[512,512]{1,0:T(8,128)(2,1)S(1)}) custom-call(s32[1]{0:T(128)} %bitcast.6.side, f32[4,56,128]{2,1,0:T(8,128)S(1)} %shard_map.141.own, f32[4,56,128]{2,1,0:T(8,128)S(1)} %collective-permute-done.other, ...), custom_call_target="tpu_custom_call" | custom-call | flops 700000000 | bytes 262144 | tf_op jit(solution)/shard_map/pallas_call | solution.py:452
  28.9 9.1 %all-to-all-done = f32[1152,1,128]{2,1,0:T(1,128)S(1)} async-done(((f32[1152,1,128]{2,1,0:T(1,128)}), f32[1152,1,128]{2,1,0:T(1,128)S(1)}, u32[]{:S(2)}, u32[]{:S(2)}) %all-to-all-start) | async-done | bytes 589856 | tf_op jit(solution)/shard_map/all_to_all | solution.py:443
  38.0 1.7 %shard_map.143 = (f32[5120,128]{1,0:T(8,128)S(1)}, f32[5120,128]{1,0:T(8,128)S(1)}, f32[5120,128]{1,0:T(8,128)S(1)}, f32[48,128]{1,0:T(8,128)S(1)}, f32[360,128]{1,0:T(8,128)S(1)}, /*index=5*/f32[224,128]{1,0:T(8,128)S(1)}) custom-call(s32[1]{0:T(128)} %bitcast.6.side, f32[1152,128]{1,0:T(8,128)S(1)} %bitcast.16, s32[1,512]{1,0:T(1,128)S(1)} %copy-done.5, ...), custom_call_target="tpu_custom_call" | custom-call | flops 2000000000 | bytes 262144 | tf_op jit(solution)/shard_map/pallas_call | solution.py:468
  39.7 4.2 %collective-permute-start.1 = (f32[224,128]{1,0:T(8,128)S(1)}, f32[224,128]{1,0:T(8,128)S(1)}, u32[]{:S(2)}, u32[]{:S(2)}) collective-permute-start(f32[224,128]{1,0:T(8,128)S(1)} %get-tuple-element.36), channel_id=1, source_target_pairs={{0,128},{128,0},{1,129},{129,1},{2,130},{130,2},{3,131},{131,3},{4... | collective-permute-start | bytes 344072 | tf_op jit(solution)/shard_map/ppermute | solution.py:487
  43.9 1.0 %collective-permute-done.1.gotten = f32[224,128]{1,0:T(8,128)S(1)} collective-permute-done((f32[224,128]{1,0:T(8,128)S(1)}, f32[224,128]{1,0:T(8,128)S(1)}, u32[]{:S(2)}, u32[]{:S(2)}) %collective-permute-start.1) | collective-permute-done | bytes 114720 | tf_op jit(solution)/shard_map/ppermute | solution.py:487
  44.8 0.0 copy-start
  44.8 0.0 copy-start.2
  44.8 0.0 copy-start.3
  44.8 1.4 %shard_map.144 = f32[256,128]{1,0:T(8,128)} custom-call(s32[1]{0:T(128)} %bitcast.6.side, f32[224,128]{1,0:T(8,128)S(1)} %collective-permute-done.1.gotten, f32[5120,128]{1,0:T(8,128)S(1)} %get-tuple-element.37.trans, f32[5120,128]{1,0:T(8,128)S(1)} %get-tuple-element.38.glow, f32[5120,128]{1,0:T(8,128)S(1)} %get-tuple-element.39.passing, ...), custom_call_target="tpu_custom_call" | custom-call | flops 900000000 | bytes 262144 | tf_op jit(solution)/shard_map/pallas_call | solution.py:488
  46.2 6.5 %all-to-all-start.1 = ((f32[256,1,128]{2,1,0:T(1,128)}), f32[256,1,128]{2,1,0:T(1,128)S(1)}, u32[]{:S(2)}, u32[]{:S(2)}) async-start(f32[256,1,128]{2,1,0:T(1,128)} %bitcast.11), calls=%async_computation.1 | async-start | bytes 262144 | tf_op jit(solution)/shard_map/all_to_all | solution.py:495
  52.7 0.0 collective-permute-done.2.from_left
  52.7 0.0 collective-permute-done.3.from_right
  52.7 0.0 copy-done
  52.7 0.0 copy-done.2
  52.7 0.0 copy-done.3
  52.7 4.2 %shard_map.145 = f32[45,4,512]{2,1,0:T(4,128)} custom-call(f32[45,4,512]{2,1,0:T(4,128)S(1)} %bitcast.19, s32[6,512]{1,0:T(8,128)S(1)} %copy-done.2, f32[6,512]{1,0:T(8,128)S(1)} %copy-done.3, f32[208,256]{1,0:T(8,128)S(1)} %collective-permute-done.2.from_left, f32[208,256]{1,0:T(8,128)S(1)} %collective-permute-done.3.from_right), custom_call_target="tpu_custom_call" | custom-call | flops 4200000000 | bytes 262144 | tf_op jit(solution)/shard_map/pallas_call | solution.py:498
  57.0 6.4 %all-to-all-done.1 = f32[256,1,128]{2,1,0:T(1,128)S(1)} async-done(((f32[256,1,128]{2,1,0:T(1,128)}), f32[256,1,128]{2,1,0:T(1,128)S(1)}, u32[]{:S(2)}, u32[]{:S(2)}) %all-to-all-start.1) | async-done | bytes 131104 | tf_op jit(solution)/shard_map/all_to_all | solution.py:495
  63.4 1.0 %shard_map.146 = f32[45,512]{1,0:T(8,128)} custom-call(f32[256,128]{1,0:T(8,128)S(1)} %bitcast.17, bf16[512,512]{1,0:T(8,128)(2,1)S(1)} %get-tuple-element.46.placing), custom_call_target="tpu_custom_call" | custom-call | flops 1000000000 | bytes 262144 | tf_op jit(solution)/shard_map/pallas_call | solution.py:510
Async XLA Ops:
  0.6 19.3 %copy-start.1 = (f32[4,56,90]{2,1,0:T(8,128)S(1)}, f32[4,56,90]{2,1,0:T(8,128)}, u32[]{:S(2)}) copy-start(f32[4,56,90]{2,1,0:T(8,128)} %opacity.1) | copy-start | bytes 241924
  0.6 19.3 %copy-start.6 = (f32[56]{0:T(128)S(1)}, f32[56]{0:T(128)}, u32[]{:S(2)}) copy-start(f32[56]{0:T(128)} %param.24) | copy-start | bytes 676
  0.7 19.3 %copy-start.7 = (f32[56]{0:T(128)S(1)}, f32[56]{0:T(128)}, u32[]{:S(2)}) copy-start(f32[56]{0:T(128)} %param.25) | copy-start | bytes 676
  3.4 18.5 %copy-start.8 = (f32[208,256]{1,0:T(8,128)S(1)}, f32[208,256]{1,0:T(8,128)}, u32[]{:S(2)}) copy-start(f32[208,256]{1,0:T(8,128)} %get-tuple-element.44) | copy-start | bytes 638980
  3.5 24.7 %copy-start.4 = (s32[1,512]{1,0:T(1,128)S(1)}, s32[1,512]{1,0:T(1,128)}, u32[]{:S(2)}) copy-start(s32[1,512]{1,0:T(1,128)} %pos.1) | copy-start | bytes 6148
  3.5 24.7 %copy-start.5 = (s32[1,512]{1,0:T(1,128)S(1)}, s32[1,512]{1,0:T(1,128)}, u32[]{:S(2)}) copy-start(s32[1,512]{1,0:T(1,128)} %member.3) | copy-start | bytes 6148
  3.5 34.5 %all-to-all-start = ((f32[1152,1,128]{2,1,0:T(1,128)}), f32[1152,1,128]{2,1,0:T(1,128)S(1)}, u32[]{:S(2)}, u32[]{:S(2)}) async-start(f32[1152,1,128]{2,1,0:T(1,128)} %bitcast.22), calls=%async_computation | async-start | bytes 1179648 | tf_op jit(solution)/shard_map/all_to_all | solution.py:443
  20.1 8.1 %collective-permute-start = (f32[4,56,128]{2,1,0:T(8,128)S(1)}, f32[4,56,128]{2,1,0:T(8,128)S(1)}, u32[]{:S(2)}, u32[]{:S(2)}) collective-permute-start(f32[4,56,128]{2,1,0:T(8,128)S(1)} %shard_map.141.own), channel_id=1, source_target_pairs={{0,128},{128,0},{1,129},{129,1},{2,130},{130,2},{3,131},{131,3},{4... | collective-permute-start | bytes 344072 | tf_op jit(solution)/shard_map/ppermute | solution.py:464
  21.1 31.6 %collective-permute-start.2 = (f32[208,256]{1,0:T(8,128)}, f32[208,256]{1,0:T(8,128)S(1)}, u32[]{:S(2)}, u32[]{:S(2)}) collective-permute-start(f32[208,256]{1,0:T(8,128)} %get-tuple-element.43), channel_id=1, source_target_pairs={{0,1},{1,2},{2,3},{3,4},{4,5},{5,6},{6,7},{7,8},{8,9},{9,10},{10,1... | collective-permute-start | bytes 638984 | tf_op jit(solution)/shard_map/ppermute | solution.py:441
  22.0 30.7 %collective-permute-start.3 = (f32[208,256]{1,0:T(8,128)S(1)}, f32[208,256]{1,0:T(8,128)S(1)}, u32[]{:S(2)}, u32[]{:S(2)}) collective-permute-start(f32[208,256]{1,0:T(8,128)S(1)} %copy-done.8), channel_id=1, source_target_pairs={{1,0},{2,1},{3,2},{4,3},{5,4},{6,5},{7,6},{8,7},{9,8},{10,9},{11,1... | collective-permute-start | bytes 638984 | tf_op jit(solution)/shard_map/ppermute | solution.py:442
  39.7 5.1 %collective-permute-start.1 = (f32[224,128]{1,0:T(8,128)S(1)}, f32[224,128]{1,0:T(8,128)S(1)}, u32[]{:S(2)}, u32[]{:S(2)}) collective-permute-start(f32[224,128]{1,0:T(8,128)S(1)} %get-tuple-element.36), channel_id=1, source_target_pairs={{0,128},{128,0},{1,129},{129,1},{2,130},{130,2},{3,131},{131,3},{4... | collective-permute-start | bytes 344072 | tf_op jit(solution)/shard_map/ppermute | solution.py:487
  44.8 7.9 %copy-start = (f32[4,45,512]{2,0,1:T(4,128)S(1)}, f32[4,45,512]{2,0,1:T(4,128)}, u32[]{:S(2)}) copy-start(f32[4,45,512]{2,0,1:T(4,128)} %param.15) | copy-start | bytes 1105924
  44.8 7.9 %copy-start.2 = (s32[6,512]{1,0:T(8,128)S(1)}, s32[6,512]{1,0:T(8,128)}, u32[]{:S(2)}) copy-start(s32[6,512]{1,0:T(8,128)} %adj.1) | copy-start | bytes 36868
  44.8 7.9 %copy-start.3 = (f32[6,512]{1,0:T(8,128)S(1)}, f32[6,512]{1,0:T(8,128)}, u32[]{:S(2)}) copy-start(f32[6,512]{1,0:T(8,128)} %coef.1) | copy-start | bytes 36868
  46.2 17.1 %all-to-all-start.1 = ((f32[256,1,128]{2,1,0:T(1,128)}), f32[256,1,128]{2,1,0:T(1,128)S(1)}, u32[]{:S(2)}, u32[]{:S(2)}) async-start(f32[256,1,128]{2,1,0:T(1,128)} %bitcast.11), calls=%async_computation.1 | async-start | bytes 262144 | tf_op jit(solution)/shard_map/all_to_all | solution.py:495

commit v11 on v10

--- a/solution.py
+++ b/solution.py
@@ -62,32 +62,23 @@
 
 
 def pack_kernel(*refs):
-    sources, outs, scratch = refs[:9], refs[9:12], refs[12:]
-    temp, thick, tracers, ground, sun, day, pos, adj, coef = scratch[:9]
-    send, right, left, bundle, sems, done = scratch[9:]
+    sources, out, scratch = refs[:7], refs[7], refs[8:]
+    temp, thick, tracers, ground, sun, day, pos = scratch[:7]
+    send, bundle, sems, done = scratch[7:]
     copies = [pltpu.make_async_copy(a, b, sems.at[i]) for i, (a, b) in enumerate(zip(sources, scratch))]
-    for i in (6, 7, 8, 2, 0, 1, 3, 4, 5):
+    for i in (6, 2, 0, 1, 3, 4, 5):
         copies[i].start()
     middle = PEERS * CHUNK // 2
-    pairs = [(send.at[0:middle, :], outs[0].at[0:middle, :]), (right, outs[1]), (left, outs[2])]
-    pairs.append((send.at[middle : 2 * middle, :], outs[0].at[middle : 2 * middle, :]))
-    stores = [pltpu.make_async_copy(a, b, done.at[i]) for i, (a, b) in enumerate(pairs)]
+    halves = [slice(0, middle), slice(middle, 2 * middle)]
+    stores = [pltpu.make_async_copy(send.at[h, :], out.at[h, :], done.at[i]) for i, h in enumerate(halves)]
     bundle[ROW + LEV : BASE, :] = jnp.zeros((ROW - LEV, COLS), F32)
     spare = BASE + LEV * SPECIES
     bundle[spare:FEAT, :] = jnp.zeros((FEAT - spare, COLS), F32)
-    for i in (6, 7, 8):
-        copies[i].wait()
+    copies[6].wait()
     placing = slot_matrix(pos[...])
-    both = mixing_table(adj, coef)
-    right[BODY : BODY + 16, :] = both[:, COLS - REACH :]
-    left[BODY : BODY + 16, :] = both[:, :REACH]
     copies[2].wait()
     for l in range(LEV):
         bundle[BASE + SPECIES * l : BASE + SPECIES * (l + 1), :] = tracers[l]
-    right[0:BODY, :] = bundle[BASE:FEAT, COLS - REACH :]
-    left[0:BODY, :] = bundle[BASE:FEAT, :REACH]
-    for i in (1, 2):
-        stores[i].start()
     for i in (0, 1, 3, 4, 5):
         copies[i].wait()
     bundle[0:LEV, :] = temp[...]
@@ -107,10 +98,21 @@
         send[pl.ds(2 * m + 1, PEERS, CHUNK), :] = block[128:256, :].T
         tails.append(block[256:288, :])
     send[pl.ds(CHUNK - 1, PEERS, CHUNK), :] = jnp.concatenate(tails, axis=0).T
-    stores[0].start()
-    stores[3].start()
+    for store in stores:
+        store.start()
     for store in stores:
         store.wait()
+
+
+def edge_kernel(tracers, adj, coef, right, left):
+    both = mixing_table(adj, coef)
+    right[BODY : BODY + 16, :] = both[:, COLS - REACH :]
+    left[BODY : BODY + 16, :] = both[:, :REACH]
+    spare = LEV * SPECIES
+    for side, first in ((right, COLS - REACH), (left, 0)):
+        side[spare:BODY, :] = jnp.zeros((BODY - spare, REACH), F32)
+        for l in range(LEV):
+            side[SPECIES * l : SPECIES * (l + 1), :] = tracers[l, :, first : first + REACH]
 
 
 def join_kernel(opacity, emission, sunshine, joined):
@@ -376,7 +378,7 @@
     return jax.ShapeDtypeStruct(dims, F32)
 
 
-LENGTH = {"pack": 27, "join": 5, "weight": 7, "mix": 42, "first": 20, "second": 9, "unplace": 10}
+LENGTH = {"pack": 27, "edges": 4, "join": 5, "weight": 30, "mix": 42, "first": 20, "second": 9, "unplace": 10}
 
 
 def call(kernel, name, out_shape, scratch, vmem_limit_bytes=16 << 20, **specs):
@@ -413,19 +415,18 @@
     tracers = jnp.transpose(absorber_amounts, (1, 0, 2))
 
     hbm = pl.BlockSpec(memory_space=pltpu.HBM)
-    packed = (shape(PEERS * CHUNK, 128), shape(halo_rows, REACH), shape(halo_rows, REACH))
+    packed = shape(PEERS * CHUNK, 128)
     given = ((LEV, COLS), (LEV, COLS), (LEV, SPECIES, COLS), (1, COLS), (1, COLS))
-    send, right, left = call(
+    send = call(
         pack_kernel,
         "pack",
         packed,
         [pltpu.VMEM(dims, F32) for dims in given]
-        + [pltpu.VMEM((rows, COLS), jnp.int32) for rows in (1, 1, NEAR)]
-        + [pltpu.VMEM((NEAR, COLS), F32)]
-        + [pltpu.VMEM(out.shape, F32) for out in packed]
-        + [pltpu.VMEM((FEAT, COLS), F32), pltpu.SemaphoreType.DMA((9,)), pltpu.SemaphoreType.DMA((4,))],
-        in_specs=[hbm] * 9,
-        out_specs=[hbm] * 3,
+        + [pltpu.VMEM((1, COLS), jnp.int32)] * 2
+        + [pltpu.VMEM(packed.shape, F32)]
+        + [pltpu.VMEM((FEAT, COLS), F32), pltpu.SemaphoreType.DMA((7,)), pltpu.SemaphoreType.DMA((2,))],
+        in_specs=[hbm] * 7,
+        out_specs=hbm,
         vmem_limit_bytes=60 << 20,
     )(
         stratum_warmth_anomaly,
@@ -435,14 +436,13 @@
         sun_elevation_factor[None],
         daytime_mask[None],
         dispatch_position,
-        adjacency_table,
-        blending_coefficient,
+    )
+    right, left = call(edge_kernel, "edges", (shape(halo_rows, REACH), shape(halo_rows, REACH)), [])(
+        tracers, adjacency_table, blending_coefficient
     )
     from_left = lax.ppermute(right, "grp", up)
     from_right = lax.ppermute(left, "grp", down)
-    arrived = lax.all_to_all(
-        send.reshape(PEERS * CHUNK, 1, 128), "grp", split_axis=0, concat_axis=0, tiled=True
-    )
+    arrived = lax.all_to_all(send.reshape(PEERS * CHUNK, 1, 128), "grp", split_axis=0, concat_axis=0, tiled=True)
     side = lax.axis_index("sec").astype(jnp.int32)[None]
     opacity = call(join_kernel, "join", shape(SPECIES, GH, 128), [])(
         opacity_table, emission_share[None], sunshine_share[None]

time: 64.6 us -> 65.9 us (1.020)
  local copies, waits for them, and re-layouts: 0.04 us -> 2.44 us
  waiting for transfers between devices: 16.4 us -> 15.1 us
    unnamed x18 -> x20, local copies, waits for them, and re-layouts: 0.04 us -> 2.44 us
    all_to_all x1, waiting for transfers between devices: 9.06 us -> 7.76 us  [per_device(): lax.all_to_all(send.reshape(PEERS * CHUNK, 1, 128), 'grp', split_axis=0,...]
where the time goes in v11:
time: 65.9 us; the launch traced here: 65.6 us
  starting transfers between devices  35.4 us (54%)
  waiting for transfers between devices  15.1 us (23%)
  Pallas kernels  11.9 us (18%)
  local copies, waits for them, and re-layouts  2.44 us (4%)
  between operations  0.8 us (1%)
    all_to_all x1, starting transfers between devices, per_device(): lax.all_to_all(send.reshape(PEERS * CHUNK, 1, 128), 'grp', split_axis=0,...  16.5 us
    all_to_all x1, waiting for transfers between devices, per_device(): lax.all_to_all(send.reshape(PEERS * CHUNK, 1, 128), 'grp', split_axis=0,...  7.76 us
    all_to_all x1, starting transfers between devices, per_device(): lax.all_to_all(back.reshape(PEERS * 2, 1, 128), 'grp', split_axis=0, conc...  6.48 us
    all_to_all x1, waiting for transfers between devices, per_device(): lax.all_to_all(back.reshape(PEERS * 2, 1, 128), 'grp', split_axis=0, conc...  6.39 us
    ppermute x1, starting transfers between devices, per_device(): from_right = lax.ppermute(left, 'grp', down)  6.27 us
    pallas_call x1, Pallas kernels, per_device(): call(mix_kernel, 'mix', shape(LEV, SPECIES, COLS), [pltpu.VMEM((2, BODY,...  4.22 us
    ppermute x1, starting transfers between devices, per_device(): gotten = lax.ppermute(edge, 'sec', swap)  4.17 us
    pallas_call x1, Pallas kernels, per_device(): call(pack_kernel, 'pack', packed, [pltpu.VMEM(dims, F32) for dims in give...  2.69 us
  transfers between devices with their start and end apart: 6, of which 3 were waited for; matrix products, arithmetic and copies ran while one was open for 0% of the time, Pallas kernels for 13%

profile of v11, /device:TPU:1, one launch (start us, length us, event | category | flops | bytes accessed | tf_op | source)
XLA Modules:
  0.0 65.6 jit_solution(13533133334515659540)
XLA Ops:
  0.6 0.0 copy-start.1
  0.6 0.0 copy-start.6
  0.7 0.0 copy-start.7
  0.7 2.7 %shard_map.140 = f32[1152,128]{1,0:T(8,128)} custom-call(f32[45,512]{1,0:T(8,128)} %refs_0_.1, f32[45,512]{1,0:T(8,128)} %refs_1_.1, f32[45,4,512]{2,1,0:T(4,128)} %bitcast.18, f32[1,512]{1,0:T(1,128)} %bitcast.24, f32[1,512]{1,0:T(1,128)} %bitcast.25, s32[1,512]{1,0:T(1,128)} %bitcast.26, s32[1,512]{1,0:T(1,128)} %pos.1), custom_call_target="tpu_custom_call" | custom-call | flops 2700000000 | bytes 262144 | tf_op jit(solution)/shard_map/pallas_call | solution.py:420
  3.4 0.0 copy-start
  3.4 0.0 copy-start.2
  3.4 0.0 copy-start.3
  3.4 0.0 copy-start.4
  3.4 0.0 copy-start.5
  3.4 16.5 %all-to-all-start = ((f32[1152,1,128]{2,1,0:T(1,128)}), f32[1152,1,128]{2,1,0:T(1,128)S(1)}, u32[]{:S(2)}, u32[]{:S(2)}) async-start(f32[1152,1,128]{2,1,0:T(1,128)} %bitcast.23), calls=%async_computation | async-start | bytes 1179648 | tf_op jit(solution)/shard_map/all_to_all | solution.py:445
  19.9 0.0 copy-done.1
  19.9 0.0 copy-done.6
  19.9 0.0 copy-done.7
  19.9 0.1 shard_map.141.own
  20.0 1.0 %collective-permute-start = (f32[4,56,128]{2,1,0:T(8,128)S(1)}, f32[4,56,128]{2,1,0:T(8,128)S(1)}, u32[]{:S(2)}, u32[]{:S(2)}) collective-permute-start(f32[4,56,128]{2,1,0:T(8,128)S(1)} %shard_map.141.own), channel_id=1, source_target_pairs={{0,128},{128,0},{1,129},{129,1},{2,130},{130,2},{3,131},{131,3},{4... | collective-permute-start | bytes 344072 | tf_op jit(solution)/shard_map/ppermute | solution.py:464
  21.1 0.0 copy-done
  21.1 0.0 copy-done.2
  21.1 0.0 copy-done.3
  21.1 0.1 shard_map.145
  21.1 0.9 %collective-permute-start.2 = (f32[208,256]{1,0:T(8,128)S(1)}, f32[208,256]{1,0:T(8,128)S(1)}, u32[]{:S(2)}, u32[]{:S(2)}) collective-permute-start(f32[208,256]{1,0:T(8,128)S(1)} %get-tuple-element.41), channel_id=1, source_target_pairs={{0,1},{1,2},{2,3},{3,4},{4,5},{5,6},{6,7},{7,8},{8,9},{9,10},{10,1... | collective-permute-start | bytes 638984 | tf_op jit(solution)/shard_map/ppermute | solution.py:443
  22.1 6.3 %collective-permute-start.3 = (f32[208,256]{1,0:T(8,128)S(1)}, f32[208,256]{1,0:T(8,128)S(1)}, u32[]{:S(2)}, u32[]{:S(2)}) collective-permute-start(f32[208,256]{1,0:T(8,128)S(1)} %get-tuple-element.42), channel_id=1, source_target_pairs={{1,0},{2,1},{3,2},{4,3},{5,4},{6,5},{7,6},{8,7},{9,8},{10,9},{11,1... | collective-permute-start | bytes 638984 | tf_op jit(solution)/shard_map/ppermute | solution.py:444
  28.3 0.0 collective-permute-done.other
  28.3 0.0 copy-done.4
  28.3 0.0 copy-done.5
  28.4 0.8 %shard_map.142 = (bf16[5120,128]{1,0:T(8,128)(2,1)S(1)}, f32[112,128]{1,0:T(8,128)S(1)}, f32[112,128]{1,0:T(8,128)S(1)}, bf16[512,128]{1,0:T(8,128)(2,1)S(1)}, bf16[512,512]{1,0:T(8,128)(2,1)S(1)}) custom-call(s32[1]{0:T(128)} %bitcast.6.side, f32[4,56,128]{2,1,0:T(8,128)S(1)} %shard_map.141.own, f32[4,56,128]{2,1,0:T(8,128)S(1)} %collective-permute-done.other, ...), custom_call_target="tpu_custom_call" | custom-call | flops 3000000000 | bytes 262144 | tf_op jit(solution)/shard_map/pallas_call | solution.py:452
  29.1 0.0 copy-start.8
  29.1 1.1 %copy-done.8 = bf16[5120,128]{1,0:T(8,128)(2,1)} copy-done((bf16[5120,128]{1,0:T(8,128)(2,1)}, bf16[5120,128]{1,0:T(8,128)(2,1)S(1)}, u32[]{:S(2)}) %copy-start.8) | copy-done | bytes 1310744
  30.2 7.8 %all-to-all-done = f32[1152,1,128]{2,1,0:T(1,128)S(1)} async-done(((f32[1152,1,128]{2,1,0:T(1,128)}), f32[1152,1,128]{2,1,0:T(1,128)S(1)}, u32[]{:S(2)}, u32[]{:S(2)}) %all-to-all-start) | async-done | bytes 589856 | tf_op jit(solution)/shard_map/all_to_all | solution.py:445
  38.0 0.0 copy-start.9
  38.0 1.3 %copy-done.9 = bf16[5120,128]{1,0:T(8,128)(2,1)S(1)} copy-done((bf16[5120,128]{1,0:T(8,128)(2,1)S(1)}, bf16[5120,128]{1,0:T(8,128)(2,1)}, u32[]{:S(2)}) %copy-start.9) | copy-done | bytes 1310744
  39.3 1.7 %shard_map.143 = (f32[5120,128]{1,0:T(8,128)S(1)}, f32[5120,128]{1,0:T(8,128)S(1)}, f32[5120,128]{1,0:T(8,128)S(1)}, f32[48,128]{1,0:T(8,128)S(1)}, f32[360,128]{1,0:T(8,128)S(1)}, /*index=5*/f32[224,128]{1,0:T(8,128)S(1)}) custom-call(s32[1]{0:T(128)} %bitcast.6.side, f32[1152,128]{1,0:T(8,128)S(1)} %bitcast.16, s32[1,512]{1,0:T(1,128)S(1)} %copy-done.5, ...), custom_call_target="tpu_custom_call" | custom-call | flops 2000000000 | bytes 262144 | tf_op jit(solution)/shard_map/pallas_call | solution.py:468
  41.0 4.2 %collective-permute-start.1 = (f32[224,128]{1,0:T(8,128)S(1)}, f32[224,128]{1,0:T(8,128)S(1)}, u32[]{:S(2)}, u32[]{:S(2)}) collective-permute-start(f32[224,128]{1,0:T(8,128)S(1)} %get-tuple-element.34), channel_id=1, source_target_pairs={{0,128},{128,0},{1,129},{129,1},{2,130},{130,2},{3,131},{131,3},{4... | collective-permute-start | bytes 344072 | tf_op jit(solution)/shard_map/ppermute | solution.py:487
  45.2 1.0 %collective-permute-done.1.gotten = f32[224,128]{1,0:T(8,128)S(1)} collective-permute-done((f32[224,128]{1,0:T(8,128)S(1)}, f32[224,128]{1,0:T(8,128)S(1)}, u32[]{:S(2)}, u32[]{:S(2)}) %collective-permute-start.1) | collective-permute-done | bytes 114720 | tf_op jit(solution)/shard_map/ppermute | solution.py:487
  46.1 1.4 %shard_map.144 = f32[256,128]{1,0:T(8,128)} custom-call(s32[1]{0:T(128)} %bitcast.6.side, f32[224,128]{1,0:T(8,128)S(1)} %collective-permute-done.1.gotten, f32[5120,128]{1,0:T(8,128)S(1)} %get-tuple-element.35.trans, f32[5120,128]{1,0:T(8,128)S(1)} %get-tuple-element.36.glow, f32[5120,128]{1,0:T(8,128)S(1)} %get-tuple-element.37.passing, ...), custom_call_target="tpu_custom_call" | custom-call | flops 900000000 | bytes 262144 | tf_op jit(solution)/shard_map/pallas_call | solution.py:488
  47.5 6.5 %all-to-all-start.1 = ((f32[256,1,128]{2,1,0:T(1,128)}), f32[256,1,128]{2,1,0:T(1,128)S(1)}, u32[]{:S(2)}, u32[]{:S(2)}) async-start(f32[256,1,128]{2,1,0:T(1,128)} %bitcast.11), calls=%async_computation.1 | async-start | bytes 262144 | tf_op jit(solution)/shard_map/all_to_all | solution.py:495
  54.0 0.0 collective-permute-done.2.from_left
  54.0 0.0 collective-permute-done.3.from_right
  54.0 4.2 %shard_map.146 = f32[45,4,512]{2,1,0:T(4,128)} custom-call(f32[45,4,512]{2,1,0:T(4,128)S(1)} %bitcast.20, s32[6,512]{1,0:T(8,128)S(1)} %copy-done.2, f32[6,512]{1,0:T(8,128)S(1)} %copy-done.3, f32[208,256]{1,0:T(8,128)S(1)} %collective-permute-done.2.from_left, f32[208,256]{1,0:T(8,128)S(1)} %collective-permute-done.3.from_right), custom_call_target="tpu_custom_call" | custom-call | flops 4200000000 | bytes 262144 | tf_op jit(solution)/shard_map/pallas_call | solution.py:498
  58.2 6.4 %all-to-all-done.1 = f32[256,1,128]{2,1,0:T(1,128)S(1)} async-done(((f32[256,1,128]{2,1,0:T(1,128)}), f32[256,1,128]{2,1,0:T(1,128)S(1)}, u32[]{:S(2)}, u32[]{:S(2)}) %all-to-all-start.1) | async-done | bytes 131104 | tf_op jit(solution)/shard_map/all_to_all | solution.py:495
  64.6 1.0 %shard_map.147 = f32[45,512]{1,0:T(8,128)} custom-call(f32[256,128]{1,0:T(8,128)S(1)} %bitcast.17, bf16[512,512]{1,0:T(8,128)(2,1)S(1)} %get-tuple-element.44.placing), custom_call_target="tpu_custom_call" | custom-call | flops 1000000000 | bytes 262144 | tf_op jit(solution)/shard_map/pallas_call | solution.py:510
Async XLA Ops:
  0.6 19.3 %copy-start.1 = (f32[4,56,90]{2,1,0:T(8,128)S(1)}, f32[4,56,90]{2,1,0:T(8,128)}, u32[]{:S(2)}) copy-start(f32[4,56,90]{2,1,0:T(8,128)} %opacity.1) | copy-start | bytes 241924
  0.6 19.3 %copy-start.6 = (f32[56]{0:T(128)S(1)}, f32[56]{0:T(128)}, u32[]{:S(2)}) copy-start(f32[56]{0:T(128)} %param.24) | copy-start | bytes 676
  0.7 19.3 %copy-start.7 = (f32[56]{0:T(128)S(1)}, f32[56]{0:T(128)}, u32[]{:S(2)}) copy-start(f32[56]{0:T(128)} %param.25) | copy-start | bytes 676
  3.4 17.7 %copy-start = (f32[4,45,512]{2,0,1:T(4,128)S(1)}, f32[4,45,512]{2,0,1:T(4,128)}, u32[]{:S(2)}) copy-start(f32[4,45,512]{2,0,1:T(4,128)} %param.15) | copy-start | bytes 1105924
  3.4 17.7 %copy-start.2 = (s32[6,512]{1,0:T(8,128)S(1)}, s32[6,512]{1,0:T(8,128)}, u32[]{:S(2)}) copy-start(s32[6,512]{1,0:T(8,128)} %adj.3) | copy-start | bytes 36868
  3.4 17.7 %copy-start.3 = (f32[6,512]{1,0:T(8,128)S(1)}, f32[6,512]{1,0:T(8,128)}, u32[]{:S(2)}) copy-start(f32[6,512]{1,0:T(8,128)} %coef.3) | copy-start | bytes 36868
  3.4 24.9 %copy-start.4 = (s32[1,512]{1,0:T(1,128)S(1)}, s32[1,512]{1,0:T(1,128)}, u32[]{:S(2)}) copy-start(s32[1,512]{1,0:T(1,128)} %pos.1) | copy-start | bytes 6148
  3.4 24.9 %copy-start.5 = (s32[1,512]{1,0:T(1,128)S(1)}, s32[1,512]{1,0:T(1,128)}, u32[]{:S(2)}) copy-start(s32[1,512]{1,0:T(1,128)} %member.3) | copy-start | bytes 6148
  3.4 34.5 %all-to-all-start = ((f32[1152,1,128]{2,1,0:T(1,128)}), f32[1152,1,128]{2,1,0:T(1,128)S(1)}, u32[]{:S(2)}, u32[]{:S(2)}) async-start(f32[1152,1,128]{2,1,0:T(1,128)} %bitcast.23), calls=%async_computation | async-start | bytes 1179648 | tf_op jit(solution)/shard_map/all_to_all | solution.py:445
  20.0 8.3 %collective-permute-start = (f32[4,56,128]{2,1,0:T(8,128)S(1)}, f32[4,56,128]{2,1,0:T(8,128)S(1)}, u32[]{:S(2)}, u32[]{:S(2)}) collective-permute-start(f32[4,56,128]{2,1,0:T(8,128)S(1)} %shard_map.141.own), channel_id=1, source_target_pairs={{0,128},{128,0},{1,129},{129,1},{2,130},{130,2},{3,131},{131,3},{4... | collective-permute-start | bytes 344072 | tf_op jit(solution)/shard_map/ppermute | solution.py:464
  21.1 32.9 %collective-permute-start.2 = (f32[208,256]{1,0:T(8,128)S(1)}, f32[208,256]{1,0:T(8,128)S(1)}, u32[]{:S(2)}, u32[]{:S(2)}) collective-permute-start(f32[208,256]{1,0:T(8,128)S(1)} %get-tuple-element.41), channel_id=1, source_target_pairs={{0,1},{1,2},{2,3},{3,4},{4,5},{5,6},{6,7},{7,8},{8,9},{9,10},{10,1... | collective-permute-start | bytes 638984 | tf_op jit(solution)/shard_map/ppermute | solution.py:443
  22.1 31.9 %collective-permute-start.3 = (f32[208,256]{1,0:T(8,128)S(1)}, f32[208,256]{1,0:T(8,128)S(1)}, u32[]{:S(2)}, u32[]{:S(2)}) collective-permute-start(f32[208,256]{1,0:T(8,128)S(1)} %get-tuple-element.42), channel_id=1, source_target_pairs={{1,0},{2,1},{3,2},{4,3},{5,4},{6,5},{7,6},{8,7},{9,8},{10,9},{11,1... | collective-permute-start | bytes 638984 | tf_op jit(solution)/shard_map/ppermute | solution.py:444
  29.1 1.1 %copy-start.8 = (bf16[5120,128]{1,0:T(8,128)(2,1)}, bf16[5120,128]{1,0:T(8,128)(2,1)S(1)}, u32[]{:S(2)}) copy-start(bf16[5120,128]{1,0:T(8,128)(2,1)S(1)} %get-tuple-element.31.weights) | copy-start | bytes 3932164
  38.0 1.3 %copy-start.9 = (bf16[5120,128]{1,0:T(8,128)(2,1)S(1)}, bf16[5120,128]{1,0:T(8,128)(2,1)}, u32[]{:S(2)}) copy-start(bf16[5120,128]{1,0:T(8,128)(2,1)} %copy-done.8) | copy-start | bytes 3932164
  41.0 5.1 %collective-permute-start.1 = (f32[224,128]{1,0:T(8,128)S(1)}, f32[224,128]{1,0:T(8,128)S(1)}, u32[]{:S(2)}, u32[]{:S(2)}) collective-permute-start(f32[224,128]{1,0:T(8,128)S(1)} %get-tuple-element.34), channel_id=1, source_target_pairs={{0,128},{128,0},{1,129},{129,1},{2,130},{130,2},{3,131},{131,3},{4... | collective-permute-start | bytes 344072 | tf_op jit(solution)/shard_map/ppermute | solution.py:487
  47.5 17.1 %all-to-all-start.1 = ((f32[256,1,128]{2,1,0:T(1,128)}), f32[256,1,128]{2,1,0:T(1,128)S(1)}, u32[]{:S(2)}, u32[]{:S(2)}) async-start(f32[256,1,128]{2,1,0:T(1,128)} %bitcast.11), calls=%async_computation.1 | async-start | bytes 262144 | tf_op jit(solution)/shard_map/all_to_all | solution.py:495

commit v12 on v10

--- a/solution.py
+++ b/solution.py
@@ -96,17 +96,20 @@
     bundle[LEV : LEV + 1, :] = ground[...]
     bundle[LEV + 1 : LEV + 2, :] = sunny
     bundle[LEV + 2 : LEV + 3, :] = day[...].astype(F32) * sunny
-    hi, lo = split(bundle[...])
-    tails = []
+    hi, lo = split(bundle[0:256, :])
+    packed = dot(placing, hi, NT) + dot(placing, lo, NT)
+    tail = bundle[256:288, :]
+    hi = tail.astype(BF).astype(F32)
+    tails = dot(placing, jnp.concatenate([hi] * SLOTS + [tail - hi] * SLOTS, axis=0).astype(BF), NT)
+    tails = tails[:, 0:128] + tails[:, 128:256]
+    lane = lax.broadcasted_iota(jnp.int32, (PEERS, 128), 1) >> 5
+    last = jnp.zeros((PEERS, 128), F32)
     for m in range(SLOTS):
-        if m % 2 == 0:
-            pair = placing[m * PEERS : (m + 2) * PEERS, :]
-            packed = dot(hi, pair, NT) + dot(lo, pair, NT)
-        block = packed[:, m % 2 * PEERS : (m % 2 + 1) * PEERS]
-        send[pl.ds(2 * m, PEERS, CHUNK), :] = block[0:128, :].T
-        send[pl.ds(2 * m + 1, PEERS, CHUNK), :] = block[128:256, :].T
-        tails.append(block[256:288, :])
-    send[pl.ds(CHUNK - 1, PEERS, CHUNK), :] = jnp.concatenate(tails, axis=0).T
+        block = packed[m * PEERS : (m + 1) * PEERS, :]
+        send[pl.ds(2 * m, PEERS, CHUNK), :] = block[:, 0:128]
+        send[pl.ds(2 * m + 1, PEERS, CHUNK), :] = block[:, 128:256]
+        last = jnp.where(lane == m, tails[m * PEERS : (m + 1) * PEERS, :], last)
+    send[pl.ds(CHUNK - 1, PEERS, CHUNK), :] = last
     stores[0].start()
     stores[3].start()
     for store in stores:

time: 64.6 us -> 64.5 us (level)
  no operation moved by 1% of the time
where the time goes in v12:
time: 64.5 us; the launch traced here: 64.3 us
  starting transfers between devices  35.2 us (55%)
  waiting for transfers between devices  16.4 us (25%)
  Pallas kernels  11.8 us (18%)
  between operations  0.8 us (1%)
    all_to_all x1, starting transfers between devices, per_device(): lax.all_to_all(send.reshape(PEERS * CHUNK, 1, 128), 'grp', split_axis=0,...  16.5 us
    all_to_all x1, waiting for transfers between devices, per_device(): lax.all_to_all(send.reshape(PEERS * CHUNK, 1, 128), 'grp', split_axis=0,...  9.04 us
    all_to_all x1, starting transfers between devices, per_device(): lax.all_to_all(back.reshape(PEERS * 2, 1, 128), 'grp', split_axis=0, conc...  6.5 us
    all_to_all x1, waiting for transfers between devices, per_device(): lax.all_to_all(back.reshape(PEERS * 2, 1, 128), 'grp', split_axis=0, conc...  6.39 us
    ppermute x1, starting transfers between devices, per_device(): from_right = lax.ppermute(left, 'grp', down)  6.18 us
    pallas_call x1, Pallas kernels, per_device(): call(mix_kernel, 'mix', shape(LEV, SPECIES, COLS), [pltpu.VMEM((2, BODY,...  4.22 us
    ppermute x1, starting transfers between devices, per_device(): gotten = lax.ppermute(edge, 'sec', swap)  4.19 us
    pallas_call x1, Pallas kernels, per_device(): call(pack_kernel, 'pack', packed, [pltpu.VMEM(dims, F32) for dims in give...  2.72 us
  transfers between devices with their start and end apart: 6, of which 3 were waited for; matrix products, arithmetic and copies ran while one was open for 0% of the time, Pallas kernels for 13%

profile of v12, /device:TPU:1, one launch (start us, length us, event | category | flops | bytes accessed | tf_op | source)
XLA Modules:
  0.0 64.3 jit_solution(16495961362479265846)
XLA Ops:
  0.6 0.0 copy-start.1
  0.6 0.0 copy-start.6
  0.7 0.0 copy-start.7
  0.7 2.7 %shard_map.140 = (f32[1152,128]{1,0:T(8,128)}, f32[208,256]{1,0:T(8,128)}, f32[208,256]{1,0:T(8,128)}) custom-call(f32[45,512]{1,0:T(8,128)} %refs_0_.1, f32[45,512]{1,0:T(8,128)} %refs_1_.1, f32[45,4,512]{2,1,0:T(4,128)} %bitcast.18, f32[1,512]{1,0:T(1,128)} %bitcast.23, f32[1,512]{1,0:T(1,128)} %bitcast.24, s32[1,512]{1,0:T(1,128)} %bitcast.25, ...), custom_call_target="tpu_custom_call" | custom-call | flops 2700000000 | bytes 262144 | tf_op jit(solution)/shard_map/pallas_call | solution.py:421
  3.4 0.0 copy-start.8
  3.4 0.0 copy-start.4
  3.4 0.0 copy-start.5
  3.4 16.5 %all-to-all-start = ((f32[1152,1,128]{2,1,0:T(1,128)}), f32[1152,1,128]{2,1,0:T(1,128)S(1)}, u32[]{:S(2)}, u32[]{:S(2)}) async-start(f32[1152,1,128]{2,1,0:T(1,128)} %bitcast.22), calls=%async_computation | async-start | bytes 1179648 | tf_op jit(solution)/shard_map/all_to_all | solution.py:446
  19.9 0.0 copy-done.1
  19.9 0.0 copy-done.6
  19.9 0.0 copy-done.7
  19.9 0.1 shard_map.141.own
  20.0 1.0 %collective-permute-start = (f32[4,56,128]{2,1,0:T(8,128)S(1)}, f32[4,56,128]{2,1,0:T(8,128)S(1)}, u32[]{:S(2)}, u32[]{:S(2)}) collective-permute-start(f32[4,56,128]{2,1,0:T(8,128)S(1)} %shard_map.141.own), channel_id=1, source_target_pairs={{0,128},{128,0},{1,129},{129,1},{2,130},{130,2},{3,131},{131,3},{4... | collective-permute-start | bytes 344072 | tf_op jit(solution)/shard_map/ppermute | solution.py:467
  21.1 0.9 %collective-permute-start.2 = (f32[208,256]{1,0:T(8,128)}, f32[208,256]{1,0:T(8,128)S(1)}, u32[]{:S(2)}, u32[]{:S(2)}) collective-permute-start(f32[208,256]{1,0:T(8,128)} %get-tuple-element.43), channel_id=1, source_target_pairs={{0,1},{1,2},{2,3},{3,4},{4,5},{5,6},{6,7},{7,8},{8,9},{9,10},{10,1... | collective-permute-start | bytes 638984 | tf_op jit(solution)/shard_map/ppermute | solution.py:444
  21.9 0.0 copy-done.8
  21.9 6.2 %collective-permute-start.3 = (f32[208,256]{1,0:T(8,128)S(1)}, f32[208,256]{1,0:T(8,128)S(1)}, u32[]{:S(2)}, u32[]{:S(2)}) collective-permute-start(f32[208,256]{1,0:T(8,128)S(1)} %copy-done.8), channel_id=1, source_target_pairs={{1,0},{2,1},{3,2},{4,3},{5,4},{6,5},{7,6},{8,7},{9,8},{10,9},{11,1... | collective-permute-start | bytes 638984 | tf_op jit(solution)/shard_map/ppermute | solution.py:445
  28.1 0.0 collective-permute-done.other
  28.1 0.0 copy-done.4
  28.1 0.0 copy-done.5
  28.1 0.8 %shard_map.142 = (bf16[5120,128]{1,0:T(8,128)(2,1)S(1)}, f32[112,128]{1,0:T(8,128)S(1)}, f32[112,128]{1,0:T(8,128)S(1)}, bf16[512,128]{1,0:T(8,128)(2,1)S(1)}, bf16[512,512]{1,0:T(8,128)(2,1)S(1)}) custom-call(s32[1]{0:T(128)} %bitcast.6.side, f32[4,56,128]{2,1,0:T(8,128)S(1)} %shard_map.141.own, f32[4,56,128]{2,1,0:T(8,128)S(1)} %collective-permute-done.other, ...), custom_call_target="tpu_custom_call" | custom-call | flops 700000000 | bytes 262144 | tf_op jit(solution)/shard_map/pallas_call | solution.py:455
  28.9 9.0 %all-to-all-done = f32[1152,1,128]{2,1,0:T(1,128)S(1)} async-done(((f32[1152,1,128]{2,1,0:T(1,128)}), f32[1152,1,128]{2,1,0:T(1,128)S(1)}, u32[]{:S(2)}, u32[]{:S(2)}) %all-to-all-start) | async-done | bytes 589856 | tf_op jit(solution)/shard_map/all_to_all | solution.py:446
  37.9 1.7 %shard_map.143 = (f32[5120,128]{1,0:T(8,128)S(1)}, f32[5120,128]{1,0:T(8,128)S(1)}, f32[5120,128]{1,0:T(8,128)S(1)}, f32[48,128]{1,0:T(8,128)S(1)}, f32[360,128]{1,0:T(8,128)S(1)}, /*index=5*/f32[224,128]{1,0:T(8,128)S(1)}) custom-call(s32[1]{0:T(128)} %bitcast.6.side, f32[1152,128]{1,0:T(8,128)S(1)} %bitcast.16, s32[1,512]{1,0:T(1,128)S(1)} %copy-done.5, ...), custom_call_target="tpu_custom_call" | custom-call | flops 2000000000 | bytes 262144 | tf_op jit(solution)/shard_map/pallas_call | solution.py:471
  39.6 4.2 %collective-permute-start.1 = (f32[224,128]{1,0:T(8,128)S(1)}, f32[224,128]{1,0:T(8,128)S(1)}, u32[]{:S(2)}, u32[]{:S(2)}) collective-permute-start(f32[224,128]{1,0:T(8,128)S(1)} %get-tuple-element.36), channel_id=1, source_target_pairs={{0,128},{128,0},{1,129},{129,1},{2,130},{130,2},{3,131},{131,3},{4... | collective-permute-start | bytes 344072 | tf_op jit(solution)/shard_map/ppermute | solution.py:490
  43.8 1.0 %collective-permute-done.1.gotten = f32[224,128]{1,0:T(8,128)S(1)} collective-permute-done((f32[224,128]{1,0:T(8,128)S(1)}, f32[224,128]{1,0:T(8,128)S(1)}, u32[]{:S(2)}, u32[]{:S(2)}) %collective-permute-start.1) | collective-permute-done | bytes 114720 | tf_op jit(solution)/shard_map/ppermute | solution.py:490
  44.8 0.0 copy-start
  44.8 0.0 copy-start.2
  44.8 0.0 copy-start.3
  44.8 1.4 %shard_map.144 = f32[256,128]{1,0:T(8,128)} custom-call(s32[1]{0:T(128)} %bitcast.6.side, f32[224,128]{1,0:T(8,128)S(1)} %collective-permute-done.1.gotten, f32[5120,128]{1,0:T(8,128)S(1)} %get-tuple-element.37.trans, f32[5120,128]{1,0:T(8,128)S(1)} %get-tuple-element.38.glow, f32[5120,128]{1,0:T(8,128)S(1)} %get-tuple-element.39.passing, ...), custom_call_target="tpu_custom_call" | custom-call | flops 900000000 | bytes 262144 | tf_op jit(solution)/shard_map/pallas_call | solution.py:491
  46.2 6.5 %all-to-all-start.1 = ((f32[256,1,128]{2,1,0:T(1,128)}), f32[256,1,128]{2,1,0:T(1,128)S(1)}, u32[]{:S(2)}, u32[]{:S(2)}) async-start(f32[256,1,128]{2,1,0:T(1,128)} %bitcast.11), calls=%async_computation.1 | async-start | bytes 262144 | tf_op jit(solution)/shard_map/all_to_all | solution.py:498
  52.7 0.0 collective-permute-done.2.from_left
  52.7 0.0 collective-permute-done.3.from_right
  52.7 0.0 copy-done
  52.7 0.0 copy-done.2
  52.7 0.0 copy-done.3
  52.7 4.2 %shard_map.145 = f32[45,4,512]{2,1,0:T(4,128)} custom-call(f32[45,4,512]{2,1,0:T(4,128)S(1)} %bitcast.19, s32[6,512]{1,0:T(8,128)S(1)} %copy-done.2, f32[6,512]{1,0:T(8,128)S(1)} %copy-done.3, f32[208,256]{1,0:T(8,128)S(1)} %collective-permute-done.2.from_left, f32[208,256]{1,0:T(8,128)S(1)} %collective-permute-done.3.from_right), custom_call_target="tpu_custom_call" | custom-call | flops 4200000000 | bytes 262144 | tf_op jit(solution)/shard_map/pallas_call | solution.py:501
  56.9 6.4 %all-to-all-done.1 = f32[256,1,128]{2,1,0:T(1,128)S(1)} async-done(((f32[256,1,128]{2,1,0:T(1,128)}), f32[256,1,128]{2,1,0:T(1,128)S(1)}, u32[]{:S(2)}, u32[]{:S(2)}) %all-to-all-start.1) | async-done | bytes 131104 | tf_op jit(solution)/shard_map/all_to_all | solution.py:498
  63.3 1.0 %shard_map.146 = f32[45,512]{1,0:T(8,128)} custom-call(f32[256,128]{1,0:T(8,128)S(1)} %bitcast.17, bf16[512,512]{1,0:T(8,128)(2,1)S(1)} %get-tuple-element.46.placing), custom_call_target="tpu_custom_call" | custom-call | flops 1000000000 | bytes 262144 | tf_op jit(solution)/shard_map/pallas_call | solution.py:513
Async XLA Ops:
  0.6 19.3 %copy-start.1 = (f32[4,56,90]{2,1,0:T(8,128)S(1)}, f32[4,56,90]{2,1,0:T(8,128)}, u32[]{:S(2)}) copy-start(f32[4,56,90]{2,1,0:T(8,128)} %opacity.1) | copy-start | bytes 241924
  0.6 19.3 %copy-start.6 = (f32[56]{0:T(128)S(1)}, f32[56]{0:T(128)}, u32[]{:S(2)}) copy-start(f32[56]{0:T(128)} %param.24) | copy-start | bytes 676
  0.7 19.3 %copy-start.7 = (f32[56]{0:T(128)S(1)}, f32[56]{0:T(128)}, u32[]{:S(2)}) copy-start(f32[56]{0:T(128)} %param.25) | copy-start | bytes 676
  3.4 18.5 %copy-start.8 = (f32[208,256]{1,0:T(8,128)S(1)}, f32[208,256]{1,0:T(8,128)}, u32[]{:S(2)}) copy-start(f32[208,256]{1,0:T(8,128)} %get-tuple-element.44) | copy-start | bytes 638980
  3.4 24.7 %copy-start.4 = (s32[1,512]{1,0:T(1,128)S(1)}, s32[1,512]{1,0:T(1,128)}, u32[]{:S(2)}) copy-start(s32[1,512]{1,0:T(1,128)} %pos.1) | copy-start | bytes 6148
  3.4 24.7 %copy-start.5 = (s32[1,512]{1,0:T(1,128)S(1)}, s32[1,512]{1,0:T(1,128)}, u32[]{:S(2)}) copy-start(s32[1,512]{1,0:T(1,128)} %member.3) | copy-start | bytes 6148
  3.4 34.5 %all-to-all-start = ((f32[1152,1,128]{2,1,0:T(1,128)}), f32[1152,1,128]{2,1,0:T(1,128)S(1)}, u32[]{:S(2)}, u32[]{:S(2)}) async-start(f32[1152,1,128]{2,1,0:T(1,128)} %bitcast.22), calls=%async_computation | async-start | bytes 1179648 | tf_op jit(solution)/shard_map/all_to_all | solution.py:446
  20.0 8.1 %collective-permute-start = (f32[4,56,128]{2,1,0:T(8,128)S(1)}, f32[4,56,128]{2,1,0:T(8,128)S(1)}, u32[]{:S(2)}, u32[]{:S(2)}) collective-permute-start(f32[4,56,128]{2,1,0:T(8,128)S(1)} %shard_map.141.own), channel_id=1, source_target_pairs={{0,128},{128,0},{1,129},{129,1},{2,130},{130,2},{3,131},{131,3},{4... | collective-permute-start | bytes 344072 | tf_op jit(solution)/shard_map/ppermute | solution.py:467
  21.1 31.6 %collective-permute-start.2 = (f32[208,256]{1,0:T(8,128)}, f32[208,256]{1,0:T(8,128)S(1)}, u32[]{:S(2)}, u32[]{:S(2)}) collective-permute-start(f32[208,256]{1,0:T(8,128)} %get-tuple-element.43), channel_id=1, source_target_pairs={{0,1},{1,2},{2,3},{3,4},{4,5},{5,6},{6,7},{7,8},{8,9},{9,10},{10,1... | collective-permute-start | bytes 638984 | tf_op jit(solution)/shard_map/ppermute | solution.py:444
  21.9 30.7 %collective-permute-start.3 = (f32[208,256]{1,0:T(8,128)S(1)}, f32[208,256]{1,0:T(8,128)S(1)}, u32[]{:S(2)}, u32[]{:S(2)}) collective-permute-start(f32[208,256]{1,0:T(8,128)S(1)} %copy-done.8), channel_id=1, source_target_pairs={{1,0},{2,1},{3,2},{4,3},{5,4},{6,5},{7,6},{8,7},{9,8},{10,9},{11,1... | collective-permute-start | bytes 638984 | tf_op jit(solution)/shard_map/ppermute | solution.py:445
  39.6 5.2 %collective-permute-start.1 = (f32[224,128]{1,0:T(8,128)S(1)}, f32[224,128]{1,0:T(8,128)S(1)}, u32[]{:S(2)}, u32[]{:S(2)}) collective-permute-start(f32[224,128]{1,0:T(8,128)S(1)} %get-tuple-element.36), channel_id=1, source_target_pairs={{0,128},{128,0},{1,129},{129,1},{2,130},{130,2},{3,131},{131,3},{4... | collective-permute-start | bytes 344072 | tf_op jit(solution)/shard_map/ppermute | solution.py:490
  44.8 7.9 %copy-start = (f32[4,45,512]{2,0,1:T(4,128)S(1)}, f32[4,45,512]{2,0,1:T(4,128)}, u32[]{:S(2)}) copy-start(f32[4,45,512]{2,0,1:T(4,128)} %param.15) | copy-start | bytes 1105924
  44.8 7.9 %copy-start.2 = (s32[6,512]{1,0:T(8,128)S(1)}, s32[6,512]{1,0:T(8,128)}, u32[]{:S(2)}) copy-start(s32[6,512]{1,0:T(8,128)} %adj.1) | copy-start | bytes 36868
  44.8 7.9 %copy-start.3 = (f32[6,512]{1,0:T(8,128)S(1)}, f32[6,512]{1,0:T(8,128)}, u32[]{:S(2)}) copy-start(f32[6,512]{1,0:T(8,128)} %coef.1) | copy-start | bytes 36868
  46.2 17.2 %all-to-all-start.1 = ((f32[256,1,128]{2,1,0:T(1,128)}), f32[256,1,128]{2,1,0:T(1,128)S(1)}, u32[]{:S(2)}, u32[]{:S(2)}) async-start(f32[256,1,128]{2,1,0:T(1,128)} %bitcast.11), calls=%async_computation.1 | async-start | bytes 262144 | tf_op jit(solution)/shard_map/all_to_all | solution.py:498
